TPU v7x, 512 devices: a whole 4x8x8 slice. The times are simulated.
512 devices in a mesh: round: 8 (over z_hi, x), tile: 64 (over z_lo, y, core).
Axes of the slice: x: 4, y: 8, z: 8 (z_hi: 2, z_lo: 4; z = z_hi * 4 + z_lo), core: 2. Of those that a mesh axis runs over, the one named last changes fastest.
Arguments:
- raw_tiles: bfloat16 [8, 4, 8, 256, 512], P('round', None, None, 'tile'), may hold values from -6 to 6
- ref_bands: bfloat16 [8, 256, 512], P('round', 'tile'), may hold values from -6 to 6
- shifts: int32 [8, 64], P('round', 'tile'), may hold values from 0 to 511
- matrix_ids: int32 [8, 4], P('round'), may hold values from 0 to 3
- resample: bfloat16 [4, 512, 512], replicated, may hold values from -0.25 to 0.25
- unmix: bfloat16 [32, 32], replicated, may hold values from -1 to 1
- conv_weight: bfloat16 [27, 64, 32], replicated, may hold values from -0.21875 to 0.21875
- conv_bias: float32 [64], replicated, may hold values from -3 to 3
- out_weight: bfloat16 [32, 64], replicated, may hold values from -0.75 to 0.75
Outputs:
- correlation: float32 [8, 4, 8, 256, 512], P('round', None, None, 'tile')
- features: bfloat16 [32, 8, 512, 256], P(None, 'round', 'tile')
All inputs are finite; a program needn't handle non-finite values.
Results may differ from a plain program's by a relative error of at most 0.0059.
Values may be sent and summed in bfloat16 or wider, within the bound.
No kernel may reach another device: no remote copies, remote signals or barrier semaphores. Data moves between devices by JAX's collectives and lax.ppermute only.
A program may use at most 64 MiB of HBM per device.

v0:
```python
import math

import jax
import jax.numpy as jnp
from jax import lax
from jax.sharding import PartitionSpec as P


def padded_2(cells, sides, width):
    for axis, dim in sides:
        count = lax.axis_size(axis)
        ends = count - 1
        head = lax.slice_in_dim(cells, 0, width, axis=dim)
        tail = lax.slice_in_dim(cells, cells.shape[dim] - width, cells.shape[dim], axis=dim)
        cells = jnp.concatenate(
            [
                lax.ppermute(tail, axis, [(i, (i + 1) % count) for i in range(ends)]),
                cells,
                lax.ppermute(head, axis, [((i + 1) % count, i) for i in range(ends)]),
            ],
            axis=dim,
        )
    return cells


def body(
    raw_tiles, ref_bands, shifts, matrix_ids, resample, unmix, conv_weight, conv_bias, out_weight
):
    tile_raw = raw_tiles[0]
    channel_count, plane_count, row_count, column_count = tile_raw.shape
    round_count = lax.axis_size("round")
    tile_count = lax.axis_size("tile")
    slab_depth = plane_count // round_count
    brick_cols = column_count // tile_count
    height = row_count * tile_count
    mixed_count = round_count * channel_count
    shifted = jnp.roll(tile_raw, shifts[0, 0], axis=3)
    matrices = jnp.take(resample, matrix_ids[0], axis=0)
    warped = jnp.einsum(
        "czyx,cxw->czyw", shifted, matrices, preferred_element_type=jnp.float32
    ).astype(jnp.bfloat16)
    half_len = column_count // 2
    index = jnp.arange(column_count, dtype=jnp.int32)
    cosine_slot = index <= half_len
    frequency = jnp.where(cosine_slot, index, index - half_len)
    products = index[:, None] * frequency[None, :] % column_count
    angles = products.astype(jnp.float32) * (2.0 * math.pi / column_count)
    table = jnp.where(cosine_slot[None, :], jnp.cos(angles), jnp.sin(angles))
    table_high = table.astype(jnp.bfloat16)
    table_back = lax.optimization_barrier(table_high).astype(jnp.float32)
    table_low = (table - table_back).astype(jnp.bfloat16)
    slot_weight = jnp.where((index == 0) | (index == half_len), 1.0, 2.0).astype(jnp.float32)
    inverse_table = table * slot_weight[None, :]

    def transform(rows):
        return jnp.dot(rows, table_high, preferred_element_type=jnp.float32) + jnp.dot(
            rows, table_low, preferred_element_type=jnp.float32
        )

    piece = lax.all_gather(ref_bands, "round", axis=0, tiled=True)
    band_spectra = transform(piece.reshape(-1, column_count)).reshape(
        piece.shape[0], row_count, column_count
    )
    warp_spectra = transform(warped.reshape(-1, column_count)).reshape(
        channel_count, plane_count, row_count, column_count
    )
    warp_cos = warp_spectra[..., : half_len + 1]
    warp_sin = warp_spectra[..., half_len + 1 :]
    band_cos = band_spectra[None, :, :, : half_len + 1]
    band_sin = band_spectra[None, :, :, half_len + 1 :]
    sine_terms = warp_sin * band_sin
    real_part = warp_cos * band_cos + jnp.pad(sine_terms, ((0, 0), (0, 0), (0, 0), (1, 1)))
    imag_part = warp_sin * band_cos[..., 1:half_len] - warp_cos[..., 1:half_len] * band_sin
    joined = jnp.concatenate([real_part, imag_part], axis=-1).reshape(-1, column_count)
    inverse = lax.dot_general(
        joined, inverse_table, (((1,), (1,)), ((), ())), precision=lax.Precision.HIGH
    )
    scale_factor = 1.0 / (column_count * math.sqrt(column_count))
    correlation = (inverse * scale_factor).reshape(
        1, channel_count, plane_count, row_count, column_count
    )
    pieces = warped.reshape(
        1, channel_count, round_count, slab_depth, row_count, tile_count, brick_cols
    )
    regrouped = lax.all_to_all(
        lax.all_to_all(pieces, "round", split_axis=2, concat_axis=0, tiled=True),
        "tile",
        split_axis=5,
        concat_axis=4,
        tiled=True,
    )
    bricks = jnp.transpose(
        regrouped.reshape(mixed_count, slab_depth, height, brick_cols), (0, 1, 3, 2)
    )
    unmixed = jnp.einsum("ji,izxy->jzxy", unmix, bricks, preferred_element_type=jnp.float32).astype(
        jnp.bfloat16
    )
    with_rims = padded_2(unmixed, (("round", 1), ("tile", 2)), 1)
    padded = jnp.pad(with_rims, ((0, 0), (0, 0), (0, 0), (1, 1)))
    total = jnp.zeros((conv_weight.shape[1], slab_depth, brick_cols, height), jnp.float32)
    for offset in range(27):
        step_z = offset // 9
        step_x = offset // 3 % 3
        step_y = offset % 3
        window = padded[
            :, step_z : step_z + slab_depth, step_x : step_x + brick_cols, step_y : step_y + height
        ]
        total = total + jnp.einsum(
            "hc,czxy->hzxy", conv_weight[offset], window, preferred_element_type=jnp.float32
        )
    hidden = jax.nn.gelu(total + conv_bias[:, None, None, None]).astype(jnp.bfloat16)
    mixed_back = jnp.einsum("ch,hzxy->czxy", out_weight, hidden, preferred_element_type=jnp.float32)
    features = (unmixed.astype(jnp.float32) + mixed_back).astype(jnp.bfloat16)
    return (correlation, features)


def solution(mesh):
    placed = (
        P("round", None, None, "tile", None),
        P("round", "tile", None),
        P("round", "tile"),
        P("round", None),
        P(),
        P(),
        P(),
        P(),
        P(),
    )
    return jax.shard_map(
        body,
        mesh=mesh,
        in_specs=placed,
        out_specs=(P("round", None, None, "tile", None), P(None, "round", "tile", None)),
        check_vma=False,
    )
```

profile of v0, /device:TPU:70, one launch (start us, length us, event | category | flops | bytes accessed | tf_op | source)
XLA Modules:
  0.0 181.1 jit_solution(1963689139146040314)
XLA Ops:
  1.5 0.7 fusion.161
  2.1 0.7 compare_and_fusion
  2.8 0.9 copy.28
  3.7 2.0 %gather_fusion = bf16[4,512,512]{2,1,0:T(8,128)(2,1)} fusion(bf16[4,512,512]{2,1,0:T(8,128)(2,1)S(1)} %copy-done, s32[1024]{0:T(1024)S(1)} %pad_clamp_fusion), kind=kCustom, calls=%fused_computation | custom fusion | bytes 4194320 | tf_op jit(solution)/shard_map/jit(_take)/gather | solution.py:38
  5.8 2.1 %fusion.22 = bf16[4,8,4,512]{3,1,2,0:T(8,128)(2,1)S(1)} fusion(bf16[4,512,512]{2,1,0:T(8,128)(2,1)} %gather_fusion, pred[4]{0:T(512)(128)(4,1)S(1)} %compare_and_fusion, s32[]{:T(128)S(6)} %select_n.84, bf16[4,8,4,512]{3,1,2,0:T(8,128)(2,1)S(1)} %bitcast.330), kind=kOutput, calls=%fused_computation.54 | convolution fusion | flops 68485120 | bytes 2359304 | tf_op jit(solution)/shard_map/czyx,cxw->czyw/dot_general | solution.py:39
  7.9 3.5 %reshape.248 = bf16[1,4,8,1,4,64,8]{6,5,2,4,1,3,0:T(8,128)(2,1)} reshape(bf16[4,8,4,512]{3,1,2,0:T(8,128)(2,1)S(1)} %fusion.22) | data formatting | bytes 262144 | tf_op jit(solution)/shard_map/reshape | solution.py:82
  11.3 1.9 %copy.21 = bf16[1,4,8,1,4,64,8]{5,6,4,3,1,0,2:T(8,128)(2,1)S(1)} copy(bf16[1,4,8,1,4,64,8]{6,5,2,4,1,3,0:T(8,128)(2,1)} %reshape.248) | data formatting | bytes 262144 | tf_op jit(solution)/shard_map/reshape | solution.py:82
  13.3 0.9 reshape.315
  14.2 12.3 %all-to-all-start = ((bf16[8,2,4096]{2,1,0:T(2,128)(2,1)}), bf16[8,2,4096]{2,1,0:T(2,128)(2,1)S(1)}, u32[]{:S(2)}, u32[]{:S(2)}) async-start(bf16[8,2,4096]{2,1,0:T(2,128)(2,1)} %reshape.315), calls=%async_computation | async-start | bytes 262144 | tf_op jit(solution)/shard_map/all_to_all | solution.py:86
  26.6 5.3 %fusion.49 = bf16[512,512]{1,0:T(8,128)(2,1)} fusion(s32[512]{0:T(512)S(1)} %add_select_fusion.1, pred[512]{0:T(512)(128)(4,1)S(1)} %iota_compare_fusion.4), kind=kLoop, calls=%fused_computation.86 | loop fusion | flops 4194304 | bytes 526848 | tf_op jit(solution)/shard_map/convert_element_type | solution.py:49
  31.9 4.5 %fusion.58 = f32[128,512]{1,0:T(8,128)S(1)} fusion(bf16[128,512]{1,0:T(8,128)(2,1)S(1)} %reshape.242, s32[512]{0:T(512)S(1)} %add_select_fusion.1, pred[512]{0:T(512)(128)(4,1)S(1)} %iota_compare_fusion.4), kind=kOutput, calls=%fused_computation.98 | convolution fusion | flops 71303168 | bytes 395776 | tf_op jit(solution)/shard_map/dot_general | solution.py:56
  36.4 44.1 %all_gather.3 = bf16[8,4,512]{2,1,0:T(4,128)(2,1)S(1)} all-gather(bf16[1,4,512]{2,1,0:T(4,128)(2,1)S(1)} %copy-done.3), channel_id=1, replica_groups=mesh['round'=8,'tile'=64] {'round'}, dimensions={0}, use_global_device_ids=true | all-gather | bytes 36864 | tf_op jit(solution)/shard_map/all_gather | solution.py:60
  80.5 4.4 %fusion.56 = f32[512,32]{0,1:T(8,128)S(1)} fusion(bf16[32,512]{1,0:T(8,128)(2,1)S(1)} %reshape.244, s32[512]{0:T(512)S(1)} %add_select_fusion.1, pred[512]{0:T(512)(128)(4,1)S(1)} %iota_compare_fusion.4), kind=kOutput, calls=%fused_computation.97 | convolution fusion | flops 20971520 | bytes 100864 | tf_op jit(solution)/shard_map/dot_general | solution.py:56
  85.0 4.6 %convolution_add_fusion.13 = f32[128,512]{1,0:T(8,128)S(1)} fusion(f32[128,512]{1,0:T(8,128)S(1)} %fusion.58, bf16[128,512]{1,0:T(8,128)(2,1)S(1)} %reshape.242, bf16[512,512]{1,0:T(8,128)(2,1)S(1)} %copy-done.6, s32[512]{0:T(512)S(1)} %add_select_fusion.1, pred[512]{0:T(512)(128)(4,1)S(1)} %iota_compare_fusion.4), kind=kOutput, calls=%fused_computation.49 | convolution fusion | flops 71892992 | bytes 1182208 | tf_op jit(solution)/shard_map/dot_general | solution.py:56
  89.5 4.5 %fusion.26 = f32[32,512]{1,0:T(8,128)S(1)} fusion(f32[512,32]{0,1:T(8,128)S(1)} %fusion.56, bf16[32,512]{1,0:T(8,128)(2,1)S(1)} %reshape.244, bf16[512,512]{1,0:T(8,128)(2,1)S(1)} %copy-done.6, s32[512]{0:T(512)S(1)} %add_select_fusion.1, pred[512]{0:T(512)(128)(4,1)S(1)} %iota_compare_fusion.4), kind=kOutput, calls=%fused_computation.58 | convolution fusion | flops 21512192 | bytes 690688 | tf_op jit(solution)/shard_map/dot_general | solution.py:56
  94.4 0.2 reshape.316
  94.6 3.9 %copy.22 = bf16[8,4,1,1,4,64,8]{6,0,4,1,3,2,5:T(8,128)(2,1)} copy(bf16[8,4,1,1,4,64,8]{5,6,4,1,0,3,2:T(8,128)(2,1)S(1)} %bitcast_bitcast_fusion.1) | data formatting | bytes 262144 | tf_op jit(solution)/shard_map/all_to_all | solution.py:86
  98.5 4.3 %reshape.317 = bf16[64,2,512]{2,1,0:T(2,128)(2,1)} reshape(bf16[64,1,1,4,4,8,8]{6,5,4,3,2,1,0:T(8,128)(2,1)} %bitcast.327) | data formatting | bytes 262144
  102.8 11.0 %all-to-all-start.1 = ((bf16[64,2,512]{2,1,0:T(2,128)(2,1)}), bf16[64,2,512]{2,1,0:T(2,128)(2,1)S(1)}, u32[]{:S(2)}, u32[]{:S(2)}) async-start(bf16[64,2,512]{2,1,0:T(2,128)(2,1)} %reshape.317), calls=%async_computation.1 | async-start | bytes 262144 | tf_op jit(solution)/shard_map/all_to_all | solution.py:85
  113.8 0.2 slice_multiply_fusion.2
  114.0 0.2 fusion.55
  114.2 9.3 %all-to-all-done.1 = bf16[64,2,512]{2,1,0:T(2,128)(2,1)S(1)} async-done(((bf16[64,2,512]{2,1,0:T(2,128)(2,1)}), bf16[64,2,512]{2,1,0:T(2,128)(2,1)S(1)}, u32[]{:S(2)}, u32[]{:S(2)}) %all-to-all-start.1) | async-done | bytes 131104 | tf_op jit(solution)/shard_map/all_to_all | solution.py:85
  123.5 3.5 %reshape.318 = bf16[64,1,1,4,4,8,8]{6,5,4,3,2,1,0:T(8,128)(2,1)} reshape(bf16[64,2,512]{2,1,0:T(2,128)(2,1)S(1)} %all-to-all-done.1) | data formatting | bytes 262144
  126.9 2.0 %bitcast_bitcast_fusion = bf16[8,4,1,1,64,4,1,8]{7,0,5,1,4,6,3,2:T(8,128)(2,1)S(1)} fusion(bf16[64,1,1,4,4,8,8]{6,5,4,3,2,1,0:T(8,128)(2,1)} %reshape.318), kind=kLoop, calls=%fused_computation.274 | loop fusion | bytes 262144 | tf_op jit(solution)/shard_map/all_to_all | solution.py:85
  128.9 2.4 %copy.23 = bf16[8,4,1,1,64,4,1,8]{7,5,4,1,0,6,3,2:T(4,128)(2,1)} copy(bf16[8,4,1,1,64,4,1,8]{7,0,5,1,4,6,3,2:T(8,128)(2,1)S(1)} %bitcast_bitcast_fusion) | data formatting | bytes 262144 | tf_op jit(solution)/shard_map/all_to_all | solution.py:85
  131.3 1.9 %copy.24 = bf16[32,1,256,8]{2,0,3,1:T(8,128)(2,1)S(1)} copy(bf16[32,1,256,8]{3,2,0,1:T(8,128)(2,1)} %bitcast.328) | data formatting | bytes 262144 | tf_op jit(solution)/shard_map/reshape | solution.py:93
  133.3 0.2 convolution_convert_fusion
  133.5 7.3 %collective-permute-start = (bf16[32,1,8,256]{3,0,2,1:T(8,128)(2,1)S(1)}, bf16[32,1,8,256]{3,0,2,1:T(8,128)(2,1)S(1)}, u32[]{:S(2)}, u32[]{:S(2)}) collective-permute-start(bf16[32,1,8,256]{3,0,2,1:T(8,128)(2,1)S(1)} %bitcast.317), channel_id=1, source_target_pairs={{0,64},{64,128},{128,192},{192,256},{256,320},{320,384},{384,448},... | collective-permute-start | bytes 393224 | tf_op jit(solution)/shard_map/ppermute | solution.py:17
  140.7 1.9 %collective-permute-start.1 = (bf16[32,1,8,256]{3,0,2,1:T(8,128)(2,1)S(1)}, bf16[32,1,8,256]{3,0,2,1:T(8,128)(2,1)S(1)}, u32[]{:S(2)}, u32[]{:S(2)}) collective-permute-start(bf16[32,1,8,256]{3,0,2,1:T(8,128)(2,1)S(1)} %bitcast.318), channel_id=1, source_target_pairs={{64,0},{128,64},{192,128},{256,192},{320,256},{384,320},{448,384},... | collective-permute-start | bytes 393224 | tf_op jit(solution)/shard_map/ppermute | solution.py:19
  142.9 3.6 %collective-permute-done = bf16[32,1,8,256]{3,0,2,1:T(8,128)(2,1)S(1)} collective-permute-done((bf16[32,1,8,256]{3,0,2,1:T(8,128)(2,1)S(1)}, bf16[32,1,8,256]{3,0,2,1:T(8,128)(2,1)S(1)}, u32[]{:S(2)}, u32[]{:S(2)}) %collective-permute-start) | collective-permute-done | bytes 131104 | tf_op jit(solution)/shard_map/ppermute | solution.py:17
  146.6 10.1 %collective-permute-done.1 = bf16[32,1,8,256]{3,0,2,1:T(8,128)(2,1)S(1)} collective-permute-done((bf16[32,1,8,256]{3,0,2,1:T(8,128)(2,1)S(1)}, bf16[32,1,8,256]{3,0,2,1:T(8,128)(2,1)S(1)}, u32[]{:S(2)}, u32[]{:S(2)}) %collective-permute-start.1) | collective-permute-done | bytes 131104 | tf_op jit(solution)/shard_map/ppermute | solution.py:19
  156.7 1.9 %collective-permute-start.2 = (bf16[32,3,1,256]{3,0,2,1:T(8,128)(2,1)S(1)}, bf16[32,3,1,256]{3,0,2,1:T(8,128)(2,1)S(1)}, u32[]{:S(2)}, u32[]{:S(2)}) collective-permute-start(bf16[32,3,1,256]{3,0,2,1:T(8,128)(2,1)S(1)} %get-tuple-element.8), channel_id=1, source_target_pairs={{0,1},{1,2},{2,3},{3,4},{4,5},{5,6},{6,7},{7,8},{8,9},{9,10},{10,1... | collective-permute-start | bytes 147464 | tf_op jit(solution)/shard_map/ppermute | solution.py:17
  158.7 5.9 %collective-permute-start.3 = (bf16[32,3,1,256]{3,0,2,1:T(8,128)(2,1)S(1)}, bf16[32,3,1,256]{3,0,2,1:T(8,128)(2,1)S(1)}, u32[]{:S(2)}, u32[]{:S(2)}) collective-permute-start(bf16[32,3,1,256]{3,0,2,1:T(8,128)(2,1)S(1)} %get-tuple-element.9), channel_id=1, source_target_pairs={{1,0},{2,1},{3,2},{4,3},{5,4},{6,5},{7,6},{8,7},{9,8},{10,9},{11,1... | collective-permute-start | bytes 147464 | tf_op jit(solution)/shard_map/ppermute | solution.py:19
  164.5 4.7 %convolution_multiply_fusion = f32[128,512]{1,0:T(8,128)S(1)} fusion(f32[128,512]{1,0:T(8,128)S(1)} %reshape.246, f32[512]{0:T(512)S(1)} %fusion.160, s32[512]{0:T(512)S(1)} %add_select_fusion.1, pred[512]{0:T(512)(128)(4,1)S(1)} %iota_compare_fusion.4), kind=kOutput, calls=%fused_computation.52 | convolution fusion | flops 205586432 | bytes 528896 | tf_op jit(solution)/shard_map/dot_general | solution.py:75
  169.3 0.8 reshape.247
  170.0 0.4 select_maximum_fusion
  170.5 0.3 fusion.95
  170.7 0.3 fusion.88
  171.0 0.3 fusion.81
  171.3 0.3 fusion.74
  171.7 0.3 convolution_bitcast_fusion.3
  172.0 0.3 convolution_add_fusion.12
  172.2 0.3 convolution_add_fusion.11
  172.6 0.3 convolution_add_fusion.10
  172.8 0.3 fusion.15
  173.1 0.3 convolution_add_fusion.8
  173.4 0.3 fusion.16
  173.7 0.3 convolution_add_fusion.6
  173.9 0.3 fusion.17
  174.2 0.3 convolution_add_fusion.4
  174.5 0.3 convolution_add_fusion.3
  174.8 0.3 convolution_add_fusion.2
  175.1 0.3 convolution_add_fusion.1
  175.4 0.3 fusion.14
  175.6 0.3 fusion.13
  176.0 0.3 fusion.12
  176.2 0.3 fusion.11
  176.5 0.3 fusion.10
  176.8 0.3 fusion.9
  177.1 0.3 fusion.18
  177.4 0.3 fusion.7
  177.7 1.1 fusion.6
  178.7 1.6 fusion.25
  180.4 0.7 copy.25
  (33 shorter events, 0.7 us)
Async XLA Ops:
  0.6 3.1 %copy-start = (bf16[4,512,512]{2,1,0:T(8,128)(2,1)S(1)}, bf16[4,512,512]{2,1,0:T(8,128)(2,1)}, u32[]{:S(2)}) copy-start(bf16[4,512,512]{2,1,0:T(8,128)(2,1)} %param.13) | copy-start | bytes 6291460
  14.2 80.2 %all-to-all-start = ((bf16[8,2,4096]{2,1,0:T(2,128)(2,1)}), bf16[8,2,4096]{2,1,0:T(2,128)(2,1)S(1)}, u32[]{:S(2)}, u32[]{:S(2)}) async-start(bf16[8,2,4096]{2,1,0:T(2,128)(2,1)} %reshape.315), calls=%async_computation | async-start | bytes 262144 | tf_op jit(solution)/shard_map/all_to_all | solution.py:86
  31.9 4.5 %copy-start.3 = (bf16[1,4,512]{2,1,0:T(4,128)(2,1)S(1)}, bf16[1,4,512]{2,1,0:T(4,128)(2,1)}, u32[]{:S(2)}) copy-start(bf16[1,4,512]{2,1,0:T(4,128)(2,1)} %param.10) | copy-start | bytes 12292
  80.5 4.4 %copy-start.6 = (bf16[512,512]{1,0:T(8,128)(2,1)S(1)}, bf16[512,512]{1,0:T(8,128)(2,1)}, u32[]{:S(2)}) copy-start(bf16[512,512]{1,0:T(8,128)(2,1)} %fusion.49) | copy-start | bytes 1572868
  102.8 20.6 %all-to-all-start.1 = ((bf16[64,2,512]{2,1,0:T(2,128)(2,1)}), bf16[64,2,512]{2,1,0:T(2,128)(2,1)S(1)}, u32[]{:S(2)}, u32[]{:S(2)}) async-start(bf16[64,2,512]{2,1,0:T(2,128)(2,1)} %reshape.317), calls=%async_computation.1 | async-start | bytes 262144 | tf_op jit(solution)/shard_map/all_to_all | solution.py:85
  131.3 1.9 %copy-start.2 = (bf16[32,32]{1,0:T(8,128)(2,1)S(1)}, bf16[32,32]{1,0:T(8,128)(2,1)}, u32[]{:S(2)}) copy-start(bf16[32,32]{1,0:T(8,128)(2,1)} %param.14) | copy-start | bytes 6148
  133.5 13.1 %collective-permute-start = (bf16[32,1,8,256]{3,0,2,1:T(8,128)(2,1)S(1)}, bf16[32,1,8,256]{3,0,2,1:T(8,128)(2,1)S(1)}, u32[]{:S(2)}, u32[]{:S(2)}) collective-permute-start(bf16[32,1,8,256]{3,0,2,1:T(8,128)(2,1)S(1)} %bitcast.317), channel_id=1, source_target_pairs={{0,64},{64,128},{128,192},{192,256},{256,320},{320,384},{384,448},... | collective-permute-start | bytes 393224 | tf_op jit(solution)/shard_map/ppermute | solution.py:17
  140.7 16.0 %collective-permute-start.1 = (bf16[32,1,8,256]{3,0,2,1:T(8,128)(2,1)S(1)}, bf16[32,1,8,256]{3,0,2,1:T(8,128)(2,1)S(1)}, u32[]{:S(2)}, u32[]{:S(2)}) collective-permute-start(bf16[32,1,8,256]{3,0,2,1:T(8,128)(2,1)S(1)} %bitcast.318), channel_id=1, source_target_pairs={{64,0},{128,64},{192,128},{256,192},{320,256},{384,320},{448,384},... | collective-permute-start | bytes 393224 | tf_op jit(solution)/shard_map/ppermute | solution.py:19
  156.7 13.3 %collective-permute-start.2 = (bf16[32,3,1,256]{3,0,2,1:T(8,128)(2,1)S(1)}, bf16[32,3,1,256]{3,0,2,1:T(8,128)(2,1)S(1)}, u32[]{:S(2)}, u32[]{:S(2)}) collective-permute-start(bf16[32,3,1,256]{3,0,2,1:T(8,128)(2,1)S(1)} %get-tuple-element.8), channel_id=1, source_target_pairs={{0,1},{1,2},{2,3},{3,4},{4,5},{5,6},{6,7},{7,8},{8,9},{9,10},{10,1... | collective-permute-start | bytes 147464 | tf_op jit(solution)/shard_map/ppermute | solution.py:17
  158.6 11.8 %copy-start.1 = (bf16[27,64,32]{1,2,0:T(8,128)(2,1)S(1)}, bf16[27,64,32]{1,2,0:T(8,128)(2,1)}, u32[]{:S(2)}) copy-start(bf16[27,64,32]{1,2,0:T(8,128)(2,1)} %param.15) | copy-start | bytes 331780
  158.7 11.4 %collective-permute-start.3 = (bf16[32,3,1,256]{3,0,2,1:T(8,128)(2,1)S(1)}, bf16[32,3,1,256]{3,0,2,1:T(8,128)(2,1)S(1)}, u32[]{:S(2)}, u32[]{:S(2)}) collective-permute-start(bf16[32,3,1,256]{3,0,2,1:T(8,128)(2,1)S(1)} %get-tuple-element.9), channel_id=1, source_target_pairs={{1,0},{2,1},{3,2},{4,3},{5,4},{6,5},{7,6},{8,7},{9,8},{10,9},{11,1... | collective-permute-start | bytes 147464 | tf_op jit(solution)/shard_map/ppermute | solution.py:19
  177.1 1.6 copy-start.4
  177.1 1.6 copy-start.5
where the time goes:
time: 182 us; the launch traced here: 181 us
  blocking collectives  44.1 us (24%)
  starting transfers between devices  40.3 us (22%)
  matrix products  34.7 us (19%)
  local copies, waits for them, and re-layouts  29.5 us (16%)
  waiting for transfers between devices  23.1 us (13%)
  other arithmetic  7.55 us (4%)
  between operations  1.85 us (1%)
    all_gather x1, blocking collectives, body(): piece = lax.all_gather(ref_bands, 'round', axis=0, tiled=True)  44.1 us
    all_to_all x1, starting transfers between devices, body(): lax.all_to_all(pieces, 'round', split_axis=2, concat_axis=0, tiled=True)  12.3 us
    all_to_all x1, starting transfers between devices, body(): lax.all_to_all(lax.all_to_all(pieces, 'round', split_axis=2, concat_axis=...  11 us
    unnamed x20, local copies, waits for them, and re-layouts  10.6 us
    ppermute x2, waiting for transfers between devices, padded_2(): lax.ppermute(head, axis, [((i + 1) % count, i) for i in range(ends)])  10.1 us
    all_to_all x1, waiting for transfers between devices, body(): lax.all_to_all(lax.all_to_all(pieces, 'round', split_axis=2, concat_axis=...  9.27 us
    ppermute x2, starting transfers between devices, padded_2(): lax.ppermute(tail, axis, [(i, (i + 1) % count) for i in range(ends)])  9.2 us
    dot_general x2, matrix products, transform(): jnp.dot(rows, table_low, preferred_element_type=jnp.float32)  9.09 us
  transfers between devices with their start and end apart: 6, of which 3 were waited for; matrix products, arithmetic and copies ran while one was open for 16% of the time, Pallas kernels for 0%

commit v1 on v0

v1 whole, which is shorter than its diff:
```python
import functools
import math

import jax
import jax.numpy as jnp
import numpy as np
from jax import lax
from jax.experimental import pallas as pl
from jax.experimental.pallas import tpu as pltpu
from jax.sharding import PartitionSpec as P

BF = jnp.bfloat16
F32 = jnp.float32
ROUNDS, TILES = 8, 64
CH, DEPTH, ROWS, WIDTH = 4, 8, 4, 512
MIXED, HIDDEN = 32, 64
PLANE = CH * ROWS
CHUNK = 3 * PLANE + 2 * ROWS
BRICK = WIDTH // TILES


def iota(shape, dim):
    return lax.broadcasted_iota(jnp.int32, shape, dim)


def dot(a, b, dims):
    return lax.dot_general(a, b, (dims, ((), ())), preferred_element_type=F32)


def warp_kernel(shift, ids, raw, band, table, out, mats, sems):
    copies = [
        pltpu.make_async_copy(table.at[ids[0, c]], mats.at[c], sems.at[c]) for c in range(CH)
    ]
    for copy in copies:
        copy.start()
    by = shift[0, 0]
    warped = []
    for c in range(CH):
        rows = jnp.concatenate([raw[c, z].astype(F32) for z in range(DEPTH)], axis=0)
        rows = pltpu.roll(rows, by, 1).astype(BF)
        copies[c].wait()
        result = dot(rows, mats[c], ((1,), (0,)))
        warped.append(result.reshape(DEPTH // 2, 2 * ROWS, WIDTH))
    low = iota((DEPTH // 2, 2 * ROWS, WIDTH), 1) < ROWS
    even, odd = [], []
    for c in range(0, CH, 2):
        a, b = warped[c], warped[c + 1]
        even.append(jnp.where(low, a, pltpu.roll(b, ROWS, 1)))
        odd.append(jnp.where(low, pltpu.roll(a, ROWS, 1), b))
    for z in range(DEPTH):
        parts = odd if z % 2 else even
        plane = jnp.concatenate([p[z // 2] for p in parts], axis=0).astype(BF)
        for side in range(3):
            peer = z + 1 - side
            if 0 <= peer < DEPTH:
                out[peer, side * PLANE : (side + 1) * PLANE, :] = plane
    nothing = jnp.zeros((PLANE, WIDTH), BF)
    out[0, :PLANE, :] = nothing
    out[DEPTH - 1, 2 * PLANE : 3 * PLANE, :] = nothing
    own = band[...].astype(F32)
    own = jnp.concatenate([own, own], axis=0).astype(BF)
    for peer in range(DEPTH):
        out[peer, 3 * PLANE :, :] = own


def warp(shift, ids, raw, band, table, interpret=False):
    return pl.pallas_call(
        warp_kernel,
        out_shape=jax.ShapeDtypeStruct((ROUNDS, CHUNK, WIDTH), BF),
        in_specs=[
            pl.BlockSpec(memory_space=pltpu.SMEM),
            pl.BlockSpec(memory_space=pltpu.SMEM),
            pl.BlockSpec(memory_space=pltpu.VMEM),
            pl.BlockSpec(memory_space=pltpu.VMEM),
            pl.BlockSpec(memory_space=pl.ANY),
        ],
        out_specs=pl.BlockSpec(memory_space=pltpu.VMEM),
        scratch_shapes=[pltpu.VMEM((CH, WIDTH, WIDTH), BF), pltpu.SemaphoreType.DMA((CH,))],
        name="warp",
        interpret=interpret,
    )(shift, ids, raw, band, table)


def prepare_kernel(unmix, conv, bias, project, spread, banded, biases, projected):
    n = MIXED * ROWS
    pick_in = (iota((n, MIXED), 0) // ROWS == iota((n, MIXED), 1)).astype(BF)
    pick_out = (iota((MIXED, n), 1) % MIXED == iota((MIXED, n), 0)).astype(BF)
    tall = dot(pick_in, unmix[...], ((1,), (1,))).astype(BF)
    wide = dot(tall, pick_out, ((1,), (0,)))
    own = iota((n, n), 0) % ROWS == iota((n, n), 1) // MIXED
    spread[...] = jnp.where(own, wide, 0.0).astype(BF)
    gap = jnp.zeros((HIDDEN, MIXED), BF)
    for ab in range(9):
        d = [conv[3 * ab + i] for i in range(3)]
        rows = [
            [d[1], d[2], gap, gap, gap, gap, gap, d[0]],
            [d[0], d[1], d[2], gap, gap, gap, gap, gap],
            [gap, d[0], d[1], d[2], gap, gap, gap, gap],
            [gap, gap, d[0], d[1], d[2], gap, gap, gap],
        ]
        for y in range(ROWS):
            banded[y * HIDDEN : (y + 1) * HIDDEN, ab * 256 : (ab + 1) * 256] = jnp.concatenate(
                rows[y], axis=1
            )
    biases[...] = jnp.concatenate([bias[...]] * ROWS, axis=1)
    hole = jnp.zeros((MIXED, HIDDEN), BF)
    for y in range(ROWS):
        row = [project[...] if i == y else hole for i in range(ROWS)]
        projected[y * MIXED : (y + 1) * MIXED, :] = jnp.concatenate(row, axis=1)


def prepare(unmix, conv, bias, project, interpret=False):
    return pl.pallas_call(
        prepare_kernel,
        out_shape=(
            jax.ShapeDtypeStruct((MIXED * ROWS, MIXED * ROWS), BF),
            jax.ShapeDtypeStruct((HIDDEN * ROWS, 9 * 256), BF),
            jax.ShapeDtypeStruct((1, HIDDEN * ROWS), F32),
            jax.ShapeDtypeStruct((MIXED * ROWS, HIDDEN * ROWS), BF),
        ),
        name="prepare",
        interpret=interpret,
    )(unmix, conv, bias, project)


def unmix_kernel(got, spread, out):
    shape = (TILES, BRICK, MIXED * ROWS)
    row = iota(shape, 1)
    edge = jnp.zeros((1,) + shape[1:], F32)
    planes = []
    rims = jnp.zeros(shape, F32)
    for side in range(3):
        mixed = got[:, side * PLANE : (side + 1) * PLANE, :].reshape(ROUNDS * PLANE, WIDTH)
        plane = dot(mixed, spread[...], ((0,), (0,))).reshape(shape)
        planes.append(plane)
        before = jnp.concatenate([edge, plane[:-1]], axis=0)
        after = jnp.concatenate([plane[1:], edge], axis=0)
        rims = jnp.where(row == side, pltpu.roll(before, (side + 1) % BRICK, 1), rims)
        rims = jnp.where(row == 3 + side, pltpu.roll(after, 3 + side, 1), rims)
    out[...] = jnp.concatenate(planes + [rims], axis=1).astype(BF)


def unmixed_chunks(got, spread, interpret=False):
    return pl.pallas_call(
        unmix_kernel,
        out_shape=jax.ShapeDtypeStruct((TILES, 4 * BRICK, MIXED * ROWS), BF),
        name="unmix",
        interpret=interpret,
    )(got, spread)


def tables():
    x = np.arange(WIDTH, dtype=np.int64)
    half = WIDTH // 2
    frequency = np.where(x < half, x, np.where(x == half, half, x - half))
    angles = (x[:, None] * frequency[None, :] % WIDTH) * (2.0 * math.pi / WIDTH)
    table = np.where((x <= half)[None, :], np.cos(angles), np.sin(angles)).astype(np.float32)
    high = table.astype(jnp.bfloat16)
    low = (table - high.astype(np.float32)).astype(jnp.bfloat16)
    return high, low


def correlate_kernel(sent, got, high, low, out):
    half = WIDTH // 2
    own = sent[:, PLANE : 2 * PLANE, :].reshape(DEPTH * PLANE, WIDTH)
    band = got[:, 3 * PLANE :, :].astype(F32).reshape(DEPTH * 2 * ROWS, WIDTH).astype(BF)
    rows = jnp.concatenate([own, band], axis=0)
    along = ((1,), (0,))
    spectra = dot(rows, high[...], along) + dot(rows, low[...], along)
    count = DEPTH * PLANE
    own_cos = spectra[:count, :half].reshape(DEPTH, 2, 2 * ROWS, half)
    own_sin = spectra[:count, half:].reshape(DEPTH, 2, 2 * ROWS, half)
    band_cos = spectra[count:, :half].reshape(DEPTH, 1, 2 * ROWS, half)
    band_sin = spectra[count:, half:].reshape(DEPTH, 1, 2 * ROWS, half)
    first = iota(own_cos.shape, 3) == 0
    sines = own_sin * band_sin
    cosines = own_cos * band_cos
    real = jnp.where(first, cosines, 2.0 * (cosines + sines))
    imag = jnp.where(first, sines, 2.0 * (own_sin * band_cos - own_cos * band_sin))
    joined = jnp.concatenate([real.reshape(count, half), imag.reshape(count, half)], axis=1)
    upper = joined.astype(BF)
    lower = (joined - upper.astype(F32)).astype(BF)
    across = ((1,), (1,))
    both = dot(jnp.concatenate([upper, lower], axis=0), high[...], across)
    inverse = both[:count] + both[count:] + dot(upper, low[...], across)
    inverse = inverse * (1.0 / (WIDTH * math.sqrt(WIDTH)))
    for z in range(DEPTH):
        for c in range(CH):
            start = z * PLANE + c * ROWS
            out[c, z] = inverse[start : start + ROWS]


def correlate(sent, got, high, low, interpret=False):
    return pl.pallas_call(
        correlate_kernel,
        out_shape=jax.ShapeDtypeStruct((CH, DEPTH, ROWS, WIDTH), F32),
        name="correlate",
        interpret=interpret,
    )(sent, got, high, low)


def layer_kernel(got, banded, biases, projected, out, wide, done, first, second):
    shape = (TILES, BRICK, MIXED * ROWS)
    flat = (TILES * BRICK, MIXED * ROWS)
    row = iota(shape, 1)
    right = iota(shape, 2) >= 64
    edge = jnp.zeros((1,) + shape[1:], F32)
    whole = got[...].astype(F32)
    rims = whole[:, 3 * BRICK :, :]
    centre = None
    for a in range(3):
        plane = whole[:, a * BRICK : (a + 1) * BRICK, :]
        if a == 1:
            centre = plane.reshape(flat)
        before = pltpu.roll(rims, (BRICK - a) % BRICK, 1) if a else rims
        after = pltpu.roll(rims, 4 - a, 1)
        views = (
            jnp.where(row == 0, before, pltpu.roll(plane, 1, 1)),
            plane,
            jnp.where(row == BRICK - 1, after, pltpu.roll(plane, BRICK - 1, 1)),
        )
        for b, view in enumerate(views):
            at = (3 * a + b) * 256
            upper = jnp.concatenate([edge, view[:-1]], axis=0)
            lower = jnp.concatenate([view[1:], edge], axis=0)
            wide[:, at : at + 128] = view.reshape(flat).astype(BF)
            wide[:, at + 128 : at + 256] = jnp.where(right, upper, lower).reshape(flat).astype(BF)
    total = dot(wide[...], banded[...], ((1,), (1,))) + biases[...]
    hidden = jax.nn.gelu(total).astype(BF)
    mixed = dot(hidden, projected[...], ((1,), (1,)))
    done[...] = centre + mixed
    left = iota((MIXED, 128), 1) < 64
    order = iota((256, 256), 1) == 4 * (iota((256, 256), 0) % 64) + iota((256, 256), 0) // 64
    order = order.astype(BF)
    lines = []
    for x in range(0, BRICK, 2):
        pair = jnp.concatenate(
            [done[pl.ds(x, TILES, stride=BRICK), :], done[pl.ds(x + 1, TILES, stride=BRICK), :]],
            axis=0,
        ).T
        y = [pair[i * MIXED : (i + 1) * MIXED, :] for i in range(ROWS)]
        lines.append(
            jnp.concatenate(
                [
                    jnp.where(left, y[0], pltpu.roll(y[1], 64, 1)),
                    jnp.where(left, y[2], pltpu.roll(y[3], 64, 1)),
                ],
                axis=1,
            )
        )
        lines.append(
            jnp.concatenate(
                [
                    jnp.where(left, pltpu.roll(y[0], 64, 1), y[1]),
                    jnp.where(left, pltpu.roll(y[2], 64, 1), y[3]),
                ],
                axis=1,
            )
        )
    ordered = dot(jnp.concatenate(lines, axis=0).astype(BF), order, ((1,), (0,)))
    for x in range(BRICK):
        rows = ordered[x * MIXED : (x + 1) * MIXED]
        first[pl.ds(x, MIXED, stride=BRICK), :] = rows[:, :128]
        second[pl.ds(x, MIXED, stride=BRICK), :] = rows[:, 128:]
    out[:, :, :128] = first[...].reshape(MIXED, BRICK, 128).astype(BF)
    out[:, :, 128:] = second[...].reshape(MIXED, BRICK, 128).astype(BF)


def layer(got, banded, biases, projected, interpret=False):
    return pl.pallas_call(
        layer_kernel,
        out_shape=jax.ShapeDtypeStruct((MIXED, BRICK, TILES * ROWS), BF),
        scratch_shapes=[
            pltpu.VMEM((TILES * BRICK, 9 * 256), BF),
            pltpu.VMEM((TILES * BRICK, MIXED * ROWS), F32),
            pltpu.VMEM((MIXED * BRICK, 128), F32),
            pltpu.VMEM((MIXED * BRICK, 128), F32),
        ],
        name="layer",
        interpret=interpret,
    )(got, banded, biases, projected)


def body(
    raw_tiles, ref_bands, shifts, matrix_ids, resample, unmix, conv_weight, conv_bias, out_weight
):
    high, low = tables()
    swap = functools.partial(lax.all_to_all, split_axis=0, concat_axis=0, tiled=True)
    spread, banded, biases, projected = prepare(
        unmix, conv_weight, conv_bias.reshape(1, -1), out_weight
    )
    sent = warp(shifts, matrix_ids, raw_tiles[0], ref_bands[0], resample)
    got = swap(sent, "round")
    chunks = swap(unmixed_chunks(got, spread), "tile")
    correlation = correlate(sent, got, jnp.asarray(high), jnp.asarray(low))
    features = layer(chunks, banded, biases, projected)
    return (correlation[None], features[:, None])


def solution(mesh):
    placed = (
        P("round", None, None, "tile", None),
        P("round", "tile", None),
        P("round", "tile"),
        P("round", None),
        P(),
        P(),
        P(),
        P(),
        P(),
    )
    return jax.shard_map(
        body,
        mesh=mesh,
        in_specs=placed,
        out_specs=(P("round", None, None, "tile", None), P(None, "round", "tile", None)),
        check_vma=False,
    )
```

time: 182 us -> 71.4 us (0.39)
  the two profiles are of different devices: /device:TPU:70 before, /device:TPU:1 now
where the time goes in v1:
time: 71.4 us; the launch traced here: 71 us
  starting transfers between devices  29.6 us (41%)
  waiting for transfers between devices  22.3 us (31%)
  Pallas kernels  15.2 us (21%)
  local copies, waits for them, and re-layouts  2.6 us (4%)
  between operations  1.35 us (2%)
    all_to_all x1, starting transfers between devices, body(): chunks = swap(unmixed_chunks(got, spread), 'tile')  16.6 us
    all_to_all x1, waiting for transfers between devices, body(): chunks = swap(unmixed_chunks(got, spread), 'tile')  14.6 us
    all_to_all x1, starting transfers between devices, body(): got = swap(sent, 'round')  13.1 us
    all_to_all x1, waiting for transfers between devices, body(): got = swap(sent, 'round')  7.65 us
    pallas_call x1, Pallas kernels, warp(): pl.pallas_call(warp_kernel, out_shape=jax.ShapeDtypeStruct((ROUNDS, CHUNK...  3.83 us
    pallas_call x1, Pallas kernels, layer(): pl.pallas_call(layer_kernel, out_shape=jax.ShapeDtypeStruct((MIXED, BRICK...  3.74 us
    pallas_call x1, Pallas kernels, correlate(): pl.pallas_call(correlate_kernel, out_shape=jax.ShapeDtypeStruct((CH, DEPT...  2.96 us
    unnamed x7, local copies, waits for them, and re-layouts  2.6 us
  transfers between devices with their start and end apart: 2, of which 2 were waited for; matrix products, arithmetic and copies ran while one was open for 1% of the time, Pallas kernels for 8%

profile of v1, /device:TPU:1, one launch (start us, length us, event | category | flops | bytes accessed | tf_op | source)
XLA Modules:
  0.0 71.0 jit_solution(17067704654326481775)
XLA Ops:
  0.6 0.0 copy-start.2
  1.3 3.8 %warp.1.sent = bf16[8,56,512]{2,1,0:T(8,128)(2,1)} custom-call(s32[1,1]{1,0:T(1,128)S(6)} %copy.15.shift, s32[1,4]{1,0:T(1,128)} %ids.1, bf16[4,8,4,512]{3,2,1,0:T(4,128)(2,1)} %bitcast.8, bf16[4,512]{1,0:T(4,128)(2,1)} %bitcast.10, bf16[4,512,512]{2,1,0:T(8,128)(2,1)} %table.1), custom_call_target="tpu_custom_call" | custom-call | tf_op jit(solution)/shard_map/warp/pallas_call | solution.py:67
  5.2 13.1 %all-to-all-start = ((bf16[8,56,512]{2,1,0:T(8,128)(2,1)}), bf16[8,56,512]{2,1,0:T(8,128)(2,1)S(1)}, u32[]{:S(2)}, u32[]{:S(2)}) async-start(bf16[8,56,512]{2,1,0:T(8,128)(2,1)} %warp.1.sent), calls=%async_computation | async-start | bytes 917504 | tf_op jit(solution)/shard_map/all_to_all | solution.py:293
  18.2 0.0 copy-done.2
  18.2 1.0 %copy.13.conv = bf16[27,64,32]{2,1,0:T(8,128)(2,1)} copy(bf16[27,64,32]{1,2,0:T(8,128)(2,1)S(1)} %copy-done.2) | data formatting | bytes 221184 | tf_op args[6]
  19.2 2.5 %prepare.1 = (bf16[128,128]{1,0:T(8,128)(2,1)}, bf16[256,2304]{1,0:T(8,128)(2,1)}, f32[1,256]{1,0:T(1,128)}, bf16[128,256]{1,0:T(8,128)(2,1)}) custom-call(bf16[32,32]{1,0:T(8,128)(2,1)} %unmix.2, bf16[27,64,32]{2,1,0:T(8,128)(2,1)} %copy.13.conv, f32[1,64]{1,0:T(1,128)} %bitcast.11, bf16[32,64]{1,0:T(8,128)(2,1)} %project.1), custom_call_target="tpu_custom_call" | custom-call | tf_op jit(solution)/shard_map/prepare/pallas_call | solution.py:113
  21.7 7.6 %all-to-all-done.got = bf16[8,56,512]{2,1,0:T(8,128)(2,1)S(1)} async-done(((bf16[8,56,512]{2,1,0:T(8,128)(2,1)}), bf16[8,56,512]{2,1,0:T(8,128)(2,1)S(1)}, u32[]{:S(2)}, u32[]{:S(2)}) %all-to-all-start) | async-done | bytes 458784 | tf_op jit(solution)/shard_map/all_to_all | solution.py:293
  29.3 0.0 copy-start
  29.3 0.8 %copy-done = bf16[8,56,512]{2,1,0:T(8,128)(2,1)} copy-done((bf16[8,56,512]{2,1,0:T(8,128)(2,1)}, bf16[8,56,512]{2,1,0:T(8,128)(2,1)S(1)}, u32[]{:S(2)}) %copy-start) | copy-done | bytes 458776
  30.1 2.2 %unmix.3 = bf16[64,32,128]{2,1,0:T(8,128)(2,1)} custom-call(bf16[8,56,512]{2,1,0:T(8,128)(2,1)} %copy-done, bf16[128,128]{1,0:T(8,128)(2,1)} %get-tuple-element.6.spread), custom_call_target="tpu_custom_call" | custom-call | tf_op jit(solution)/shard_map/unmix/pallas_call | solution.py:144
  32.3 16.6 %all-to-all-start.1 = ((bf16[64,32,128]{2,1,0:T(8,128)(2,1)}), bf16[64,32,128]{2,1,0:T(8,128)(2,1)S(1)}, u32[]{:S(2)}, u32[]{:S(2)}) async-start(bf16[64,32,128]{2,1,0:T(8,128)(2,1)} %unmix.3), calls=%async_computation.1 | async-start | bytes 1048576 | tf_op jit(solution)/shard_map/all_to_all | solution.py:294
  48.8 3.0 %correlate.1 = f32[4,8,4,512]{3,2,1,0:T(4,128)} custom-call(bf16[8,56,512]{2,1,0:T(8,128)(2,1)} %warp.1.sent, bf16[8,56,512]{2,1,0:T(8,128)(2,1)} %copy-done, bf16[512,512]{1,0:T(8,128)(2,1)} %constant.4.clone.high, bf16[512,512]{1,0:T(8,128)(2,1)} %constant.5.clone.low), custom_call_target="tpu_custom_call" | custom-call | tf_op jit(solution)/shard_map/correlate/pallas_call | solution.py:194
  51.8 14.6 %all-to-all-done.1.got = bf16[64,32,128]{2,1,0:T(8,128)(2,1)S(1)} async-done(((bf16[64,32,128]{2,1,0:T(8,128)(2,1)}), bf16[64,32,128]{2,1,0:T(8,128)(2,1)S(1)}, u32[]{:S(2)}, u32[]{:S(2)}) %all-to-all-start.1) | async-done | bytes 524320 | tf_op jit(solution)/shard_map/all_to_all | solution.py:294
  66.4 0.0 copy-start.1
  66.4 0.8 %copy-done.1 = bf16[64,32,128]{2,1,0:T(8,128)(2,1)} copy-done((bf16[64,32,128]{2,1,0:T(8,128)(2,1)}, bf16[64,32,128]{2,1,0:T(8,128)(2,1)S(1)}, u32[]{:S(2)}) %copy-start.1) | copy-done | bytes 524312
  67.3 3.7 %layer.1 = bf16[32,8,256]{2,1,0:T(8,128)(2,1)} custom-call(bf16[64,32,128]{2,1,0:T(8,128)(2,1)} %copy-done.1, bf16[256,2304]{1,0:T(8,128)(2,1)} %get-tuple-element.7.banded, f32[1,256]{1,0:T(1,128)} %get-tuple-element.8.biases, bf16[128,256]{1,0:T(8,128)(2,1)} %get-tuple-element.9.projected), custom_call_target="tpu_custom_call" | custom-call | tf_op jit(solution)/shard_map/layer/pallas_call | solution.py:270
Async XLA Ops:
  0.6 17.6 %copy-start.2 = (bf16[27,64,32]{1,2,0:T(8,128)(2,1)S(1)}, bf16[27,64,32]{1,2,0:T(8,128)(2,1)}, u32[]{:S(2)}) copy-start(bf16[27,64,32]{1,2,0:T(8,128)(2,1)} %param.17) | copy-start | bytes 331780
  5.2 24.2 %all-to-all-start = ((bf16[8,56,512]{2,1,0:T(8,128)(2,1)}), bf16[8,56,512]{2,1,0:T(8,128)(2,1)S(1)}, u32[]{:S(2)}, u32[]{:S(2)}) async-start(bf16[8,56,512]{2,1,0:T(8,128)(2,1)} %warp.1.sent), calls=%async_computation | async-start | bytes 917504 | tf_op jit(solution)/shard_map/all_to_all | solution.py:293
  29.3 0.8 %copy-start = (bf16[8,56,512]{2,1,0:T(8,128)(2,1)}, bf16[8,56,512]{2,1,0:T(8,128)(2,1)S(1)}, u32[]{:S(2)}) copy-start(bf16[8,56,512]{2,1,0:T(8,128)(2,1)S(1)} %all-to-all-done.got) | copy-start | bytes 1376260
  32.3 34.2 %all-to-all-start.1 = ((bf16[64,32,128]{2,1,0:T(8,128)(2,1)}), bf16[64,32,128]{2,1,0:T(8,128)(2,1)S(1)}, u32[]{:S(2)}, u32[]{:S(2)}) async-start(bf16[64,32,128]{2,1,0:T(8,128)(2,1)} %unmix.3), calls=%async_computation.1 | async-start | bytes 1048576 | tf_op jit(solution)/shard_map/all_to_all | solution.py:294
  66.4 0.8 %copy-start.1 = (bf16[64,32,128]{2,1,0:T(8,128)(2,1)}, bf16[64,32,128]{2,1,0:T(8,128)(2,1)S(1)}, u32[]{:S(2)}) copy-start(bf16[64,32,128]{2,1,0:T(8,128)(2,1)S(1)} %all-to-all-done.1.got) | copy-start | bytes 1572868

commit v2 on v1

v2 whole, which is shorter than its diff:
```python
import functools
import math

import jax
import jax.numpy as jnp
import numpy as np
from jax import lax
from jax.experimental import pallas as pl
from jax.experimental.pallas import tpu as pltpu
from jax.sharding import PartitionSpec as P

BF = jnp.bfloat16
F32 = jnp.float32
ROUNDS, TILES = 8, 64
CH, DEPTH, ROWS, WIDTH = 4, 8, 4, 512
MIXED, HIDDEN = 32, 64
PLANE = CH * ROWS
CHUNK = 3 * PLANE + 2 * ROWS
BRICK = WIDTH // TILES
SPAN = BRICK + 2


def iota(shape, dim):
    return lax.broadcasted_iota(jnp.int32, shape, dim)


def dot(a, b, dims):
    return lax.dot_general(a, b, (dims, ((), ())), preferred_element_type=F32)


def warp_kernel(shift, ids, raw, table, out, own, mats, sems):
    copies = [
        pltpu.make_async_copy(table.at[ids[0, c]], mats.at[c], sems.at[c]) for c in range(CH)
    ]
    for copy in copies:
        copy.start()
    by = shift[0, 0]
    warped = []
    for c in range(CH):
        rows = jnp.concatenate([raw[c, z].astype(F32) for z in range(DEPTH)], axis=0)
        rows = pltpu.roll(rows, by, 1).astype(BF)
        copies[c].wait()
        result = dot(rows, mats[c], ((1,), (0,)))
        own[c] = result.astype(BF)
        warped.append(result.reshape(DEPTH // 2, 2 * ROWS, WIDTH))
    low = iota((DEPTH // 2, 2 * ROWS, WIDTH), 1) < ROWS
    even, odd = [], []
    for c in range(0, CH, 2):
        a, b = warped[c], warped[c + 1]
        even.append(jnp.where(low, a, pltpu.roll(b, ROWS, 1)))
        odd.append(jnp.where(low, pltpu.roll(a, ROWS, 1), b))
    planes = []
    for z in range(DEPTH):
        planes += [p[z // 2] for p in (odd if z % 2 else even)]
    upright = jnp.concatenate(planes, axis=0).T.reshape(TILES, BRICK, DEPTH * PLANE)
    edge = jnp.zeros((1, BRICK, DEPTH * PLANE), F32)
    before = jnp.concatenate([edge, upright[:-1]], axis=0)
    after = jnp.concatenate([upright[1:], edge], axis=0)
    row = iota(upright.shape, 1)
    rims = jnp.where(row == 0, pltpu.roll(before, 1, 1), pltpu.roll(after, 1, 1))
    out[...] = jnp.concatenate([upright, rims], axis=1).astype(BF)


def warp(shift, ids, raw, table, interpret=False):
    return pl.pallas_call(
        warp_kernel,
        out_shape=(
            jax.ShapeDtypeStruct((TILES, 2 * BRICK, DEPTH * PLANE), BF),
            jax.ShapeDtypeStruct((CH, DEPTH * ROWS, WIDTH), BF),
        ),
        in_specs=[
            pl.BlockSpec(memory_space=pltpu.SMEM),
            pl.BlockSpec(memory_space=pltpu.SMEM),
            pl.BlockSpec(memory_space=pltpu.VMEM),
            pl.BlockSpec(memory_space=pl.ANY),
        ],
        scratch_shapes=[pltpu.VMEM((CH, WIDTH, WIDTH), BF), pltpu.SemaphoreType.DMA((CH,))],
        name="warp",
        interpret=interpret,
    )(shift, ids, raw, table)


def prepare_kernel(unmix, conv, bias, project, spread, banded, biases, projected):
    n = MIXED * ROWS
    pick_in = (iota((n, MIXED), 0) // ROWS == iota((n, MIXED), 1)).astype(BF)
    pick_out = (iota((MIXED, n), 1) % MIXED == iota((MIXED, n), 0)).astype(BF)
    tall = dot(pick_in, unmix[...], ((1,), (1,))).astype(BF)
    wide = dot(tall, pick_out, ((1,), (0,)))
    own = iota((n, n), 0) % ROWS == iota((n, n), 1) // MIXED
    spread[...] = jnp.where(own, wide, 0.0).astype(BF)
    gap = jnp.zeros((HIDDEN, MIXED), BF)
    for ab in range(9):
        at = (ab % 3 * 3 + ab // 3) * 256
        d = [conv[3 * ab + i] for i in range(3)]
        rows = [
            [d[1], d[2], gap, gap, gap, gap, gap, d[0]],
            [d[0], d[1], d[2], gap, gap, gap, gap, gap],
            [gap, d[0], d[1], d[2], gap, gap, gap, gap],
            [gap, gap, d[0], d[1], d[2], gap, gap, gap],
        ]
        for y in range(ROWS):
            banded[y * HIDDEN : (y + 1) * HIDDEN, at : at + 256] = jnp.concatenate(
                rows[y], axis=1
            )
    biases[...] = jnp.concatenate([bias[...]] * ROWS, axis=1)
    hole = jnp.zeros((MIXED, HIDDEN), BF)
    for y in range(ROWS):
        row = [project[...] if i == y else hole for i in range(ROWS)]
        projected[y * MIXED : (y + 1) * MIXED, :] = jnp.concatenate(row, axis=1)


def prepare(unmix, conv, bias, project, interpret=False):
    return pl.pallas_call(
        prepare_kernel,
        out_shape=(
            jax.ShapeDtypeStruct((MIXED * ROWS, MIXED * ROWS), BF),
            jax.ShapeDtypeStruct((HIDDEN * ROWS, 9 * 256), BF),
            jax.ShapeDtypeStruct((1, HIDDEN * ROWS), F32),
            jax.ShapeDtypeStruct((MIXED * ROWS, HIDDEN * ROWS), BF),
        ),
        name="prepare",
        interpret=interpret,
    )(unmix, conv, bias, project)


def regroup_kernel(got, band, out, tall):
    mine = band[...].astype(F32)
    mine = jnp.concatenate([mine, mine], axis=0).astype(BF)
    for peer in range(ROUNDS):
        out[peer, 3 * PLANE :, :WIDTH] = mine
        out[peer, 3 * PLANE :, WIDTH:] = jnp.zeros((2 * ROWS, SPAN * TILES - WIDTH), BF)
    tall[...] = got[...].astype(F32).reshape(TILES * 2 * BRICK, DEPTH * PLANE)
    columns = [BRICK] + list(range(BRICK)) + [BRICK + 1]
    for pair in range(SPAN // 2):
        upright = [
            tall[pl.ds(x, TILES, stride=2 * BRICK), :] for x in columns[2 * pair : 2 * pair + 2]
        ]
        flat = jnp.concatenate(upright, axis=0).T.astype(BF)
        for z in range(DEPTH):
            for side in range(3):
                peer = z + 1 - side
                if 0 <= peer < DEPTH:
                    out[
                        peer, side * PLANE : (side + 1) * PLANE, pair * 128 : (pair + 1) * 128
                    ] = flat[z * PLANE : (z + 1) * PLANE]
    nothing = jnp.zeros((PLANE, SPAN * TILES), BF)
    out[0, :PLANE, :] = nothing
    out[DEPTH - 1, 2 * PLANE : 3 * PLANE, :] = nothing


def regroup(got, band, interpret=False):
    return pl.pallas_call(
        regroup_kernel,
        out_shape=jax.ShapeDtypeStruct((ROUNDS, CHUNK, SPAN * TILES), BF),
        scratch_shapes=[pltpu.VMEM((TILES * 2 * BRICK, DEPTH * PLANE), F32)],
        name="regroup",
        interpret=interpret,
    )(got, band)


def tables():
    x = np.arange(WIDTH, dtype=np.int64)
    half = WIDTH // 2
    frequency = np.where(x < half, x, np.where(x == half, half, x - half))
    angles = (x[:, None] * frequency[None, :] % WIDTH) * (2.0 * math.pi / WIDTH)
    table = np.where((x <= half)[None, :], np.cos(angles), np.sin(angles)).astype(np.float32)
    high = table.astype(jnp.bfloat16)
    low = (table - high.astype(np.float32)).astype(jnp.bfloat16)
    return high, low


def spectra_kernel(own, high, low, out):
    rows = own[...].reshape(CH * DEPTH * ROWS, WIDTH)
    out[...] = dot(rows, high[...], ((1,), (0,))) + dot(rows, low[...], ((1,), (0,)))


def own_spectra(own, high, low, interpret=False):
    return pl.pallas_call(
        spectra_kernel,
        out_shape=jax.ShapeDtypeStruct((CH * DEPTH * ROWS, WIDTH), F32),
        name="spectra",
        interpret=interpret,
    )(own, high, low)


def correlate_kernel(own, got, high, low, out):
    half = WIDTH // 2
    count = CH * DEPTH * ROWS
    band = jnp.concatenate(
        [got[z, 3 * PLANE :, :WIDTH].astype(F32)[:ROWS] for z in range(DEPTH)], axis=0
    ).astype(BF)
    along = ((1,), (0,))
    band = dot(band, high[...], along) + dot(band, low[...], along)
    own_cos = own[:, :half].reshape(CH, DEPTH * ROWS, half)
    own_sin = own[:, half:].reshape(CH, DEPTH * ROWS, half)
    band_cos = band[:, :half]
    band_sin = band[:, half:]
    first = iota(own_cos.shape, 2) == 0
    sines = own_sin * band_sin
    cosines = own_cos * band_cos
    real = jnp.where(first, cosines, 2.0 * (cosines + sines))
    imag = jnp.where(first, sines, 2.0 * (own_sin * band_cos - own_cos * band_sin))
    joined = jnp.concatenate([real.reshape(count, half), imag.reshape(count, half)], axis=1)
    upper = joined.astype(BF)
    lower = (joined - upper.astype(F32)).astype(BF)
    across = ((1,), (1,))
    both = dot(jnp.concatenate([upper, lower], axis=0), high[...], across)
    inverse = both[:count] + both[count:] + dot(upper, low[...], across)
    inverse = inverse * (1.0 / (WIDTH * math.sqrt(WIDTH)))
    for c in range(CH):
        for z in range(DEPTH):
            start = (c * DEPTH + z) * ROWS
            out[c, z] = inverse[start : start + ROWS]


def correlate(own, got, high, low, interpret=False):
    return pl.pallas_call(
        correlate_kernel,
        out_shape=jax.ShapeDtypeStruct((CH, DEPTH, ROWS, WIDTH), F32),
        name="correlate",
        interpret=interpret,
    )(own, got, high, low)


def layer_kernel(got, spread, banded, biases, projected, out, wide, first, second):
    n = MIXED * ROWS
    shape = (SPAN, TILES, n)
    flat = (SPAN * TILES, n)
    tile = iota(shape, 1).reshape(flat)
    right = iota(flat, 1) >= 64
    count = BRICK * TILES
    centre = None
    for a in range(3):
        mixed = got[:, a * PLANE : (a + 1) * PLANE, :].reshape(ROUNDS * PLANE, SPAN * TILES)
        plane = dot(mixed, spread[...], ((0,), (0,))).astype(BF)
        at = a * 256
        wide[:, at : at + 128] = plane
        plane = plane.astype(F32)
        if a == 1:
            centre = plane[TILES : TILES + count]
        upper = jnp.where(tile == 0, 0.0, pltpu.roll(plane, 1, 0))
        lower = jnp.where(tile == TILES - 1, 0.0, pltpu.roll(plane, SPAN * TILES - 1, 0))
        wide[:, at + 128 : at + 256] = jnp.where(right, upper, lower).astype(BF)
    total = biases[...]
    for b in range(3):
        total = total + dot(
            wide[b * TILES : b * TILES + count, :],
            banded[:, b * 768 : (b + 1) * 768],
            ((1,), (1,)),
        )
    hidden = jax.nn.gelu(total).astype(BF)
    mixed = dot(hidden, projected[...], ((1,), (1,)))
    done = centre + mixed
    left = iota((MIXED, 128), 1) < 64
    order = iota((256, 256), 1) == 4 * (iota((256, 256), 0) % 64) + iota((256, 256), 0) // 64
    order = order.astype(BF)
    lines = []
    for x in range(0, BRICK, 2):
        pair = done[x * TILES : (x + 2) * TILES, :].T
        y = [pair[i * MIXED : (i + 1) * MIXED, :] for i in range(ROWS)]
        lines.append(
            jnp.concatenate(
                [
                    jnp.where(left, y[0], pltpu.roll(y[1], 64, 1)),
                    jnp.where(left, y[2], pltpu.roll(y[3], 64, 1)),
                ],
                axis=1,
            )
        )
        lines.append(
            jnp.concatenate(
                [
                    jnp.where(left, pltpu.roll(y[0], 64, 1), y[1]),
                    jnp.where(left, pltpu.roll(y[2], 64, 1), y[3]),
                ],
                axis=1,
            )
        )
    ordered = dot(jnp.concatenate(lines, axis=0).astype(BF), order, ((1,), (0,)))
    for x in range(BRICK):
        rows = ordered[x * MIXED : (x + 1) * MIXED]
        first[pl.ds(x, MIXED, stride=BRICK), :] = rows[:, :128]
        second[pl.ds(x, MIXED, stride=BRICK), :] = rows[:, 128:]
    out[:, :, :128] = first[...].reshape(MIXED, BRICK, 128).astype(BF)
    out[:, :, 128:] = second[...].reshape(MIXED, BRICK, 128).astype(BF)


def layer(got, spread, banded, biases, projected, interpret=False):
    return pl.pallas_call(
        layer_kernel,
        out_shape=jax.ShapeDtypeStruct((MIXED, BRICK, TILES * ROWS), BF),
        scratch_shapes=[
            pltpu.VMEM((SPAN * TILES, 3 * 256), BF),
            pltpu.VMEM((MIXED * BRICK, 128), F32),
            pltpu.VMEM((MIXED * BRICK, 128), F32),
        ],
        name="layer",
        interpret=interpret,
    )(got, spread, banded, biases, projected)


def body(
    raw_tiles, ref_bands, shifts, matrix_ids, resample, unmix, conv_weight, conv_bias, out_weight
):
    high, low = tables()
    swap = functools.partial(lax.all_to_all, split_axis=0, concat_axis=0, tiled=True)
    spread, banded, biases, projected = prepare(
        unmix, conv_weight, conv_bias.reshape(1, -1), out_weight
    )
    high, low = jnp.asarray(high), jnp.asarray(low)
    sent, own = warp(shifts, matrix_ids, raw_tiles[0], resample)
    with jax.named_scope("tiles"):
        got = swap(sent, "tile")
    with jax.named_scope("slabs"):
        slabs = swap(regroup(got, ref_bands[0]), "round")
    correlation = correlate(own_spectra(own, high, low), slabs, high, low)
    features = layer(slabs, spread, banded, biases, projected)
    return (correlation[None], features[:, None])


def solution(mesh):
    placed = (
        P("round", None, None, "tile", None),
        P("round", "tile", None),
        P("round", "tile"),
        P("round", None),
        P(),
        P(),
        P(),
        P(),
        P(),
    )
    return jax.shard_map(
        body,
        mesh=mesh,
        in_specs=placed,
        out_specs=(P("round", None, None, "tile", None), P(None, "round", "tile", None)),
        check_vma=False,
    )
```

time: 71.4 us -> 69.2 us (0.969)
  the two profiles are of different devices: /device:TPU:1 before, /device:TPU:72 now
where the time goes in v2:
time: 69.2 us; the launch traced here: 68.8 us
  blocking collectives  24.1 us (35%)
  Pallas kernels  17.2 us (25%)
  waiting for transfers between devices  14.5 us (21%)
  starting transfers between devices  9.83 us (14%)
  local copies, waits for them, and re-layouts  1.83 us (3%)
  between operations  1.3 us (2%)
    all_to_all x1, blocking collectives, body(): got = swap(sent, 'tile')  24.1 us
    all_to_all x1, waiting for transfers between devices, body(): slabs = swap(regroup(got, ref_bands[0]), 'round')  14.5 us
    all_to_all x1, starting transfers between devices, body(): slabs = swap(regroup(got, ref_bands[0]), 'round')  9.83 us
    pallas_call x1, Pallas kernels, warp(): pl.pallas_call(warp_kernel, out_shape=(jax.ShapeDtypeStruct((TILES, 2 * B...  3.87 us
    pallas_call x1, Pallas kernels, layer(): pl.pallas_call(layer_kernel, out_shape=jax.ShapeDtypeStruct((MIXED, BRICK...  3.78 us
    pallas_call x1, Pallas kernels, correlate(): pl.pallas_call(correlate_kernel, out_shape=jax.ShapeDtypeStruct((CH, DEPT...  2.86 us
    pallas_call x1, Pallas kernels, prepare(): pl.pallas_call(prepare_kernel, out_shape=(jax.ShapeDtypeStruct((MIXED * R...  2.47 us
    pallas_call x1, Pallas kernels, own_spectra(): pl.pallas_call(spectra_kernel, out_shape=jax.ShapeDtypeStruct((CH * DEPTH...  2.24 us
  transfers between devices with their start and end apart: 1, of which 1 were waited for; matrix products, arithmetic and copies ran while one was open for 1% of the time, Pallas kernels for 7%

profile of v2, /device:TPU:72, one launch (start us, length us, event | category | flops | bytes accessed | tf_op | source)
XLA Modules:
  0.0 68.8 jit_solution(12920268257856586985)
XLA Ops:
  1.3 0.0 copy-start.1
  1.3 3.9 %warp.1 = (bf16[64,16,128]{2,1,0:T(8,128)(2,1)}, bf16[4,32,512]{2,1,0:T(8,128)(2,1)}) custom-call(s32[1,1]{1,0:T(1,128)S(6)} %copy.15.shift, s32[1,4]{1,0:T(1,128)} %ids.1, bf16[4,8,4,512]{3,2,1,0:T(4,128)(2,1)} %bitcast.8, bf16[4,512,512]{2,1,0:T(8,128)(2,1)} %table.1), custom_call_target="tpu_custom_call" | custom-call | tf_op jit(solution)/shard_map/warp/pallas_call | solution.py:65
  5.2 24.1 %all_to_all.10.got = bf16[64,16,128]{2,1,0:T(8,128)(2,1)} all-to-all(bf16[64,16,128]{2,1,0:T(8,128)(2,1)} %get-tuple-element.9), channel_id=1, replica_groups=mesh['round'=8,'tile'=64] {'tile'}, dimensions={0} | all-to-all | bytes 524288 | tf_op jit(solution)/shard_map/tiles/all_to_all | solution.py:313
  29.2 2.0 %regroup.1 = bf16[8,56,640]{2,1,0:T(8,128)(2,1)} custom-call(bf16[64,16,128]{2,1,0:T(8,128)(2,1)} %all_to_all.10.got, bf16[4,512]{1,0:T(4,128)(2,1)} %bitcast.10), custom_call_target="tpu_custom_call" | custom-call | tf_op jit(solution)/shard_map/slabs/regroup/pallas_call | solution.py:152
  31.2 9.8 %all-to-all-start.1 = ((bf16[8,56,640]{2,1,0:T(8,128)(2,1)}), bf16[8,56,640]{2,1,0:T(8,128)(2,1)S(1)}, u32[]{:S(2)}, u32[]{:S(2)}) async-start(bf16[8,56,640]{2,1,0:T(8,128)(2,1)} %regroup.1), calls=%async_computation.1 | async-start | bytes 1146880 | tf_op jit(solution)/shard_map/slabs/all_to_all | solution.py:315
  41.1 0.0 copy-done.1
  41.1 1.0 %copy.13.conv = bf16[27,64,32]{2,1,0:T(8,128)(2,1)} copy(bf16[27,64,32]{1,2,0:T(8,128)(2,1)S(1)} %copy-done.1) | data formatting | bytes 221184 | tf_op args[6]
  42.0 2.2 %spectra.1.own = f32[128,512]{1,0:T(8,128)} custom-call(bf16[4,32,512]{2,1,0:T(8,128)(2,1)} %get-tuple-element.8.own, bf16[512,512]{1,0:T(8,128)(2,1)} %constant.4.clone.high, bf16[512,512]{1,0:T(8,128)(2,1)} %constant.5.clone.low), custom_call_target="tpu_custom_call" | custom-call | tf_op jit(solution)/shard_map/spectra/pallas_call | solution.py:178
  44.3 2.5 %prepare.1 = (bf16[128,128]{1,0:T(8,128)(2,1)}, bf16[256,2304]{1,0:T(8,128)(2,1)}, f32[1,256]{1,0:T(1,128)}, bf16[128,256]{1,0:T(8,128)(2,1)}) custom-call(bf16[32,32]{1,0:T(8,128)(2,1)} %unmix.1, bf16[27,64,32]{2,1,0:T(8,128)(2,1)} %copy.13.conv, f32[1,64]{1,0:T(1,128)} %bitcast.11, bf16[32,64]{1,0:T(8,128)(2,1)} %project.1), custom_call_target="tpu_custom_call" | custom-call | tf_op jit(solution)/shard_map/prepare/pallas_call | solution.py:113
  46.8 14.5 %all-to-all-done.1.got = bf16[8,56,640]{2,1,0:T(8,128)(2,1)S(1)} async-done(((bf16[8,56,640]{2,1,0:T(8,128)(2,1)}), bf16[8,56,640]{2,1,0:T(8,128)(2,1)S(1)}, u32[]{:S(2)}, u32[]{:S(2)}) %all-to-all-start.1) | async-done | bytes 573472 | tf_op jit(solution)/shard_map/slabs/all_to_all | solution.py:315
  61.3 0.0 copy-start
  61.3 0.8 %copy-done = bf16[8,56,640]{2,1,0:T(8,128)(2,1)} copy-done((bf16[8,56,640]{2,1,0:T(8,128)(2,1)}, bf16[8,56,640]{2,1,0:T(8,128)(2,1)S(1)}, u32[]{:S(2)}) %copy-start) | copy-done | bytes 573464
  62.1 2.9 %correlate.1 = f32[4,8,4,512]{3,2,1,0:T(4,128)} custom-call(f32[128,512]{1,0:T(8,128)} %spectra.1.own, bf16[8,56,640]{2,1,0:T(8,128)(2,1)} %copy-done, bf16[512,512]{1,0:T(8,128)(2,1)} %constant.4.clone.high, bf16[512,512]{1,0:T(8,128)(2,1)} %constant.5.clone.low), custom_call_target="tpu_custom_call" | custom-call | tf_op jit(solution)/shard_map/correlate/pallas_call | solution.py:217
  65.0 3.8 %layer.1 = bf16[32,8,256]{2,1,0:T(8,128)(2,1)} custom-call(bf16[8,56,640]{2,1,0:T(8,128)(2,1)} %copy-done, bf16[128,128]{1,0:T(8,128)(2,1)} %get-tuple-element.10.spread, bf16[256,2304]{1,0:T(8,128)(2,1)} %get-tuple-element.11.banded, f32[1,256]{1,0:T(1,128)} %get-tuple-element.12.biases, bf16[128,256]{1,0:T(8,128)(2,1)} %get-tuple-element.13.projected), custom_call_target="tpu_custom_call" | custom-call | tf_op jit(solution)/shard_map/layer/pallas_call | solution.py:289
Async XLA Ops:
  1.3 39.8 %copy-start.1 = (bf16[27,64,32]{1,2,0:T(8,128)(2,1)S(1)}, bf16[27,64,32]{1,2,0:T(8,128)(2,1)}, u32[]{:S(2)}) copy-start(bf16[27,64,32]{1,2,0:T(8,128)(2,1)} %param.17) | copy-start | bytes 331780
  31.2 30.0 %all-to-all-start.1 = ((bf16[8,56,640]{2,1,0:T(8,128)(2,1)}), bf16[8,56,640]{2,1,0:T(8,128)(2,1)S(1)}, u32[]{:S(2)}, u32[]{:S(2)}) async-start(bf16[8,56,640]{2,1,0:T(8,128)(2,1)} %regroup.1), calls=%async_computation.1 | async-start | bytes 1146880 | tf_op jit(solution)/shard_map/slabs/all_to_all | solution.py:315
  61.3 0.8 %copy-start = (bf16[8,56,640]{2,1,0:T(8,128)(2,1)}, bf16[8,56,640]{2,1,0:T(8,128)(2,1)S(1)}, u32[]{:S(2)}) copy-start(bf16[8,56,640]{2,1,0:T(8,128)(2,1)S(1)} %all-to-all-done.1.got) | copy-start | bytes 1720324

commit v3 on v2

--- a/solution.py
+++ b/solution.py
@@ -14,10 +14,30 @@
 ROUNDS, TILES = 8, 64
 CH, DEPTH, ROWS, WIDTH = 4, 8, 4, 512
 MIXED, HIDDEN = 32, 64
+HALVES, FAR = 2, 4
+PAIRS = TILES // 2
 PLANE = CH * ROWS
-CHUNK = 3 * PLANE + 2 * ROWS
 BRICK = WIDTH // TILES
 SPAN = BRICK + 2
+LINES = 3 * HALVES * PLANE
+ALONG = SPAN * PAIRS
+PADDED = 384
+
+
+def device(half, far, pair, core):
+    return (half * FAR + far) * TILES + 2 * pair + core
+
+
+RINGS = [
+    [device(half, far, pair, core) for half in range(HALVES) for pair in range(PAIRS)]
+    for far in range(FAR)
+    for core in range(2)
+]
+NEAR = [
+    [device(half, far, pair, core) for far in range(FAR) for core in range(2)]
+    for half in range(HALVES)
+    for pair in range(PAIRS)
+]
 
 
 def iota(shape, dim):
@@ -52,21 +72,40 @@
     planes = []
     for z in range(DEPTH):
         planes += [p[z // 2] for p in (odd if z % 2 else even)]
-    upright = jnp.concatenate(planes, axis=0).T.reshape(TILES, BRICK, DEPTH * PLANE)
+    upright = jnp.concatenate(planes, axis=0).T.reshape(PAIRS, 2, BRICK, DEPTH * PLANE)
+    left, right = upright[:, 0], upright[:, 1]
     edge = jnp.zeros((1, BRICK, DEPTH * PLANE), F32)
-    before = jnp.concatenate([edge, upright[:-1]], axis=0)
-    after = jnp.concatenate([upright[1:], edge], axis=0)
-    row = iota(upright.shape, 1)
-    rims = jnp.where(row == 0, pltpu.roll(before, 1, 1), pltpu.roll(after, 1, 1))
-    out[...] = jnp.concatenate([upright, rims], axis=1).astype(BF)
+    before = jnp.concatenate([edge, right[:-1]], axis=0)
+    after = jnp.concatenate([left[1:], edge], axis=0)
+    row, lane = iota(left.shape, 1), iota(left.shape, 2)
+
+    def put(base, value, start, to, width, only=None, turn=0):
+        value = pltpu.roll(value, turn, 1) if turn else value
+        value = pltpu.roll(value, (to - start) % 128, 2) if to != start else value
+        here = (lane >= to) & (lane < to + width)
+        return jnp.where(here if only is None else here & (row == only), value, base)
+
+    for half in range(HALVES):
+        start = 64 * half
+        main = put(left, right, start, 64, 64) if half == 0 else put(right, left, start, 0, 64)
+        more = jnp.zeros(left.shape, F32)
+        more = put(more, before, start, 64, 64, 0, 1)
+        more = put(more, after, start, 64, 64, 1, 1)
+        outer = 64 if half == 0 else 48
+        slot = 32 if half == 0 else 0
+        more = put(more, left, outer, slot, PLANE)
+        more = put(more, right, outer, slot + PLANE, PLANE)
+        more = put(more, before, outer, 64 + slot // 2, PLANE, 2, 3)
+        more = put(more, after, outer, 96 + slot // 2, PLANE, 2, 2)
+        out[half * PAIRS : (half + 1) * PAIRS] = jnp.concatenate([main, more], axis=1).astype(BF)
 
 
 def warp(shift, ids, raw, table, interpret=False):
     return pl.pallas_call(
         warp_kernel,
         out_shape=(
-            jax.ShapeDtypeStruct((TILES, 2 * BRICK, DEPTH * PLANE), BF),
-            jax.ShapeDtypeStruct((CH, DEPTH * ROWS, WIDTH), BF),
+            pltpu.VMEM((TILES, 2 * BRICK, DEPTH * PLANE), BF),
+            pltpu.VMEM((CH, DEPTH * ROWS, WIDTH), BF),
         ),
         in_specs=[
             pl.BlockSpec(memory_space=pltpu.SMEM),
@@ -74,7 +113,10 @@
             pl.BlockSpec(memory_space=pltpu.VMEM),
             pl.BlockSpec(memory_space=pl.ANY),
         ],
-        scratch_shapes=[pltpu.VMEM((CH, WIDTH, WIDTH), BF), pltpu.SemaphoreType.DMA((CH,))],
+        scratch_shapes=[
+            pltpu.VMEM((CH, WIDTH, WIDTH), BF),
+            pltpu.SemaphoreType.DMA((CH,)),
+        ],
         name="warp",
         interpret=interpret,
     )(shift, ids, raw, table)
@@ -82,7 +124,9 @@
 
 def prepare_kernel(unmix, conv, bias, project, spread, banded, biases, projected):
     n = MIXED * ROWS
-    pick_in = (iota((n, MIXED), 0) // ROWS == iota((n, MIXED), 1)).astype(BF)
+    k = iota((n, MIXED), 0)
+    source = (k // PLANE % HALVES * FAR + k // (HALVES * PLANE)) * CH + k // ROWS % CH
+    pick_in = (source == iota((n, MIXED), 1)).astype(BF)
     pick_out = (iota((MIXED, n), 1) % MIXED == iota((MIXED, n), 0)).astype(BF)
     tall = dot(pick_in, unmix[...], ((1,), (1,))).astype(BF)
     wide = dot(tall, pick_out, ((1,), (0,)))
@@ -113,49 +157,80 @@
     return pl.pallas_call(
         prepare_kernel,
         out_shape=(
-            jax.ShapeDtypeStruct((MIXED * ROWS, MIXED * ROWS), BF),
+            pltpu.VMEM((MIXED * ROWS, MIXED * ROWS), BF),
             jax.ShapeDtypeStruct((HIDDEN * ROWS, 9 * 256), BF),
-            jax.ShapeDtypeStruct((1, HIDDEN * ROWS), F32),
-            jax.ShapeDtypeStruct((MIXED * ROWS, HIDDEN * ROWS), BF),
+            pltpu.VMEM((1, HIDDEN * ROWS), F32),
+            pltpu.VMEM((MIXED * ROWS, HIDDEN * ROWS), BF),
         ),
         name="prepare",
         interpret=interpret,
     )(unmix, conv, bias, project)
 
 
-def regroup_kernel(got, band, out, tall):
-    mine = band[...].astype(F32)
-    mine = jnp.concatenate([mine, mine], axis=0).astype(BF)
-    for peer in range(ROUNDS):
-        out[peer, 3 * PLANE :, :WIDTH] = mine
-        out[peer, 3 * PLANE :, WIDTH:] = jnp.zeros((2 * ROWS, SPAN * TILES - WIDTH), BF)
+def regroup_kernel(got, band, other, out, tall):
     tall[...] = got[...].astype(F32).reshape(TILES * 2 * BRICK, DEPTH * PLANE)
-    columns = [BRICK] + list(range(BRICK)) + [BRICK + 1]
-    for pair in range(SPAN // 2):
-        upright = [
-            tall[pl.ds(x, TILES, stride=2 * BRICK), :] for x in columns[2 * pair : 2 * pair + 2]
-        ]
-        flat = jnp.concatenate(upright, axis=0).T.astype(BF)
-        for z in range(DEPTH):
-            for side in range(3):
-                peer = z + 1 - side
-                if 0 <= peer < DEPTH:
-                    out[
-                        peer, side * PLANE : (side + 1) * PLANE, pair * 128 : (pair + 1) * 128
-                    ] = flat[z * PLANE : (z + 1) * PLANE]
-    nothing = jnp.zeros((PLANE, SPAN * TILES), BF)
-    out[0, :PLANE, :] = nothing
-    out[DEPTH - 1, 2 * PLANE : 3 * PLANE, :] = nothing
-
-
-def regroup(got, band, interpret=False):
+    turned = []
+    for q in range(BRICK):
+        both = [tall[pl.ds(q + at, TILES, stride=2 * BRICK), :] for at in (0, BRICK)]
+        turned.append(jnp.concatenate(both, axis=0).T)
+
+    def piece(slot, column):
+        x = column - 1
+        if 0 <= x < 2 * BRICK:
+            block, q = x // BRICK, x % BRICK
+            if 1 <= slot <= 4:
+                start, at = block * 64 + (slot - 1) * PLANE, 0
+            else:
+                start, at = (32 if slot else 0) + block * PLANE, 64
+        else:
+            side = 0 if x < 0 else 1
+            if 1 <= slot <= 4:
+                q, start, at = side, 64 + (slot - 1) * PLANE, 64
+            else:
+                q, start, at = 2, 64 + 32 * side + (PLANE if slot else 0), 64
+        return turned[q][start : start + PLANE], at
+
+    refs = jnp.concatenate([band[...].astype(F32), other[...].astype(F32)], axis=0)
+    marks = []
+    for p in range(0, 8, 2):
+        pair = refs[:, p * 64 : (p + 2) * 64]
+        marks.append(jnp.concatenate([pltpu.roll(pair, 64, 1), pair], axis=0))
+    lane = iota((PLANE, 128), 1)
+    for core in range(2):
+        for slot in range(6):
+            pieces = [piece(slot, core * BRICK + k) for k in range(SPAN)]
+            for half in range(HALVES):
+                blocks = []
+                for m in range(3):
+                    block = jnp.zeros((PLANE, 128), F32)
+                    for k in range(4 * m, min(4 * m + 4, SPAN)):
+                        rows, at = pieces[k]
+                        to = k % 4 * PAIRS
+                        turn = (to - at - half * PAIRS) % 128
+                        rows = pltpu.roll(rows, turn, 1) if turn else rows
+                        block = jnp.where((lane >= to) & (lane < to + PAIRS), rows, block)
+                    blocks.append(block)
+                main = [block.astype(BF) for block in blocks[:2]]
+                for far in range(FAR):
+                    step = slot - far
+                    if not 0 <= step < 3:
+                        continue
+                    w = step * HALVES + half
+                    last = jnp.where(lane >= 64, marks[w], blocks[2]) if w < 4 else blocks[2]
+                    rows = slice(w * PLANE, (w + 1) * PLANE)
+                    out[2 * far + core, rows, :128] = main[0]
+                    out[2 * far + core, rows, 128:256] = main[1]
+                    out[2 * far + core, rows, 256:] = last.astype(BF)
+
+
+def regroup(got, band, other, interpret=False):
     return pl.pallas_call(
         regroup_kernel,
-        out_shape=jax.ShapeDtypeStruct((ROUNDS, CHUNK, SPAN * TILES), BF),
+        out_shape=pltpu.VMEM((2 * FAR, LINES, PADDED), BF),
         scratch_shapes=[pltpu.VMEM((TILES * 2 * BRICK, DEPTH * PLANE), F32)],
         name="regroup",
         interpret=interpret,
-    )(got, band)
+    )(got, band, other)
 
 
 def tables():
@@ -177,17 +252,33 @@
 def own_spectra(own, high, low, interpret=False):
     return pl.pallas_call(
         spectra_kernel,
-        out_shape=jax.ShapeDtypeStruct((CH * DEPTH * ROWS, WIDTH), F32),
+        out_shape=pltpu.VMEM((CH * DEPTH * ROWS, WIDTH), F32),
         name="spectra",
         interpret=interpret,
     )(own, high, low)
 
 
-def correlate_kernel(own, got, high, low, out):
+def correlate_kernel(place, own, got, high, low, out):
     half = WIDTH // 2
     count = CH * DEPTH * ROWS
+    left = iota((2 * ROWS, 128), 1) < 64
+    near, away = [], []
+    for far in range(FAR):
+        pieces = jnp.where(
+            place[1] == 0, got[2 * far].astype(F32), got[2 * far + 1].astype(F32)
+        )
+        lanes = []
+        for p in range(0, 8, 2):
+            a = pieces[p * 2 * ROWS : (p + 1) * 2 * ROWS]
+            b = pieces[(p + 1) * 2 * ROWS : (p + 2) * 2 * ROWS]
+            lanes.append(jnp.where(left, pltpu.roll(a, 64, 1), b))
+        rows = jnp.concatenate(lanes, axis=1)
+        near.append(rows[:ROWS])
+        away.append(rows[ROWS:])
+    near, away = jnp.concatenate(near, axis=0), jnp.concatenate(away, axis=0)
+    first_half = place[0] == 0
     band = jnp.concatenate(
-        [got[z, 3 * PLANE :, :WIDTH].astype(F32)[:ROWS] for z in range(DEPTH)], axis=0
+        [jnp.where(first_half, near, away), jnp.where(first_half, away, near)], axis=0
     ).astype(BF)
     along = ((1,), (0,))
     band = dot(band, high[...], along) + dot(band, low[...], along)
@@ -213,50 +304,80 @@
             out[c, z] = inverse[start : start + ROWS]
 
 
-def correlate(own, got, high, low, interpret=False):
+def correlate(place, own, got, high, low, interpret=False):
+    def whole(*shape):
+        return pl.BlockSpec(shape, lambda i: (0,) * len(shape))
+
     return pl.pallas_call(
         correlate_kernel,
+        grid=(1,),
+        in_specs=[
+            pl.BlockSpec(memory_space=pltpu.SMEM),
+            whole(*own.shape),
+            pl.BlockSpec((2 * FAR, 64, 128), lambda i: (0, 0, 2)),
+            whole(WIDTH, WIDTH),
+            whole(WIDTH, WIDTH),
+        ],
+        out_specs=whole(CH, DEPTH, ROWS, WIDTH),
         out_shape=jax.ShapeDtypeStruct((CH, DEPTH, ROWS, WIDTH), F32),
         name="correlate",
         interpret=interpret,
-    )(own, got, high, low)
-
-
-def layer_kernel(got, spread, banded, biases, projected, out, wide, first, second):
+    )(place, own, got, high, low)
+
+
+def layer_kernel(got, spread, banded, biases, projected, out, wide, first, second, weights, sem):
+    fetch = pltpu.make_async_copy(banded, weights, sem.at[0])
+    fetch.start()
     n = MIXED * ROWS
-    shape = (SPAN, TILES, n)
-    flat = (SPAN * TILES, n)
-    tile = iota(shape, 1).reshape(flat)
-    right = iota(flat, 1) >= 64
-    count = BRICK * TILES
+    pair = iota((SPAN, PAIRS, n), 1).reshape(ALONG, n)
+    right = iota((ALONG, n), 1) >= 64
+    count = BRICK * PAIRS
     centre = None
     for a in range(3):
-        mixed = got[:, a * PLANE : (a + 1) * PLANE, :].reshape(ROUNDS * PLANE, SPAN * TILES)
-        plane = dot(mixed, spread[...], ((0,), (0,))).astype(BF)
         at = a * 256
-        wide[:, at : at + 128] = plane
-        plane = plane.astype(F32)
+        planes = []
+        for core in range(2):
+            mixed = jnp.concatenate(
+                [
+                    got[2 * far + core, a * HALVES * PLANE : (a + 1) * HALVES * PLANE, :]
+                    for far in range(FAR)
+                ],
+                axis=0,
+            )
+            plane = dot(mixed, spread[...], ((0,), (0,)))[:ALONG].astype(BF)
+            wide[core, :, at : at + 128] = plane
+            planes.append(plane.astype(F32))
+        even, odd = planes
         if a == 1:
-            centre = plane[TILES : TILES + count]
-        upper = jnp.where(tile == 0, 0.0, pltpu.roll(plane, 1, 0))
-        lower = jnp.where(tile == TILES - 1, 0.0, pltpu.roll(plane, SPAN * TILES - 1, 0))
-        wide[:, at + 128 : at + 256] = jnp.where(right, upper, lower).astype(BF)
+            centre = jnp.concatenate([p[PAIRS : PAIRS + count] for p in planes], axis=0)
+        upper = jnp.where(pair == 0, 0.0, pltpu.roll(odd, 1, 0))
+        lower = jnp.where(pair == PAIRS - 1, 0.0, pltpu.roll(even, ALONG - 1, 0))
+        wide[0, :, at + 128 : at + 256] = jnp.where(right, upper, odd).astype(BF)
+        wide[1, :, at + 128 : at + 256] = jnp.where(right, even, lower).astype(BF)
+    fetch.wait()
     total = biases[...]
     for b in range(3):
-        total = total + dot(
-            wide[b * TILES : b * TILES + count, :],
-            banded[:, b * 768 : (b + 1) * 768],
-            ((1,), (1,)),
+        rows = jnp.concatenate(
+            [wide[core, b * PAIRS : b * PAIRS + count, :] for core in range(2)], axis=0
         )
+        total = total + dot(rows, weights[:, b * 768 : (b + 1) * 768], ((1,), (1,)))
     hidden = jax.nn.gelu(total).astype(BF)
     mixed = dot(hidden, projected[...], ((1,), (1,)))
     done = centre + mixed
     left = iota((MIXED, 128), 1) < 64
-    order = iota((256, 256), 1) == 4 * (iota((256, 256), 0) % 64) + iota((256, 256), 0) // 64
+    k = iota((256, 256), 0)
+    order = iota((256, 256), 1) == 8 * (k % PAIRS) + 4 * (k // PAIRS % 2) + k // 64
     order = order.astype(BF)
     lines = []
     for x in range(0, BRICK, 2):
-        pair = done[x * TILES : (x + 2) * TILES, :].T
+        pair = jnp.concatenate(
+            [
+                done[core * count + at * PAIRS : core * count + (at + 1) * PAIRS]
+                for at in (x, x + 1)
+                for core in range(2)
+            ],
+            axis=0,
+        ).T
         y = [pair[i * MIXED : (i + 1) * MIXED, :] for i in range(ROWS)]
         lines.append(
             jnp.concatenate(
@@ -286,34 +407,47 @@
 
 
 def layer(got, spread, banded, biases, projected, interpret=False):
+    inside = pl.BlockSpec(memory_space=pltpu.VMEM)
     return pl.pallas_call(
         layer_kernel,
+        in_specs=[inside, inside, pl.BlockSpec(memory_space=pl.ANY), inside, inside],
         out_shape=jax.ShapeDtypeStruct((MIXED, BRICK, TILES * ROWS), BF),
         scratch_shapes=[
-            pltpu.VMEM((SPAN * TILES, 3 * 256), BF),
+            pltpu.VMEM((2, ALONG, 3 * 256), BF),
             pltpu.VMEM((MIXED * BRICK, 128), F32),
             pltpu.VMEM((MIXED * BRICK, 128), F32),
+            pltpu.VMEM((HIDDEN * ROWS, 9 * 256), BF),
+            pltpu.SemaphoreType.DMA((1,)),
         ],
         name="layer",
         interpret=interpret,
     )(got, spread, banded, biases, projected)
+
+
+def close(value):
+    return pltpu.with_memory_space_constraint(value, pltpu.VMEM)
 
 
 def body(
     raw_tiles, ref_bands, shifts, matrix_ids, resample, unmix, conv_weight, conv_bias, out_weight
 ):
     high, low = tables()
-    swap = functools.partial(lax.all_to_all, split_axis=0, concat_axis=0, tiled=True)
+    swap = functools.partial(
+        lax.all_to_all, axis_name=("round", "tile"), split_axis=0, concat_axis=0, tiled=True
+    )
+    place = jnp.stack([lax.axis_index("round") >> 2, lax.axis_index("tile") & 1])
+    band = ref_bands[0]
+    other = lax.ppermute(band, "round", [(i, (i + FAR) % ROUNDS) for i in range(ROUNDS)])
     spread, banded, biases, projected = prepare(
         unmix, conv_weight, conv_bias.reshape(1, -1), out_weight
     )
-    high, low = jnp.asarray(high), jnp.asarray(low)
-    sent, own = warp(shifts, matrix_ids, raw_tiles[0], resample)
-    with jax.named_scope("tiles"):
-        got = swap(sent, "tile")
-    with jax.named_scope("slabs"):
-        slabs = swap(regroup(got, ref_bands[0]), "round")
-    correlation = correlate(own_spectra(own, high, low), slabs, high, low)
+    spread, biases, projected = map(close, (spread, biases, projected))
+    high, low = close(jnp.asarray(high)), close(jnp.asarray(low))
+    sent, own = map(close, warp(shifts, matrix_ids, raw_tiles[0], resample))
+    got = close(swap(sent, axis_index_groups=RINGS))
+    slabs = close(swap(close(regroup(got, band, other)), axis_index_groups=NEAR))
+    spectra = close(own_spectra(own, high, low))
+    correlation = correlate(place, spectra, slabs, high, low)
     features = layer(slabs, spread, banded, biases, projected)
     return (correlation[None], features[:, None])
 

time: 69.2 us -> 61.1 us (0.88)
  the two profiles are of different devices: /device:TPU:72 before, /device:TPU:1 now
where the time goes in v3:
time: 61.1 us; the launch traced here: 60.8 us
  starting transfers between devices  31.7 us (52%)
  Pallas kernels  14.6 us (24%)
  waiting for transfers between devices  11.6 us (19%)
  between operations  1.37 us (2%)
  local copies, waits for them, and re-layouts  1.02 us (2%)
    all_to_all x1, starting transfers between devices, body(): got = close(swap(sent, axis_index_groups=RINGS))  17.1 us
    all_to_all x1, starting transfers between devices, body(): swap(close(regroup(got, band, other)), axis_index_groups=NEAR)  7.69 us
    ppermute x1, starting transfers between devices, body(): lax.ppermute(band, 'round', [(i, (i + FAR) % ROUNDS) for i in range(ROUND...  6.93 us
    all_to_all x1, waiting for transfers between devices, body(): swap(close(regroup(got, band, other)), axis_index_groups=NEAR)  5.68 us
    pallas_call x1, Pallas kernels, warp(): pl.pallas_call(warp_kernel, out_shape=(pltpu.VMEM((TILES, 2 * BRICK, DEPT...  4.05 us
    all_to_all x1, waiting for transfers between devices, body(): got = close(swap(sent, axis_index_groups=RINGS))  3.94 us
    pallas_call x1, Pallas kernels, layer(): pl.pallas_call(layer_kernel, in_specs=[inside, inside, pl.BlockSpec(memor...  3.65 us
    pallas_call x1, Pallas kernels, prepare(): pl.pallas_call(prepare_kernel, out_shape=(pltpu.VMEM((MIXED * ROWS, MIXED...  2.45 us
  transfers between devices with their start and end apart: 3, of which 3 were waited for; matrix products, arithmetic and copies ran while one was open for 3% of the time, Pallas kernels for 5%

profile of v3, /device:TPU:1, one launch (start us, length us, event | category | flops | bytes accessed | tf_op | source)
XLA Modules:
  0.0 60.8 jit_solution(18166244003208371193)
XLA Ops:
  0.6 0.0 copy-start.3
  1.3 0.0 copy-start.2
  1.3 4.0 %warp.1 = (bf16[64,16,128]{2,1,0:T(8,128)(2,1)}, bf16[4,32,512]{2,1,0:T(8,128)(2,1)S(1)}) custom-call(s32[1,1]{1,0:T(1,128)S(6)} %copy.15.shift, s32[1,4]{1,0:T(1,128)} %ids.1, bf16[4,8,4,512]{3,2,1,0:T(4,128)(2,1)} %bitcast.10, bf16[4,512,512]{2,1,0:T(8,128)(2,1)} %table.1), custom_call_target="tpu_custom_call" | custom-call | tf_op jit(solution)/shard_map/warp/pallas_call | solution.py:104
  5.4 0.0 copy-start
  5.4 0.0 copy-start.1
  5.4 17.1 %all-to-all-start = ((bf16[64,16,128]{2,1,0:T(8,128)(2,1)}), bf16[64,16,128]{2,1,0:T(8,128)(2,1)S(1)}, u32[]{:S(2)}, u32[]{:S(2)}) async-start(bf16[64,16,128]{2,1,0:T(8,128)(2,1)} %get-tuple-element.9), calls=%async_computation | async-start | bytes 524288 | tf_op jit(solution)/shard_map/all_to_all | solution.py:447
  22.5 0.0 copy-done.3
  22.5 6.9 %collective-permute-start = (bf16[4,512]{1,0:T(4,128)(2,1)S(1)}, bf16[4,512]{1,0:T(4,128)(2,1)S(1)}, u32[]{:S(2)}, u32[]{:S(2)}) collective-permute-start(bf16[4,512]{1,0:T(4,128)(2,1)S(1)} %bitcast.13), channel_id=1, source_target_pairs={{0,256},{64,320},{128,384},{192,448},{256,0},{320,64},{384,128},{4... | collective-permute-start | bytes 12296 | tf_op jit(solution)/shard_map/ppermute | solution.py:440
  29.4 1.9 %collective-permute-done.other = bf16[4,512]{1,0:T(4,128)(2,1)S(1)} collective-permute-done((bf16[4,512]{1,0:T(4,128)(2,1)S(1)}, bf16[4,512]{1,0:T(4,128)(2,1)S(1)}, u32[]{:S(2)}, u32[]{:S(2)}) %collective-permute-start) | collective-permute-done | bytes 4128 | tf_op jit(solution)/shard_map/ppermute | solution.py:440
  31.4 0.0 copy-start.4
  31.4 3.9 %all-to-all-done.got = bf16[64,16,128]{2,1,0:T(8,128)(2,1)S(1)} async-done(((bf16[64,16,128]{2,1,0:T(8,128)(2,1)}), bf16[64,16,128]{2,1,0:T(8,128)(2,1)S(1)}, u32[]{:S(2)}, u32[]{:S(2)}) %all-to-all-start) | async-done | bytes 262176 | tf_op jit(solution)/shard_map/all_to_all | solution.py:447
  35.3 0.0 copy-done.4
  35.3 2.0 %regroup.1 = bf16[8,96,384]{2,1,0:T(8,128)(2,1)} custom-call(bf16[64,16,128]{2,1,0:T(8,128)(2,1)S(1)} %all-to-all-done.got, bf16[4,512]{1,0:T(4,128)(2,1)} %bitcast.12, bf16[4,512]{1,0:T(4,128)(2,1)} %copy-done.4), custom_call_target="tpu_custom_call" | custom-call | tf_op jit(solution)/shard_map/regroup/pallas_call | solution.py:227
  37.3 7.7 %all-to-all-start.1 = ((bf16[8,96,384]{2,1,0:T(8,128)(2,1)}), bf16[8,96,384]{2,1,0:T(8,128)(2,1)S(1)}, u32[]{:S(2)}, u32[]{:S(2)}) async-start(bf16[8,96,384]{2,1,0:T(8,128)(2,1)} %regroup.1), calls=%async_computation.1 | async-start | bytes 1179648 | tf_op jit(solution)/shard_map/all_to_all | solution.py:448
  45.0 0.0 copy-done.2
  45.0 1.0 %copy.13.conv = bf16[27,64,32]{2,1,0:T(8,128)(2,1)} copy(bf16[27,64,32]{1,2,0:T(8,128)(2,1)S(1)} %copy-done.2) | data formatting | bytes 221184 | tf_op args[6]
  46.0 0.0 copy-done
  46.0 0.0 copy-done.1
  46.0 0.3 spectra.1.own
  46.3 2.5 %prepare.1 = (bf16[128,128]{1,0:T(8,128)(2,1)S(1)}, bf16[256,2304]{1,0:T(8,128)(2,1)}, f32[1,256]{1,0:T(1,128)S(1)}, bf16[128,256]{1,0:T(8,128)(2,1)S(1)}) custom-call(bf16[32,32]{1,0:T(8,128)(2,1)} %unmix.1, bf16[27,64,32]{2,1,0:T(8,128)(2,1)} %copy.13.conv, f32[1,64]{1,0:T(1,128)} %bitcast.14, bf16[32,64]{1,0:T(8,128)(2,1)} %project.1), custom_call_target="tpu_custom_call" | custom-call | tf_op jit(solution)/shard_map/prepare/pallas_call | solution.py:157
  48.8 0.6 pad_add_fusion.place
  49.4 5.7 %all-to-all-done.1.got = bf16[8,96,384]{2,1,0:T(8,128)(2,1)S(1)} async-done(((bf16[8,96,384]{2,1,0:T(8,128)(2,1)}), bf16[8,96,384]{2,1,0:T(8,128)(2,1)S(1)}, u32[]{:S(2)}, u32[]{:S(2)}) %all-to-all-start.1) | async-done | bytes 589856 | tf_op jit(solution)/shard_map/all_to_all | solution.py:448
  55.1 2.1 %correlate.1 = f32[4,8,4,512]{3,2,1,0:T(4,128)} custom-call(s32[2]{0:T(128)} %pad_add_fusion.place, f32[128,512]{1,0:T(8,128)S(1)} %spectra.1.own, bf16[8,96,384]{2,1,0:T(8,128)(2,1)S(1)} %all-to-all-done.1.got, bf16[512,512]{1,0:T(8,128)(2,1)S(1)} %copy-done, bf16[512,512]{1,0:T(8,128)(2,1)S(1)} %copy-done.1), custom_call_target="tpu_custom_call" | custom-call | tf_op jit(solution)/shard_map/correlate/pallas_call | solution.py:311
  57.2 3.7 %layer.1 = bf16[32,8,256]{2,1,0:T(8,128)(2,1)} custom-call(bf16[8,96,384]{2,1,0:T(8,128)(2,1)S(1)} %all-to-all-done.1.got, bf16[128,128]{1,0:T(8,128)(2,1)S(1)} %get-tuple-element.10.spread, bf16[256,2304]{1,0:T(8,128)(2,1)} %get-tuple-element.11.banded, f32[1,256]{1,0:T(1,128)S(1)} %get-tuple-element.12.biases, bf16[128,256]{1,0:T(8,128)(2,1)S(1)} %get-tuple-element.13.projected), custom_call_target="tpu_custom_call" | custom-call | tf_op jit(solution)/shard_map/layer/pallas_call | solution.py:411
Async XLA Ops:
  0.6 21.9 %copy-start.3 = (bf16[1,4,512]{2,1,0:T(4,128)(2,1)S(1)}, bf16[1,4,512]{2,1,0:T(4,128)(2,1)}, u32[]{:S(2)}) copy-start(bf16[1,4,512]{2,1,0:T(4,128)(2,1)} %param.12) | copy-start | bytes 12292
  1.3 43.7 %copy-start.2 = (bf16[27,64,32]{1,2,0:T(8,128)(2,1)S(1)}, bf16[27,64,32]{1,2,0:T(8,128)(2,1)}, u32[]{:S(2)}) copy-start(bf16[27,64,32]{1,2,0:T(8,128)(2,1)} %param.17) | copy-start | bytes 331780
  5.4 40.6 %copy-start = (bf16[512,512]{1,0:T(8,128)(2,1)S(1)}, bf16[512,512]{1,0:T(8,128)(2,1)}, u32[]{:S(2)}) copy-start(bf16[512,512]{1,0:T(8,128)(2,1)} %constant.17.clone.high) | copy-start | bytes 1572868
  5.4 40.6 %copy-start.1 = (bf16[512,512]{1,0:T(8,128)(2,1)S(1)}, bf16[512,512]{1,0:T(8,128)(2,1)}, u32[]{:S(2)}) copy-start(bf16[512,512]{1,0:T(8,128)(2,1)} %constant.18.clone.low) | copy-start | bytes 1572868
  5.4 29.9 %all-to-all-start = ((bf16[64,16,128]{2,1,0:T(8,128)(2,1)}), bf16[64,16,128]{2,1,0:T(8,128)(2,1)S(1)}, u32[]{:S(2)}, u32[]{:S(2)}) async-start(bf16[64,16,128]{2,1,0:T(8,128)(2,1)} %get-tuple-element.9), calls=%async_computation | async-start | bytes 524288 | tf_op jit(solution)/shard_map/all_to_all | solution.py:447
  22.5 8.9 %collective-permute-start = (bf16[4,512]{1,0:T(4,128)(2,1)S(1)}, bf16[4,512]{1,0:T(4,128)(2,1)S(1)}, u32[]{:S(2)}, u32[]{:S(2)}) collective-permute-start(bf16[4,512]{1,0:T(4,128)(2,1)S(1)} %bitcast.13), channel_id=1, source_target_pairs={{0,256},{64,320},{128,384},{192,448},{256,0},{320,64},{384,128},{4... | collective-permute-start | bytes 12296 | tf_op jit(solution)/shard_map/ppermute | solution.py:440
  31.4 3.9 %copy-start.4 = (bf16[4,512]{1,0:T(4,128)(2,1)}, bf16[4,512]{1,0:T(4,128)(2,1)S(1)}, u32[]{:S(2)}) copy-start(bf16[4,512]{1,0:T(4,128)(2,1)S(1)} %collective-permute-done.other) | copy-start | bytes 12292
  37.3 17.7 %all-to-all-start.1 = ((bf16[8,96,384]{2,1,0:T(8,128)(2,1)}), bf16[8,96,384]{2,1,0:T(8,128)(2,1)S(1)}, u32[]{:S(2)}, u32[]{:S(2)}) async-start(bf16[8,96,384]{2,1,0:T(8,128)(2,1)} %regroup.1), calls=%async_computation.1 | async-start | bytes 1179648 | tf_op jit(solution)/shard_map/all_to_all | solution.py:448

commit v4 on v3

--- a/solution.py
+++ b/solution.py
@@ -48,19 +48,27 @@
     return lax.dot_general(a, b, (dims, ((), ())), preferred_element_type=F32)
 
 
-def warp_kernel(shift, ids, raw, table, out, own, mats, sems):
-    copies = [
-        pltpu.make_async_copy(table.at[ids[0, c]], mats.at[c], sems.at[c]) for c in range(CH)
+def warp_kernel(shift, ids, tiles, table, out, own, raw, mats, chosen, sent, sems):
+    inward = [
+        pltpu.make_async_copy(tiles, raw, sems.at[0]),
+        pltpu.make_async_copy(ids, chosen, sems.at[1]),
     ]
-    for copy in copies:
+    inward += [
+        pltpu.make_async_copy(table.at[k], mats.at[k], sems.at[2 + k]) for k in range(len(mats))
+    ]
+    for copy in inward:
         copy.start()
     by = shift[0, 0]
+    inward[0].wait()
+    turned = []
+    for c in range(CH):
+        rows = jnp.concatenate([raw[c, z].astype(F32) for z in range(DEPTH)], axis=0)
+        turned.append(pltpu.roll(rows, by, 1).astype(BF))
+    for copy in inward[1:]:
+        copy.wait()
     warped = []
     for c in range(CH):
-        rows = jnp.concatenate([raw[c, z].astype(F32) for z in range(DEPTH)], axis=0)
-        rows = pltpu.roll(rows, by, 1).astype(BF)
-        copies[c].wait()
-        result = dot(rows, mats[c], ((1,), (0,)))
+        result = dot(turned[c], mats[chosen[0, c]], ((1,), (0,)))
         own[c] = result.astype(BF)
         warped.append(result.reshape(DEPTH // 2, 2 * ROWS, WIDTH))
     low = iota((DEPTH // 2, 2 * ROWS, WIDTH), 1) < ROWS
@@ -85,6 +93,7 @@
         here = (lane >= to) & (lane < to + width)
         return jnp.where(here if only is None else here & (row == only), value, base)
 
+    outward = []
     for half in range(HALVES):
         start = 64 * half
         main = put(left, right, start, 64, 64) if half == 0 else put(right, left, start, 0, 64)
@@ -97,25 +106,32 @@
         more = put(more, right, outer, slot + PLANE, PLANE)
         more = put(more, before, outer, 64 + slot // 2, PLANE, 2, 3)
         more = put(more, after, outer, 96 + slot // 2, PLANE, 2, 2)
-        out[half * PAIRS : (half + 1) * PAIRS] = jnp.concatenate([main, more], axis=1).astype(BF)
+        part = slice(half * PAIRS, (half + 1) * PAIRS)
+        sent[part] = jnp.concatenate([main, more], axis=1).astype(BF)
+        copy = pltpu.make_async_copy(sent.at[part], out.at[part], sems.at[6 + half])
+        copy.start()
+        outward.append(copy)
+    for copy in outward:
+        copy.wait()
 
 
 def warp(shift, ids, raw, table, interpret=False):
+    away = pl.BlockSpec(memory_space=pl.ANY)
+    shape = (TILES, 2 * BRICK, DEPTH * PLANE)
     return pl.pallas_call(
         warp_kernel,
         out_shape=(
-            pltpu.VMEM((TILES, 2 * BRICK, DEPTH * PLANE), BF),
+            jax.ShapeDtypeStruct(shape, BF),
             pltpu.VMEM((CH, DEPTH * ROWS, WIDTH), BF),
         ),
-        in_specs=[
-            pl.BlockSpec(memory_space=pltpu.SMEM),
-            pl.BlockSpec(memory_space=pltpu.SMEM),
-            pl.BlockSpec(memory_space=pltpu.VMEM),
-            pl.BlockSpec(memory_space=pl.ANY),
-        ],
+        in_specs=[pl.BlockSpec(memory_space=pltpu.SMEM), away, away, away],
+        out_specs=(away, pl.BlockSpec(memory_space=pltpu.VMEM)),
         scratch_shapes=[
-            pltpu.VMEM((CH, WIDTH, WIDTH), BF),
-            pltpu.SemaphoreType.DMA((CH,)),
+            pltpu.VMEM(raw.shape, BF),
+            pltpu.VMEM(table.shape, BF),
+            pltpu.SMEM(ids.shape, jnp.int32),
+            pltpu.VMEM(shape, BF),
+            pltpu.SemaphoreType.DMA((8,)),
         ],
         name="warp",
         interpret=interpret,
@@ -167,7 +183,7 @@
     )(unmix, conv, bias, project)
 
 
-def regroup_kernel(got, band, other, out, tall):
+def regroup_kernel(got, band, other, out, tall, sent, sems):
     tall[...] = got[...].astype(F32).reshape(TILES * 2 * BRICK, DEPTH * PLANE)
     turned = []
     for q in range(BRICK):
@@ -196,6 +212,7 @@
         pair = refs[:, p * 64 : (p + 2) * 64]
         marks.append(jnp.concatenate([pltpu.roll(pair, 64, 1), pair], axis=0))
     lane = iota((PLANE, 128), 1)
+    outward = []
     for core in range(2):
         for slot in range(6):
             pieces = [piece(slot, core * BRICK + k) for k in range(SPAN)]
@@ -218,16 +235,30 @@
                     w = step * HALVES + half
                     last = jnp.where(lane >= 64, marks[w], blocks[2]) if w < 4 else blocks[2]
                     rows = slice(w * PLANE, (w + 1) * PLANE)
-                    out[2 * far + core, rows, :128] = main[0]
-                    out[2 * far + core, rows, 128:256] = main[1]
-                    out[2 * far + core, rows, 256:] = last.astype(BF)
+                    sent[2 * far + core, rows, :128] = main[0]
+                    sent[2 * far + core, rows, 128:256] = main[1]
+                    sent[2 * far + core, rows, 256:] = last.astype(BF)
+            if slot >= 2:
+                peer = 2 * (slot - 2) + core
+                copy = pltpu.make_async_copy(sent.at[peer], out.at[peer], sems.at[peer])
+                copy.start()
+                outward.append(copy)
+    for copy in outward:
+        copy.wait()
 
 
 def regroup(got, band, other, interpret=False):
+    shape = (2 * FAR, LINES, PADDED)
     return pl.pallas_call(
         regroup_kernel,
-        out_shape=pltpu.VMEM((2 * FAR, LINES, PADDED), BF),
-        scratch_shapes=[pltpu.VMEM((TILES * 2 * BRICK, DEPTH * PLANE), F32)],
+        out_shape=jax.ShapeDtypeStruct(shape, BF),
+        in_specs=[pl.BlockSpec(memory_space=pltpu.VMEM)] * 3,
+        out_specs=pl.BlockSpec(memory_space=pl.ANY),
+        scratch_shapes=[
+            pltpu.VMEM((TILES * 2 * BRICK, DEPTH * PLANE), F32),
+            pltpu.VMEM(shape, BF),
+            pltpu.SemaphoreType.DMA((2 * FAR,)),
+        ],
         name="regroup",
         interpret=interpret,
     )(got, band, other)
@@ -258,14 +289,16 @@
     )(own, high, low)
 
 
-def correlate_kernel(place, own, got, high, low, out):
+def correlate(place, own, got, high, low, out):
     half = WIDTH // 2
     count = CH * DEPTH * ROWS
     left = iota((2 * ROWS, 128), 1) < 64
     near, away = [], []
     for far in range(FAR):
         pieces = jnp.where(
-            place[1] == 0, got[2 * far].astype(F32), got[2 * far + 1].astype(F32)
+            place[1, :1, :128] == 0,
+            got[2 * far, :64, 256:].astype(F32),
+            got[2 * far + 1, :64, 256:].astype(F32),
         )
         lanes = []
         for p in range(0, 8, 2):
@@ -276,7 +309,7 @@
         near.append(rows[:ROWS])
         away.append(rows[ROWS:])
     near, away = jnp.concatenate(near, axis=0), jnp.concatenate(away, axis=0)
-    first_half = place[0] == 0
+    first_half = place[0, :1, :] == 0
     band = jnp.concatenate(
         [jnp.where(first_half, near, away), jnp.where(first_half, away, near)], axis=0
     ).astype(BF)
@@ -304,30 +337,15 @@
             out[c, z] = inverse[start : start + ROWS]
 
 
-def correlate(place, own, got, high, low, interpret=False):
-    def whole(*shape):
-        return pl.BlockSpec(shape, lambda i: (0,) * len(shape))
-
-    return pl.pallas_call(
-        correlate_kernel,
-        grid=(1,),
-        in_specs=[
-            pl.BlockSpec(memory_space=pltpu.SMEM),
-            whole(*own.shape),
-            pl.BlockSpec((2 * FAR, 64, 128), lambda i: (0, 0, 2)),
-            whole(WIDTH, WIDTH),
-            whole(WIDTH, WIDTH),
-        ],
-        out_specs=whole(CH, DEPTH, ROWS, WIDTH),
-        out_shape=jax.ShapeDtypeStruct((CH, DEPTH, ROWS, WIDTH), F32),
-        name="correlate",
-        interpret=interpret,
-    )(place, own, got, high, low)
-
-
-def layer_kernel(got, spread, banded, biases, projected, out, wide, first, second, weights, sem):
-    fetch = pltpu.make_async_copy(banded, weights, sem.at[0])
+def finish_kernel(
+    place, own, got, high, low, spread, banded, biases, projected, away, out,
+    found, wide, first, second, weights, sems,
+):
+    fetch = pltpu.make_async_copy(banded, weights, sems.at[0])
     fetch.start()
+    correlate(place, own, got, high, low, found)
+    leave = pltpu.make_async_copy(found, away, sems.at[1])
+    leave.start()
     n = MIXED * ROWS
     pair = iota((SPAN, PAIRS, n), 1).reshape(ALONG, n)
     right = iota((ALONG, n), 1) >= 64
@@ -404,24 +422,32 @@
         second[pl.ds(x, MIXED, stride=BRICK), :] = rows[:, 128:]
     out[:, :, :128] = first[...].reshape(MIXED, BRICK, 128).astype(BF)
     out[:, :, 128:] = second[...].reshape(MIXED, BRICK, 128).astype(BF)
-
-
-def layer(got, spread, banded, biases, projected, interpret=False):
+    leave.wait()
+
+
+def finish(place, own, got, high, low, spread, banded, biases, projected, interpret=False):
     inside = pl.BlockSpec(memory_space=pltpu.VMEM)
+    outside = pl.BlockSpec(memory_space=pl.ANY)
+    found = (CH, DEPTH, ROWS, WIDTH)
     return pl.pallas_call(
-        layer_kernel,
-        in_specs=[inside, inside, pl.BlockSpec(memory_space=pl.ANY), inside, inside],
-        out_shape=jax.ShapeDtypeStruct((MIXED, BRICK, TILES * ROWS), BF),
+        finish_kernel,
+        in_specs=[inside] * 6 + [outside] + [inside] * 2,
+        out_specs=(outside, inside),
+        out_shape=(
+            jax.ShapeDtypeStruct(found, F32),
+            jax.ShapeDtypeStruct((MIXED, BRICK, TILES * ROWS), BF),
+        ),
         scratch_shapes=[
+            pltpu.VMEM(found, F32),
             pltpu.VMEM((2, ALONG, 3 * 256), BF),
             pltpu.VMEM((MIXED * BRICK, 128), F32),
             pltpu.VMEM((MIXED * BRICK, 128), F32),
-            pltpu.VMEM((HIDDEN * ROWS, 9 * 256), BF),
-            pltpu.SemaphoreType.DMA((1,)),
+            pltpu.VMEM(banded.shape, BF),
+            pltpu.SemaphoreType.DMA((2,)),
         ],
-        name="layer",
+        name="finish",
         interpret=interpret,
-    )(got, spread, banded, biases, projected)
+    )(place, own, got, high, low, spread, banded, biases, projected)
 
 
 def close(value):
@@ -436,19 +462,22 @@
         lax.all_to_all, axis_name=("round", "tile"), split_axis=0, concat_axis=0, tiled=True
     )
     place = jnp.stack([lax.axis_index("round") >> 2, lax.axis_index("tile") & 1])
-    band = ref_bands[0]
-    other = lax.ppermute(band, "round", [(i, (i + FAR) % ROUNDS) for i in range(ROUNDS)])
+    place = close(jnp.broadcast_to(place[:, None, None], (2, 8, WIDTH)))
+    band = close(ref_bands[0])
+    ahead = [(i, (i + FAR) % ROUNDS) for i in range(ROUNDS)]
+    other = close(lax.ppermute(band, "round", ahead))
     spread, banded, biases, projected = prepare(
         unmix, conv_weight, conv_bias.reshape(1, -1), out_weight
     )
     spread, biases, projected = map(close, (spread, biases, projected))
     high, low = close(jnp.asarray(high)), close(jnp.asarray(low))
-    sent, own = map(close, warp(shifts, matrix_ids, raw_tiles[0], resample))
+    sent, own = warp(shifts, matrix_ids, raw_tiles[0], resample)
     got = close(swap(sent, axis_index_groups=RINGS))
-    slabs = close(swap(close(regroup(got, band, other)), axis_index_groups=NEAR))
-    spectra = close(own_spectra(own, high, low))
-    correlation = correlate(place, spectra, slabs, high, low)
-    features = layer(slabs, spread, banded, biases, projected)
+    slabs = close(swap(regroup(got, band, other), axis_index_groups=NEAR))
+    spectra = close(own_spectra(close(own), high, low))
+    correlation, features = finish(
+        place, spectra, slabs, high, low, spread, banded, biases, projected
+    )
     return (correlation[None], features[:, None])
 
 

time: 61.1 us -> 58.1 us (0.951)
  Pallas kernels: 14.6 us -> 11.5 us
    pallas_call x4 -> x3, Pallas kernels: 11.8 us -> 8.76 us  [the longest x1 4.34 us: finish(): pl.pallas_call(finish_kernel, in_specs=[inside] * 6 + [outside] + [inside...]
  transfers between devices with their start and end apart: 3 -> 3, of which waited for: 3 -> 3; matrix products, arithmetic and copies ran while one was open for 3% -> 2% of each run, Pallas kernels for 5% -> 5%
where the time goes in v4:
time: 58.1 us; the launch traced here: 57.7 us
  starting transfers between devices  31.6 us (54%)
  waiting for transfers between devices  12.1 us (21%)
  Pallas kernels  11.5 us (20%)
  between operations  1.37 us (2%)
  local copies, waits for them, and re-layouts  1.09 us (2%)
    all_to_all x1, starting transfers between devices, body(): got = close(swap(sent, axis_index_groups=RINGS))  17.3 us
    all_to_all x1, starting transfers between devices, body(): slabs = close(swap(regroup(got, band, other), axis_index_groups=NEAR))  7.37 us
    ppermute x1, starting transfers between devices, body(): other = close(lax.ppermute(band, 'round', ahead))  6.93 us
    all_to_all x1, waiting for transfers between devices, body(): slabs = close(swap(regroup(got, band, other), axis_index_groups=NEAR))  6.21 us
    pallas_call x1, Pallas kernels, finish(): pl.pallas_call(finish_kernel, in_specs=[inside] * 6 + [outside] + [inside...  4.34 us
    all_to_all x1, waiting for transfers between devices, body(): got = close(swap(sent, axis_index_groups=RINGS))  3.94 us
    pallas_call x1, Pallas kernels, warp(): pl.pallas_call(warp_kernel, out_shape=(jax.ShapeDtypeStruct(shape, BF), p...  3.18 us
    pallas_call x1, Pallas kernels, prepare(): pl.pallas_call(prepare_kernel, out_shape=(pltpu.VMEM((MIXED * ROWS, MIXED...  2.45 us
  transfers between devices with their start and end apart: 3, of which 3 were waited for; matrix products, arithmetic and copies ran while one was open for 2% of the time, Pallas kernels for 5%

profile of v4, /device:TPU:1, one launch (start us, length us, event | category | flops | bytes accessed | tf_op | source)
XLA Modules:
  0.0 57.7 jit_solution(17911042251898419234)
XLA Ops:
  0.6 0.0 copy-start.2
  1.3 0.0 copy-start.3
  1.3 3.2 %warp.1 = (bf16[64,16,128]{2,1,0:T(8,128)(2,1)}, bf16[4,32,512]{2,1,0:T(8,128)(2,1)S(1)}) custom-call(s32[1,1]{1,0:T(1,128)S(6)} %copy.15.shift, s32[1,4]{1,0:T(1,128)} %ids.1, bf16[4,8,4,512]{3,2,1,0:T(4,128)(2,1)} %bitcast.11, bf16[4,512,512]{2,1,0:T(8,128)(2,1)} %table.1), custom_call_target="tpu_custom_call" | custom-call | tf_op jit(solution)/shard_map/warp/pallas_call | solution.py:121
  4.5 0.0 copy-start
  4.5 0.0 copy-start.1
  4.5 17.3 %all-to-all-start = ((bf16[64,16,128]{2,1,0:T(8,128)(2,1)}), bf16[64,16,128]{2,1,0:T(8,128)(2,1)S(1)}, u32[]{:S(2)}, u32[]{:S(2)}) async-start(bf16[64,16,128]{2,1,0:T(8,128)(2,1)} %get-tuple-element.11), calls=%async_computation | async-start | bytes 524288 | tf_op jit(solution)/shard_map/all_to_all | solution.py:475
  21.8 0.0 copy-done.2
  21.8 6.9 %collective-permute-start = (bf16[4,512]{1,0:T(4,128)(2,1)S(1)}, bf16[4,512]{1,0:T(4,128)(2,1)S(1)}, u32[]{:S(2)}, u32[]{:S(2)}) collective-permute-start(bf16[4,512]{1,0:T(4,128)(2,1)S(1)} %bitcast.9), channel_id=1, source_target_pairs={{0,256},{64,320},{128,384},{192,448},{256,0},{320,64},{384,128},{4... | collective-permute-start | bytes 12296 | tf_op jit(solution)/shard_map/ppermute | solution.py:468
  28.7 1.9 %collective-permute-done.other = bf16[4,512]{1,0:T(4,128)(2,1)S(1)} collective-permute-done((bf16[4,512]{1,0:T(4,128)(2,1)S(1)}, bf16[4,512]{1,0:T(4,128)(2,1)S(1)}, u32[]{:S(2)}, u32[]{:S(2)}) %collective-permute-start) | collective-permute-done | bytes 4128 | tf_op jit(solution)/shard_map/ppermute | solution.py:468
  30.7 3.9 %all-to-all-done.got = bf16[64,16,128]{2,1,0:T(8,128)(2,1)S(1)} async-done(((bf16[64,16,128]{2,1,0:T(8,128)(2,1)}), bf16[64,16,128]{2,1,0:T(8,128)(2,1)S(1)}, u32[]{:S(2)}, u32[]{:S(2)}) %all-to-all-start) | async-done | bytes 262176 | tf_op jit(solution)/shard_map/all_to_all | solution.py:475
  34.6 1.2 %regroup.1 = bf16[8,96,384]{2,1,0:T(8,128)(2,1)} custom-call(bf16[64,16,128]{2,1,0:T(8,128)(2,1)S(1)} %all-to-all-done.got, bf16[4,512]{1,0:T(4,128)(2,1)S(1)} %bitcast.10, bf16[4,512]{1,0:T(4,128)(2,1)S(1)} %collective-permute-done.other), custom_call_target="tpu_custom_call" | custom-call | tf_op jit(solution)/shard_map/regroup/pallas_call | solution.py:252
  35.9 7.4 %all-to-all-start.1 = ((bf16[8,96,384]{2,1,0:T(8,128)(2,1)}), bf16[8,96,384]{2,1,0:T(8,128)(2,1)S(1)}, u32[]{:S(2)}, u32[]{:S(2)}) async-start(bf16[8,96,384]{2,1,0:T(8,128)(2,1)} %regroup.1), calls=%async_computation.1 | async-start | bytes 1179648 | tf_op jit(solution)/shard_map/all_to_all | solution.py:476
  43.3 0.0 copy-done.3
  43.3 1.0 %copy.13.conv = bf16[27,64,32]{2,1,0:T(8,128)(2,1)} copy(bf16[27,64,32]{1,2,0:T(8,128)(2,1)S(1)} %copy-done.3) | data formatting | bytes 221184 | tf_op args[6]
  44.3 0.0 copy-done
  44.3 0.0 copy-done.1
  44.3 0.3 spectra.1.own
  44.6 2.5 %prepare.1 = (bf16[128,128]{1,0:T(8,128)(2,1)S(1)}, bf16[256,2304]{1,0:T(8,128)(2,1)}, f32[1,256]{1,0:T(1,128)S(1)}, bf16[128,256]{1,0:T(8,128)(2,1)S(1)}) custom-call(bf16[32,32]{1,0:T(8,128)(2,1)} %unmix.1, bf16[27,64,32]{2,1,0:T(8,128)(2,1)} %copy.13.conv, f32[1,64]{1,0:T(1,128)} %bitcast.12, bf16[32,64]{1,0:T(8,128)(2,1)} %project.1), custom_call_target="tpu_custom_call" | custom-call | tf_op jit(solution)/shard_map/prepare/pallas_call | solution.py:173
  47.0 0.1 pad_add_fusion
  47.1 6.2 %all-to-all-done.1.got = bf16[8,96,384]{2,1,0:T(8,128)(2,1)S(1)} async-done(((bf16[8,96,384]{2,1,0:T(8,128)(2,1)}), bf16[8,96,384]{2,1,0:T(8,128)(2,1)S(1)}, u32[]{:S(2)}, u32[]{:S(2)}) %all-to-all-start.1) | async-done | bytes 589856 | tf_op jit(solution)/shard_map/all_to_all | solution.py:476
  53.3 0.1 broadcast_in_dim.12.place
  53.4 4.3 %finish.1 = (f32[4,8,4,512]{3,2,1,0:T(4,128)}, bf16[32,8,256]{2,1,0:T(8,128)(2,1)}) custom-call(s32[2,8,512]{2,1,0:T(8,128)S(1)} %broadcast_in_dim.12.place, f32[128,512]{1,0:T(8,128)S(1)} %spectra.1.own, bf16[8,96,384]{2,1,0:T(8,128)(2,1)S(1)} %all-to-all-done.1.got, bf16[512,512]{1,0:T(8,128)(2,1)S(1)} %copy-done, bf16[512,512]{1,0:T(8,128)(2,1)S(1)} %copy-done.1, ...), custom_call_target="tpu_custom_call" | custom-call | tf_op jit(solution)/shard_map/finish/pallas_call | solution.py:432
Async XLA Ops:
  0.6 21.2 %copy-start.2 = (bf16[1,4,512]{2,1,0:T(4,128)(2,1)S(1)}, bf16[1,4,512]{2,1,0:T(4,128)(2,1)}, u32[]{:S(2)}) copy-start(bf16[1,4,512]{2,1,0:T(4,128)(2,1)} %param.12) | copy-start | bytes 12292
  1.3 42.0 %copy-start.3 = (bf16[27,64,32]{1,2,0:T(8,128)(2,1)S(1)}, bf16[27,64,32]{1,2,0:T(8,128)(2,1)}, u32[]{:S(2)}) copy-start(bf16[27,64,32]{1,2,0:T(8,128)(2,1)} %param.17) | copy-start | bytes 331780
  4.5 39.8 %copy-start = (bf16[512,512]{1,0:T(8,128)(2,1)S(1)}, bf16[512,512]{1,0:T(8,128)(2,1)}, u32[]{:S(2)}) copy-start(bf16[512,512]{1,0:T(8,128)(2,1)} %constant.17.clone.high) | copy-start | bytes 1572868
  4.5 39.7 %copy-start.1 = (bf16[512,512]{1,0:T(8,128)(2,1)S(1)}, bf16[512,512]{1,0:T(8,128)(2,1)}, u32[]{:S(2)}) copy-start(bf16[512,512]{1,0:T(8,128)(2,1)} %constant.18.clone.low) | copy-start | bytes 1572868
  4.5 30.1 %all-to-all-start = ((bf16[64,16,128]{2,1,0:T(8,128)(2,1)}), bf16[64,16,128]{2,1,0:T(8,128)(2,1)S(1)}, u32[]{:S(2)}, u32[]{:S(2)}) async-start(bf16[64,16,128]{2,1,0:T(8,128)(2,1)} %get-tuple-element.11), calls=%async_computation | async-start | bytes 524288 | tf_op jit(solution)/shard_map/all_to_all | solution.py:475
  21.8 8.9 %collective-permute-start = (bf16[4,512]{1,0:T(4,128)(2,1)S(1)}, bf16[4,512]{1,0:T(4,128)(2,1)S(1)}, u32[]{:S(2)}, u32[]{:S(2)}) collective-permute-start(bf16[4,512]{1,0:T(4,128)(2,1)S(1)} %bitcast.9), channel_id=1, source_target_pairs={{0,256},{64,320},{128,384},{192,448},{256,0},{320,64},{384,128},{4... | collective-permute-start | bytes 12296 | tf_op jit(solution)/shard_map/ppermute | solution.py:468
  35.9 17.4 %all-to-all-start.1 = ((bf16[8,96,384]{2,1,0:T(8,128)(2,1)}), bf16[8,96,384]{2,1,0:T(8,128)(2,1)S(1)}, u32[]{:S(2)}, u32[]{:S(2)}) async-start(bf16[8,96,384]{2,1,0:T(8,128)(2,1)} %regroup.1), calls=%async_computation.1 | async-start | bytes 1179648 | tf_op jit(solution)/shard_map/all_to_all | solution.py:476

commit v5 on v4

--- a/solution.py
+++ b/solution.py
@@ -22,6 +22,7 @@
 LINES = 3 * HALVES * PLANE
 ALONG = SPAN * PAIRS
 PADDED = 384
+SMALL = 9 * 256
 
 
 def device(half, far, pair, core):
@@ -50,11 +51,15 @@
 
 def warp_kernel(shift, ids, tiles, table, out, own, raw, mats, chosen, sent, sems):
     inward = [
-        pltpu.make_async_copy(tiles, raw, sems.at[0]),
-        pltpu.make_async_copy(ids, chosen, sems.at[1]),
+        pltpu.make_async_copy(tiles, raw, sems.at[0, 0]),
+        pltpu.make_async_copy(ids, chosen, sems.at[1, 0]),
     ]
     inward += [
-        pltpu.make_async_copy(table.at[k], mats.at[k], sems.at[2 + k]) for k in range(len(mats))
+        pltpu.make_async_copy(
+            table.at[k, pl.ds(at, 128)], mats.at[k, pl.ds(at, 128)], sems.at[2 + k, at // 128]
+        )
+        for k in range(CH)
+        for at in range(0, WIDTH, 128)
     ]
     for copy in inward:
         copy.start()
@@ -108,7 +113,7 @@
         more = put(more, after, outer, 96 + slot // 2, PLANE, 2, 2)
         part = slice(half * PAIRS, (half + 1) * PAIRS)
         sent[part] = jnp.concatenate([main, more], axis=1).astype(BF)
-        copy = pltpu.make_async_copy(sent.at[part], out.at[part], sems.at[6 + half])
+        copy = pltpu.make_async_copy(sent.at[part], out.at[part], sems.at[6 + half, 0])
         copy.start()
         outward.append(copy)
     for copy in outward:
@@ -131,14 +136,16 @@
             pltpu.VMEM(table.shape, BF),
             pltpu.SMEM(ids.shape, jnp.int32),
             pltpu.VMEM(shape, BF),
-            pltpu.SemaphoreType.DMA((8,)),
+            pltpu.SemaphoreType.DMA((8, 4)),
         ],
         name="warp",
         interpret=interpret,
     )(shift, ids, raw, table)
 
 
-def prepare_kernel(unmix, conv, bias, project, spread, banded, biases, projected):
+def prepare_kernel(unmix, conv, project, own, high, low, banded, spectra):
+    rows = own[...].reshape(CH * DEPTH * ROWS, WIDTH)
+    spectra[...] = dot(rows, high[...], ((1,), (0,))) + dot(rows, low[...], ((1,), (0,)))
     n = MIXED * ROWS
     k = iota((n, MIXED), 0)
     source = (k // PLANE % HALVES * FAR + k // (HALVES * PLANE)) * CH + k // ROWS % CH
@@ -147,7 +154,8 @@
     tall = dot(pick_in, unmix[...], ((1,), (1,))).astype(BF)
     wide = dot(tall, pick_out, ((1,), (0,)))
     own = iota((n, n), 0) % ROWS == iota((n, n), 1) // MIXED
-    spread[...] = jnp.where(own, wide, 0.0).astype(BF)
+    banded[n:, SMALL : SMALL + n] = jnp.where(own, wide, 0.0).astype(BF)
+    banded[n:, SMALL + n :] = jnp.zeros((n, n), BF)
     gap = jnp.zeros((HIDDEN, MIXED), BF)
     for ab in range(9):
         at = (ab % 3 * 3 + ab // 3) * 256
@@ -162,25 +170,23 @@
             banded[y * HIDDEN : (y + 1) * HIDDEN, at : at + 256] = jnp.concatenate(
                 rows[y], axis=1
             )
-    biases[...] = jnp.concatenate([bias[...]] * ROWS, axis=1)
     hole = jnp.zeros((MIXED, HIDDEN), BF)
     for y in range(ROWS):
         row = [project[...] if i == y else hole for i in range(ROWS)]
-        projected[y * MIXED : (y + 1) * MIXED, :] = jnp.concatenate(row, axis=1)
-
-
-def prepare(unmix, conv, bias, project, interpret=False):
+        banded[y * MIXED : (y + 1) * MIXED, SMALL:] = jnp.concatenate(row, axis=1)
+
+
+def prepare(unmix, conv, project, own, high, low, interpret=False):
     return pl.pallas_call(
         prepare_kernel,
         out_shape=(
-            pltpu.VMEM((MIXED * ROWS, MIXED * ROWS), BF),
-            jax.ShapeDtypeStruct((HIDDEN * ROWS, 9 * 256), BF),
-            pltpu.VMEM((1, HIDDEN * ROWS), F32),
-            pltpu.VMEM((MIXED * ROWS, HIDDEN * ROWS), BF),
+            pltpu.VMEM((HIDDEN * ROWS, SMALL + 256), BF),
+            pltpu.HBM((CH * DEPTH * ROWS, WIDTH), F32),
         ),
+        compiler_params=pltpu.CompilerParams(vmem_limit_bytes=16 << 20),
         name="prepare",
         interpret=interpret,
-    )(unmix, conv, bias, project)
+    )(unmix, conv, project, own, high, low)
 
 
 def regroup_kernel(got, band, other, out, tall, sent, sems):
@@ -260,6 +266,7 @@
             pltpu.SemaphoreType.DMA((2 * FAR,)),
         ],
         name="regroup",
+        compiler_params=pltpu.CompilerParams(vmem_limit_bytes=16 << 20),
         interpret=interpret,
     )(got, band, other)
 
@@ -273,20 +280,6 @@
     high = table.astype(jnp.bfloat16)
     low = (table - high.astype(np.float32)).astype(jnp.bfloat16)
     return high, low
-
-
-def spectra_kernel(own, high, low, out):
-    rows = own[...].reshape(CH * DEPTH * ROWS, WIDTH)
-    out[...] = dot(rows, high[...], ((1,), (0,))) + dot(rows, low[...], ((1,), (0,)))
-
-
-def own_spectra(own, high, low, interpret=False):
-    return pl.pallas_call(
-        spectra_kernel,
-        out_shape=pltpu.VMEM((CH * DEPTH * ROWS, WIDTH), F32),
-        name="spectra",
-        interpret=interpret,
-    )(own, high, low)
 
 
 def correlate(place, own, got, high, low, out):
@@ -338,14 +331,15 @@
 
 
 def finish_kernel(
-    place, own, got, high, low, spread, banded, biases, projected, away, out,
-    found, wide, first, second, weights, sems,
+    place, spectra, got, high, low, banded, bias, away, out,
+    found, wide, first, second, own, shared, sems,
 ):
-    fetch = pltpu.make_async_copy(banded, weights, sems.at[0])
-    fetch.start()
-    correlate(place, own, got, high, low, found)
-    leave = pltpu.make_async_copy(found, away, sems.at[1])
-    leave.start()
+    fetch = [
+        pltpu.make_async_copy(spectra, own, sems.at[2]),
+        pltpu.make_async_copy(bias, shared, sems.at[1]),
+    ]
+    for copy in fetch:
+        copy.start()
     n = MIXED * ROWS
     pair = iota((SPAN, PAIRS, n), 1).reshape(ALONG, n)
     right = iota((ALONG, n), 1) >= 64
@@ -362,7 +356,7 @@
                 ],
                 axis=0,
             )
-            plane = dot(mixed, spread[...], ((0,), (0,)))[:ALONG].astype(BF)
+            plane = dot(mixed, banded[n:, SMALL : SMALL + n], ((0,), (0,)))[:ALONG].astype(BF)
             wide[core, :, at : at + 128] = plane
             planes.append(plane.astype(F32))
         even, odd = planes
@@ -372,15 +366,19 @@
         lower = jnp.where(pair == PAIRS - 1, 0.0, pltpu.roll(even, ALONG - 1, 0))
         wide[0, :, at + 128 : at + 256] = jnp.where(right, upper, odd).astype(BF)
         wide[1, :, at + 128 : at + 256] = jnp.where(right, even, lower).astype(BF)
-    fetch.wait()
-    total = biases[...]
+    for copy in fetch:
+        copy.wait()
+    correlate(place, own, got, high, low, found)
+    leave = pltpu.make_async_copy(found, away, sems.at[0])
+    leave.start()
+    total = jnp.concatenate([shared[...]] * ROWS, axis=1)
     for b in range(3):
         rows = jnp.concatenate(
             [wide[core, b * PAIRS : b * PAIRS + count, :] for core in range(2)], axis=0
         )
-        total = total + dot(rows, weights[:, b * 768 : (b + 1) * 768], ((1,), (1,)))
+        total = total + dot(rows, banded[:, b * 768 : (b + 1) * 768], ((1,), (1,)))
     hidden = jax.nn.gelu(total).astype(BF)
-    mixed = dot(hidden, projected[...], ((1,), (1,)))
+    mixed = dot(hidden, banded[:n, SMALL:], ((1,), (1,)))
     done = centre + mixed
     left = iota((MIXED, 128), 1) < 64
     k = iota((256, 256), 0)
@@ -425,13 +423,13 @@
     leave.wait()
 
 
-def finish(place, own, got, high, low, spread, banded, biases, projected, interpret=False):
+def finish(place, own, got, high, low, banded, bias, interpret=False):
     inside = pl.BlockSpec(memory_space=pltpu.VMEM)
     outside = pl.BlockSpec(memory_space=pl.ANY)
     found = (CH, DEPTH, ROWS, WIDTH)
     return pl.pallas_call(
         finish_kernel,
-        in_specs=[inside] * 6 + [outside] + [inside] * 2,
+        in_specs=[inside, pl.BlockSpec(memory_space=pltpu.HBM)] + [inside] * 4 + [outside],
         out_specs=(outside, inside),
         out_shape=(
             jax.ShapeDtypeStruct(found, F32),
@@ -442,12 +440,14 @@
             pltpu.VMEM((2, ALONG, 3 * 256), BF),
             pltpu.VMEM((MIXED * BRICK, 128), F32),
             pltpu.VMEM((MIXED * BRICK, 128), F32),
-            pltpu.VMEM(banded.shape, BF),
-            pltpu.SemaphoreType.DMA((2,)),
+            pltpu.VMEM(own.shape, F32),
+            pltpu.VMEM(bias.shape, F32),
+            pltpu.SemaphoreType.DMA((3,)),
         ],
         name="finish",
+        compiler_params=pltpu.CompilerParams(vmem_limit_bytes=16 << 20),
         interpret=interpret,
-    )(place, own, got, high, low, spread, banded, biases, projected)
+    )(place, own, got, high, low, banded, bias)
 
 
 def close(value):
@@ -466,18 +466,15 @@
     band = close(ref_bands[0])
     ahead = [(i, (i + FAR) % ROUNDS) for i in range(ROUNDS)]
     other = close(lax.ppermute(band, "round", ahead))
-    spread, banded, biases, projected = prepare(
-        unmix, conv_weight, conv_bias.reshape(1, -1), out_weight
-    )
-    spread, biases, projected = map(close, (spread, biases, projected))
     high, low = close(jnp.asarray(high)), close(jnp.asarray(low))
     sent, own = warp(shifts, matrix_ids, raw_tiles[0], resample)
     got = close(swap(sent, axis_index_groups=RINGS))
     slabs = close(swap(regroup(got, band, other), axis_index_groups=NEAR))
-    spectra = close(own_spectra(close(own), high, low))
-    correlation, features = finish(
-        place, spectra, slabs, high, low, spread, banded, biases, projected
-    )
+    prepared = prepare(unmix, conv_weight, out_weight, close(own), high, low)
+    banded = close(prepared[0])
+    spectra = pltpu.with_memory_space_constraint(prepared[1], pltpu.HBM)
+    bias = conv_bias.reshape(1, -1)
+    correlation, features = finish(place, spectra, slabs, high, low, banded, bias)
     return (correlation[None], features[:, None])
 
 

time: 58.1 us -> 58.3 us (level)
  waiting for transfers between devices: 12.1 us -> 14.5 us
  Pallas kernels: 11.5 us -> 9.97 us
  local copies, waits for them, and re-layouts: 1.09 us -> 0.37 us
    all_to_all x1, waiting for transfers between devices: 6.21 us -> 8.62 us  [body(): slabs = close(swap(regroup(got, band, other), axis_index_groups=NEAR))]
    pallas_call x3 -> x2, Pallas kernels: 7.09 us -> 5.33 us  [the longest x1 4.28 us: finish(): pl.pallas_call(finish_kernel, in_specs=[inside, pl.BlockSpec(memory_space...]
    unnamed x9 -> x15, local copies, waits for them, and re-layouts: 1.02 us -> 0.3 us
  transfers between devices with their start and end apart: 3 -> 3, of which waited for: 3 -> 3; matrix products, arithmetic and copies ran while one was open for 2% -> 1% of each run, Pallas kernels for 5% -> 2%
where the time goes in v5:
time: 58.3 us; the launch traced here: 57.9 us
  starting transfers between devices  31.6 us (54%)
  waiting for transfers between devices  14.5 us (25%)
  Pallas kernels  9.97 us (17%)
  between operations  1.43 us (2%)
    all_to_all x1, starting transfers between devices, body(): got = close(swap(sent, axis_index_groups=RINGS))  17.3 us
    all_to_all x1, waiting for transfers between devices, body(): slabs = close(swap(regroup(got, band, other), axis_index_groups=NEAR))  8.62 us
    all_to_all x1, starting transfers between devices, body(): slabs = close(swap(regroup(got, band, other), axis_index_groups=NEAR))  7.37 us
    ppermute x1, starting transfers between devices, body(): other = close(lax.ppermute(band, 'round', ahead))  6.93 us
    pallas_call x1, Pallas kernels, finish(): pl.pallas_call(finish_kernel, in_specs=[inside, pl.BlockSpec(memory_space...  4.28 us
    all_to_all x1, waiting for transfers between devices, body(): got = close(swap(sent, axis_index_groups=RINGS))  3.94 us
    pallas_call x1, Pallas kernels, warp(): pl.pallas_call(warp_kernel, out_shape=(jax.ShapeDtypeStruct(shape, BF), p...  3.44 us
    ppermute x1, waiting for transfers between devices, body(): other = close(lax.ppermute(band, 'round', ahead))  1.94 us
  transfers between devices with their start and end apart: 3, of which 3 were waited for; matrix products, arithmetic and copies ran while one was open for 1% of the time, Pallas kernels for 2%

profile of v5, /device:TPU:1, one launch (start us, length us, event | category | flops | bytes accessed | tf_op | source)
XLA Modules:
  0.0 57.9 jit_solution(13276406992700331023)
XLA Ops:
  0.6 0.0 copy-start.4
  1.3 0.0 copy-start.6
  1.3 3.4 %warp.1 = (bf16[64,16,128]{2,1,0:T(8,128)(2,1)}, bf16[4,32,512]{2,1,0:T(8,128)(2,1)S(1)}) custom-call(s32[1,1]{1,0:T(1,128)S(6)} %copy.15.shift, s32[1,4]{1,0:T(1,128)} %ids.1, bf16[4,8,4,512]{3,2,1,0:T(4,128)(2,1)} %bitcast.12, bf16[4,512,512]{2,1,0:T(8,128)(2,1)} %table.1), custom_call_target="tpu_custom_call" | custom-call | tf_op jit(solution)/shard_map/warp/pallas_call | solution.py:126
  4.8 0.0 copy-start
  4.8 0.0 copy-start.1
  4.8 0.0 copy-start.2
  4.8 0.0 copy-start.3
  4.8 17.3 %all-to-all-start = ((bf16[64,16,128]{2,1,0:T(8,128)(2,1)}), bf16[64,16,128]{2,1,0:T(8,128)(2,1)S(1)}, u32[]{:S(2)}, u32[]{:S(2)}) async-start(bf16[64,16,128]{2,1,0:T(8,128)(2,1)} %get-tuple-element.10), calls=%async_computation | async-start | bytes 524288 | tf_op jit(solution)/shard_map/all_to_all | solution.py:471
  22.1 0.0 copy-done.4
  22.1 0.0 copy-start.5
  22.1 6.9 %collective-permute-start = (bf16[4,512]{1,0:T(4,128)(2,1)S(1)}, bf16[4,512]{1,0:T(4,128)(2,1)S(1)}, u32[]{:S(2)}, u32[]{:S(2)}) collective-permute-start(bf16[4,512]{1,0:T(4,128)(2,1)S(1)} %bitcast.9), channel_id=1, source_target_pairs={{0,256},{64,320},{128,384},{192,448},{256,0},{320,64},{384,128},{4... | collective-permute-start | bytes 12296 | tf_op jit(solution)/shard_map/ppermute | solution.py:468
  29.0 1.9 %collective-permute-done.other = bf16[4,512]{1,0:T(4,128)(2,1)S(1)} collective-permute-done((bf16[4,512]{1,0:T(4,128)(2,1)S(1)}, bf16[4,512]{1,0:T(4,128)(2,1)S(1)}, u32[]{:S(2)}, u32[]{:S(2)}) %collective-permute-start) | collective-permute-done | bytes 4128 | tf_op jit(solution)/shard_map/ppermute | solution.py:468
  31.0 3.9 %all-to-all-done.got = bf16[64,16,128]{2,1,0:T(8,128)(2,1)S(1)} async-done(((bf16[64,16,128]{2,1,0:T(8,128)(2,1)}), bf16[64,16,128]{2,1,0:T(8,128)(2,1)S(1)}, u32[]{:S(2)}, u32[]{:S(2)}) %all-to-all-start) | async-done | bytes 262176 | tf_op jit(solution)/shard_map/all_to_all | solution.py:471
  34.9 1.2 %regroup.1 = bf16[8,96,384]{2,1,0:T(8,128)(2,1)} custom-call(bf16[64,16,128]{2,1,0:T(8,128)(2,1)S(1)} %all-to-all-done.got, bf16[4,512]{1,0:T(4,128)(2,1)S(1)} %bitcast.10, bf16[4,512]{1,0:T(4,128)(2,1)S(1)} %collective-permute-done.other), custom_call_target="tpu_custom_call" | custom-call | tf_op jit(solution)/shard_map/regroup/pallas_call | solution.py:258
  36.1 7.4 %all-to-all-start.1 = ((bf16[8,96,384]{2,1,0:T(8,128)(2,1)}), bf16[8,96,384]{2,1,0:T(8,128)(2,1)S(1)}, u32[]{:S(2)}, u32[]{:S(2)}) async-start(bf16[8,96,384]{2,1,0:T(8,128)(2,1)} %regroup.1), calls=%async_computation.1 | async-start | bytes 1179648 | tf_op jit(solution)/shard_map/all_to_all | solution.py:472
  43.5 0.0 copy-done.6
  43.5 0.3 copy.13.conv
  43.8 0.0 copy-done
  43.8 0.0 copy-done.1
  43.8 0.0 copy-done.2
  43.8 0.0 copy-done.3
  43.8 1.0 %prepare.1 = (bf16[256,2560]{1,0:T(8,128)(2,1)S(1)}, f32[128,512]{1,0:T(8,128)}) custom-call(bf16[32,32]{1,0:T(8,128)(2,1)S(1)} %copy-done.2, bf16[27,64,32]{2,1,0:T(8,128)(2,1)S(1)} %copy.13.conv, bf16[32,64]{1,0:T(8,128)(2,1)S(1)} %copy-done.3, bf16[4,32,512]{2,1,0:T(8,128)(2,1)S(1)} %get-tuple-element.8.own, bf16[512,512]{1,0:T(8,128)(2,1)S(1)} %copy-done, ...), custom_call_target="tpu_custom_call" | custom-call | tf_op jit(solution)/shard_map/prepare/pallas_call | solution.py:180
  44.9 0.1 pad_add_fusion
  44.9 8.6 %all-to-all-done.1.got = bf16[8,96,384]{2,1,0:T(8,128)(2,1)S(1)} async-done(((bf16[8,96,384]{2,1,0:T(8,128)(2,1)}), bf16[8,96,384]{2,1,0:T(8,128)(2,1)S(1)}, u32[]{:S(2)}, u32[]{:S(2)}) %all-to-all-start.1) | async-done | bytes 589856 | tf_op jit(solution)/shard_map/all_to_all | solution.py:472
  53.6 0.1 broadcast_in_dim.12.place
  53.6 0.0 copy-done.5
  53.6 4.3 %finish.1 = (f32[4,8,4,512]{3,2,1,0:T(4,128)}, bf16[32,8,256]{2,1,0:T(8,128)(2,1)}) custom-call(s32[2,8,512]{2,1,0:T(8,128)S(1)} %broadcast_in_dim.12.place, f32[128,512]{1,0:T(8,128)} %get-tuple-element.9.spectra, bf16[8,96,384]{2,1,0:T(8,128)(2,1)S(1)} %all-to-all-done.1.got, bf16[512,512]{1,0:T(8,128)(2,1)S(1)} %copy-done, ...), custom_call_target="tpu_custom_call" | custom-call | tf_op jit(solution)/shard_map/finish/pallas_call | solution.py:430
Async XLA Ops:
  0.6 21.5 %copy-start.4 = (bf16[1,4,512]{2,1,0:T(4,128)(2,1)S(1)}, bf16[1,4,512]{2,1,0:T(4,128)(2,1)}, u32[]{:S(2)}) copy-start(bf16[1,4,512]{2,1,0:T(4,128)(2,1)} %param.12) | copy-start | bytes 12292
  1.3 42.2 %copy-start.6 = (bf16[27,64,32]{1,2,0:T(8,128)(2,1)S(1)}, bf16[27,64,32]{1,2,0:T(8,128)(2,1)}, u32[]{:S(2)}) copy-start(bf16[27,64,32]{1,2,0:T(8,128)(2,1)} %param.17) | copy-start | bytes 331780
  4.8 39.0 %copy-start = (bf16[512,512]{1,0:T(8,128)(2,1)S(1)}, bf16[512,512]{1,0:T(8,128)(2,1)}, u32[]{:S(2)}) copy-start(bf16[512,512]{1,0:T(8,128)(2,1)} %constant.17.clone.high) | copy-start | bytes 1572868
  4.8 39.0 %copy-start.1 = (bf16[512,512]{1,0:T(8,128)(2,1)S(1)}, bf16[512,512]{1,0:T(8,128)(2,1)}, u32[]{:S(2)}) copy-start(bf16[512,512]{1,0:T(8,128)(2,1)} %constant.18.clone.low) | copy-start | bytes 1572868
  4.8 39.0 %copy-start.2 = (bf16[32,32]{1,0:T(8,128)(2,1)S(1)}, bf16[32,32]{1,0:T(8,128)(2,1)}, u32[]{:S(2)}) copy-start(bf16[32,32]{1,0:T(8,128)(2,1)} %unmix.1) | copy-start | bytes 6148
  4.8 39.0 %copy-start.3 = (bf16[32,64]{1,0:T(8,128)(2,1)S(1)}, bf16[32,64]{1,0:T(8,128)(2,1)}, u32[]{:S(2)}) copy-start(bf16[32,64]{1,0:T(8,128)(2,1)} %project.1) | copy-start | bytes 12292
  4.8 30.1 %all-to-all-start = ((bf16[64,16,128]{2,1,0:T(8,128)(2,1)}), bf16[64,16,128]{2,1,0:T(8,128)(2,1)S(1)}, u32[]{:S(2)}, u32[]{:S(2)}) async-start(bf16[64,16,128]{2,1,0:T(8,128)(2,1)} %get-tuple-element.10), calls=%async_computation | async-start | bytes 524288 | tf_op jit(solution)/shard_map/all_to_all | solution.py:471
  22.1 31.5 %copy-start.5 = (f32[64]{0:T(128)S(1)}, f32[64]{0:T(128)}, u32[]{:S(2)}) copy-start(f32[64]{0:T(128)} %param.18) | copy-start | bytes 772
  22.1 8.9 %collective-permute-start = (bf16[4,512]{1,0:T(4,128)(2,1)S(1)}, bf16[4,512]{1,0:T(4,128)(2,1)S(1)}, u32[]{:S(2)}, u32[]{:S(2)}) collective-permute-start(bf16[4,512]{1,0:T(4,128)(2,1)S(1)} %bitcast.9), channel_id=1, source_target_pairs={{0,256},{64,320},{128,384},{192,448},{256,0},{320,64},{384,128},{4... | collective-permute-start | bytes 12296 | tf_op jit(solution)/shard_map/ppermute | solution.py:468
  36.1 17.4 %all-to-all-start.1 = ((bf16[8,96,384]{2,1,0:T(8,128)(2,1)}), bf16[8,96,384]{2,1,0:T(8,128)(2,1)S(1)}, u32[]{:S(2)}, u32[]{:S(2)}) async-start(bf16[8,96,384]{2,1,0:T(8,128)(2,1)} %regroup.1), calls=%async_computation.1 | async-start | bytes 1179648 | tf_op jit(solution)/shard_map/all_to_all | solution.py:472

commit v6 on v5

--- a/solution.py
+++ b/solution.py
@@ -51,15 +51,11 @@
 
 def warp_kernel(shift, ids, tiles, table, out, own, raw, mats, chosen, sent, sems):
     inward = [
-        pltpu.make_async_copy(tiles, raw, sems.at[0, 0]),
-        pltpu.make_async_copy(ids, chosen, sems.at[1, 0]),
+        pltpu.make_async_copy(tiles, raw, sems.at[0]),
+        pltpu.make_async_copy(ids, chosen, sems.at[1]),
     ]
     inward += [
-        pltpu.make_async_copy(
-            table.at[k, pl.ds(at, 128)], mats.at[k, pl.ds(at, 128)], sems.at[2 + k, at // 128]
-        )
-        for k in range(CH)
-        for at in range(0, WIDTH, 128)
+        pltpu.make_async_copy(table.at[k], mats.at[k], sems.at[2 + k]) for k in range(CH)
     ]
     for copy in inward:
         copy.start()
@@ -113,7 +109,7 @@
         more = put(more, after, outer, 96 + slot // 2, PLANE, 2, 2)
         part = slice(half * PAIRS, (half + 1) * PAIRS)
         sent[part] = jnp.concatenate([main, more], axis=1).astype(BF)
-        copy = pltpu.make_async_copy(sent.at[part], out.at[part], sems.at[6 + half, 0])
+        copy = pltpu.make_async_copy(sent.at[part], out.at[part], sems.at[6 + half])
         copy.start()
         outward.append(copy)
     for copy in outward:
@@ -136,16 +132,14 @@
             pltpu.VMEM(table.shape, BF),
             pltpu.SMEM(ids.shape, jnp.int32),
             pltpu.VMEM(shape, BF),
-            pltpu.SemaphoreType.DMA((8, 4)),
+            pltpu.SemaphoreType.DMA((8,)),
         ],
         name="warp",
         interpret=interpret,
     )(shift, ids, raw, table)
 
 
-def prepare_kernel(unmix, conv, project, own, high, low, banded, spectra):
-    rows = own[...].reshape(CH * DEPTH * ROWS, WIDTH)
-    spectra[...] = dot(rows, high[...], ((1,), (0,))) + dot(rows, low[...], ((1,), (0,)))
+def prepare_kernel(unmix, conv, project, banded):
     n = MIXED * ROWS
     k = iota((n, MIXED), 0)
     source = (k // PLANE % HALVES * FAR + k // (HALVES * PLANE)) * CH + k // ROWS % CH
@@ -171,25 +165,24 @@
                 rows[y], axis=1
             )
     hole = jnp.zeros((MIXED, HIDDEN), BF)
+    halved = (0.5 * project[...].astype(F32)).astype(BF)
     for y in range(ROWS):
-        row = [project[...] if i == y else hole for i in range(ROWS)]
+        row = [halved if i == y else hole for i in range(ROWS)]
         banded[y * MIXED : (y + 1) * MIXED, SMALL:] = jnp.concatenate(row, axis=1)
 
 
-def prepare(unmix, conv, project, own, high, low, interpret=False):
+def prepare(unmix, conv, project, interpret=False):
     return pl.pallas_call(
         prepare_kernel,
-        out_shape=(
-            pltpu.VMEM((HIDDEN * ROWS, SMALL + 256), BF),
-            pltpu.HBM((CH * DEPTH * ROWS, WIDTH), F32),
-        ),
+        out_shape=pltpu.VMEM((HIDDEN * ROWS, SMALL + 256), BF),
         compiler_params=pltpu.CompilerParams(vmem_limit_bytes=16 << 20),
         name="prepare",
         interpret=interpret,
-    )(unmix, conv, project, own, high, low)
-
-
-def regroup_kernel(got, band, other, out, tall, sent, sems):
+    )(unmix, conv, project)
+
+
+def regroup_kernel(got, bands, out, passed, tall, sent, sems):
+    passed[...] = bands[...]
     tall[...] = got[...].astype(F32).reshape(TILES * 2 * BRICK, DEPTH * PLANE)
     turned = []
     for q in range(BRICK):
@@ -212,11 +205,6 @@
                 q, start, at = 2, 64 + 32 * side + (PLANE if slot else 0), 64
         return turned[q][start : start + PLANE], at
 
-    refs = jnp.concatenate([band[...].astype(F32), other[...].astype(F32)], axis=0)
-    marks = []
-    for p in range(0, 8, 2):
-        pair = refs[:, p * 64 : (p + 2) * 64]
-        marks.append(jnp.concatenate([pltpu.roll(pair, 64, 1), pair], axis=0))
     lane = iota((PLANE, 128), 1)
     outward = []
     for core in range(2):
@@ -233,17 +221,16 @@
                         rows = pltpu.roll(rows, turn, 1) if turn else rows
                         block = jnp.where((lane >= to) & (lane < to + PAIRS), rows, block)
                     blocks.append(block)
-                main = [block.astype(BF) for block in blocks[:2]]
+                main = [block.astype(BF) for block in blocks]
                 for far in range(FAR):
                     step = slot - far
                     if not 0 <= step < 3:
                         continue
                     w = step * HALVES + half
-                    last = jnp.where(lane >= 64, marks[w], blocks[2]) if w < 4 else blocks[2]
                     rows = slice(w * PLANE, (w + 1) * PLANE)
                     sent[2 * far + core, rows, :128] = main[0]
                     sent[2 * far + core, rows, 128:256] = main[1]
-                    sent[2 * far + core, rows, 256:] = last.astype(BF)
+                    sent[2 * far + core, rows, 256:] = main[2]
             if slot >= 2:
                 peer = 2 * (slot - 2) + core
                 copy = pltpu.make_async_copy(sent.at[peer], out.at[peer], sems.at[peer])
@@ -253,13 +240,13 @@
         copy.wait()
 
 
-def regroup(got, band, other, interpret=False):
+def regroup(got, bands, interpret=False):
     shape = (2 * FAR, LINES, PADDED)
     return pl.pallas_call(
         regroup_kernel,
-        out_shape=jax.ShapeDtypeStruct(shape, BF),
-        in_specs=[pl.BlockSpec(memory_space=pltpu.VMEM)] * 3,
-        out_specs=pl.BlockSpec(memory_space=pl.ANY),
+        out_shape=(jax.ShapeDtypeStruct(shape, BF), jax.ShapeDtypeStruct(bands.shape, BF)),
+        in_specs=[pl.BlockSpec(memory_space=pltpu.VMEM)] * 2,
+        out_specs=(pl.BlockSpec(memory_space=pl.ANY), pl.BlockSpec(memory_space=pltpu.VMEM)),
         scratch_shapes=[
             pltpu.VMEM((TILES * 2 * BRICK, DEPTH * PLANE), F32),
             pltpu.VMEM(shape, BF),
@@ -268,7 +255,7 @@
         name="regroup",
         compiler_params=pltpu.CompilerParams(vmem_limit_bytes=16 << 20),
         interpret=interpret,
-    )(got, band, other)
+    )(got, bands)
 
 
 def tables():
@@ -282,32 +269,14 @@
     return high, low
 
 
-def correlate(place, own, got, high, low, out):
+def correlate_kernel(slots, own, bands, high, low, out):
     half = WIDTH // 2
     count = CH * DEPTH * ROWS
-    left = iota((2 * ROWS, 128), 1) < 64
-    near, away = [], []
-    for far in range(FAR):
-        pieces = jnp.where(
-            place[1, :1, :128] == 0,
-            got[2 * far, :64, 256:].astype(F32),
-            got[2 * far + 1, :64, 256:].astype(F32),
-        )
-        lanes = []
-        for p in range(0, 8, 2):
-            a = pieces[p * 2 * ROWS : (p + 1) * 2 * ROWS]
-            b = pieces[(p + 1) * 2 * ROWS : (p + 2) * 2 * ROWS]
-            lanes.append(jnp.where(left, pltpu.roll(a, 64, 1), b))
-        rows = jnp.concatenate(lanes, axis=1)
-        near.append(rows[:ROWS])
-        away.append(rows[ROWS:])
-    near, away = jnp.concatenate(near, axis=0), jnp.concatenate(away, axis=0)
-    first_half = place[0, :1, :] == 0
-    band = jnp.concatenate(
-        [jnp.where(first_half, near, away), jnp.where(first_half, away, near)], axis=0
-    ).astype(BF)
+    band = jnp.concatenate([bands[slots[z]].astype(F32) for z in range(DEPTH)], axis=0).astype(BF)
+    rows = jnp.concatenate([own[...].reshape(count, WIDTH), band], axis=0)
     along = ((1,), (0,))
-    band = dot(band, high[...], along) + dot(band, low[...], along)
+    spectra = dot(rows, high[...], along) + dot(rows, low[...], along)
+    own, band = spectra[:count], spectra[count:]
     own_cos = own[:, :half].reshape(CH, DEPTH * ROWS, half)
     own_sin = own[:, half:].reshape(CH, DEPTH * ROWS, half)
     band_cos = band[:, :half]
@@ -330,16 +299,21 @@
             out[c, z] = inverse[start : start + ROWS]
 
 
-def finish_kernel(
-    place, spectra, got, high, low, banded, bias, away, out,
-    found, wide, first, second, own, shared, sems,
-):
-    fetch = [
-        pltpu.make_async_copy(spectra, own, sems.at[2]),
-        pltpu.make_async_copy(bias, shared, sems.at[1]),
-    ]
-    for copy in fetch:
-        copy.start()
+def correlate(slots, own, bands, high, low, interpret=False):
+    inside = pl.BlockSpec(memory_space=pltpu.VMEM)
+    return pl.pallas_call(
+        correlate_kernel,
+        out_shape=jax.ShapeDtypeStruct((CH, DEPTH, ROWS, WIDTH), F32),
+        in_specs=[pl.BlockSpec(memory_space=pltpu.SMEM)] + [inside] * 4,
+        compiler_params=pltpu.CompilerParams(vmem_limit_bytes=16 << 20),
+        name="correlate",
+        interpret=interpret,
+    )(slots, own, bands, high, low)
+
+
+def finish_kernel(got, banded, bias, out, wide, first, second, shared, sems):
+    fetch = pltpu.make_async_copy(bias, shared, sems.at[0])
+    fetch.start()
     n = MIXED * ROWS
     pair = iota((SPAN, PAIRS, n), 1).reshape(ALONG, n)
     right = iota((ALONG, n), 1) >= 64
@@ -366,18 +340,16 @@
         lower = jnp.where(pair == PAIRS - 1, 0.0, pltpu.roll(even, ALONG - 1, 0))
         wide[0, :, at + 128 : at + 256] = jnp.where(right, upper, odd).astype(BF)
         wide[1, :, at + 128 : at + 256] = jnp.where(right, even, lower).astype(BF)
-    for copy in fetch:
-        copy.wait()
-    correlate(place, own, got, high, low, found)
-    leave = pltpu.make_async_copy(found, away, sems.at[0])
-    leave.start()
+    fetch.wait()
     total = jnp.concatenate([shared[...]] * ROWS, axis=1)
     for b in range(3):
         rows = jnp.concatenate(
             [wide[core, b * PAIRS : b * PAIRS + count, :] for core in range(2)], axis=0
         )
         total = total + dot(rows, banded[:, b * 768 : (b + 1) * 768], ((1,), (1,)))
-    hidden = jax.nn.gelu(total).astype(BF)
+    slope = math.sqrt(2.0 / math.pi)
+    hidden = total + total * jnp.tanh(total * (slope + slope * 0.044715 * (total * total)))
+    hidden = hidden.astype(BF)
     mixed = dot(hidden, banded[:n, SMALL:], ((1,), (1,)))
     done = centre + mixed
     left = iota((MIXED, 128), 1) < 64
@@ -420,34 +392,25 @@
         second[pl.ds(x, MIXED, stride=BRICK), :] = rows[:, 128:]
     out[:, :, :128] = first[...].reshape(MIXED, BRICK, 128).astype(BF)
     out[:, :, 128:] = second[...].reshape(MIXED, BRICK, 128).astype(BF)
-    leave.wait()
-
-
-def finish(place, own, got, high, low, banded, bias, interpret=False):
+
+
+def finish(got, banded, bias, interpret=False):
     inside = pl.BlockSpec(memory_space=pltpu.VMEM)
-    outside = pl.BlockSpec(memory_space=pl.ANY)
-    found = (CH, DEPTH, ROWS, WIDTH)
     return pl.pallas_call(
         finish_kernel,
-        in_specs=[inside, pl.BlockSpec(memory_space=pltpu.HBM)] + [inside] * 4 + [outside],
-        out_specs=(outside, inside),
-        out_shape=(
-            jax.ShapeDtypeStruct(found, F32),
-            jax.ShapeDtypeStruct((MIXED, BRICK, TILES * ROWS), BF),
-        ),
+        in_specs=[inside, inside, pl.BlockSpec(memory_space=pltpu.HBM)],
+        out_shape=jax.ShapeDtypeStruct((MIXED, BRICK, TILES * ROWS), BF),
         scratch_shapes=[
-            pltpu.VMEM(found, F32),
             pltpu.VMEM((2, ALONG, 3 * 256), BF),
             pltpu.VMEM((MIXED * BRICK, 128), F32),
             pltpu.VMEM((MIXED * BRICK, 128), F32),
-            pltpu.VMEM(own.shape, F32),
             pltpu.VMEM(bias.shape, F32),
-            pltpu.SemaphoreType.DMA((3,)),
+            pltpu.SemaphoreType.DMA((1,)),
         ],
+        compiler_params=pltpu.CompilerParams(vmem_limit_bytes=16 << 20),
         name="finish",
-        compiler_params=pltpu.CompilerParams(vmem_limit_bytes=16 << 20),
         interpret=interpret,
-    )(place, own, got, high, low, banded, bias)
+    )(got, banded, bias)
 
 
 def close(value):
@@ -461,20 +424,25 @@
     swap = functools.partial(
         lax.all_to_all, axis_name=("round", "tile"), split_axis=0, concat_axis=0, tiled=True
     )
-    place = jnp.stack([lax.axis_index("round") >> 2, lax.axis_index("tile") & 1])
-    place = close(jnp.broadcast_to(place[:, None, None], (2, 8, WIDTH)))
-    band = close(ref_bands[0])
-    ahead = [(i, (i + FAR) % ROUNDS) for i in range(ROUNDS)]
-    other = close(lax.ppermute(band, "round", ahead))
     high, low = close(jnp.asarray(high)), close(jnp.asarray(low))
     sent, own = warp(shifts, matrix_ids, raw_tiles[0], resample)
     got = close(swap(sent, axis_index_groups=RINGS))
-    slabs = close(swap(regroup(got, band, other), axis_index_groups=NEAR))
-    prepared = prepare(unmix, conv_weight, out_weight, close(own), high, low)
-    banded = close(prepared[0])
-    spectra = pltpu.with_memory_space_constraint(prepared[1], pltpu.HBM)
-    bias = conv_bias.reshape(1, -1)
-    correlation, features = finish(place, spectra, slabs, high, low, banded, bias)
+    bands = ref_bands
+
+    def doubled(bands, step):
+        pairs = [(i, i ^ step) for i in range(ROUNDS)]
+        return jnp.concatenate([bands, lax.ppermute(bands, "round", pairs)], axis=0)
+
+    for step in (1, 2):
+        bands = doubled(bands, step)
+    slots = jnp.arange(ROUNDS, dtype=jnp.int32) ^ lax.axis_index("round")
+    banded = close(prepare(unmix, conv_weight, out_weight))
+    chunks, bands = regroup(got, bands)
+    slabs = close(swap(chunks, axis_index_groups=NEAR))
+    bands = doubled(bands, 4)
+    correlation = correlate(slots, own, bands, high, low)
+    bias = pltpu.with_memory_space_constraint(conv_bias.reshape(1, -1), pltpu.HBM)
+    features = finish(slabs, banded, bias)
     return (correlation[None], features[:, None])
 
 

time: 58.3 us -> 58.7 us (level)
  waiting for transfers between devices: 14.5 us -> 7.09 us
  starting transfers between devices: 31.6 us -> 37.4 us
  other arithmetic: 0.07 us -> 1.28 us
    all_to_all x1, waiting for transfers between devices: 8.62 us -> 0.01 us  [body(): slabs = close(swap(chunks, axis_index_groups=NEAR))]
    ppermute x1 -> x3, starting transfers between devices: 6.93 us -> 12.9 us  [doubled(): return jnp.concatenate([bands, lax.ppermute(bands, 'round', pairs)], axis=0)]
    ppermute x1 -> x3, waiting for transfers between devices: 1.94 us -> 5.29 us  [doubled(): return jnp.concatenate([bands, lax.ppermute(bands, 'round', pairs)], axis=0)]
    all_to_all x1, waiting for transfers between devices: 3.94 us -> 1.79 us  [body(): got = close(swap(sent, axis_index_groups=RINGS))]
    concatenate x0 -> x3, other arithmetic: none -> 0.77 us  [doubled(): return jnp.concatenate([bands, lax.ppermute(bands, 'round', pairs)], axis=0)]
    unnamed x15, local copies, waits for them, and re-layouts: 0.3 us -> 0.94 us
    pallas_call x3 -> x4, Pallas kernels: 6.54 us -> 6.63 us  [the longest x1 3.02 us: finish(): pl.pallas_call(finish_kernel, in_specs=[inside, inside, pl.BlockSpec(memo...]
  transfers between devices with their start and end apart: 3 -> 5, of which waited for: 3 -> 4; matrix products, arithmetic and copies ran while one was open for 1% -> 3% of each run, Pallas kernels for 2% -> 4%
where the time goes in v6:
time: 58.7 us; the launch traced here: 58 us
  starting transfers between devices  37.4 us (64%)
  Pallas kernels  9.82 us (17%)
  waiting for transfers between devices  7.09 us (12%)
  between operations  1.46 us (2%)
  other arithmetic  1.28 us (2%)
  local copies, waits for them, and re-layouts  0.94 us (2%)
    all_to_all x1, starting transfers between devices, body(): got = close(swap(sent, axis_index_groups=RINGS))  17.1 us
    ppermute x3, starting transfers between devices, doubled(): return jnp.concatenate([bands, lax.ppermute(bands, 'round', pairs)], axis=0)  12.9 us
    all_to_all x1, starting transfers between devices, body(): slabs = close(swap(chunks, axis_index_groups=NEAR))  7.37 us
    ppermute x3, waiting for transfers between devices, doubled(): return jnp.concatenate([bands, lax.ppermute(bands, 'round', pairs)], axis=0)  5.29 us
    pallas_call x1, Pallas kernels, warp(): pl.pallas_call(warp_kernel, out_shape=(jax.ShapeDtypeStruct(shape, BF), p...  3.18 us
    pallas_call x1, Pallas kernels, finish(): pl.pallas_call(finish_kernel, in_specs=[inside, inside, pl.BlockSpec(memo...  3.02 us
    pallas_call x1, Pallas kernels, correlate(): pl.pallas_call(correlate_kernel, out_shape=jax.ShapeDtypeStruct((CH, DEPT...  2 us
    all_to_all x1, waiting for transfers between devices, body(): got = close(swap(sent, axis_index_groups=RINGS))  1.79 us
  transfers between devices with their start and end apart: 5, of which 4 were waited for; matrix products, arithmetic and copies ran while one was open for 3% of the time, Pallas kernels for 4%

profile of v6, /device:TPU:1, one launch (start us, length us, event | category | flops | bytes accessed | tf_op | source)
XLA Modules:
  0.0 58.0 jit_solution(12908292104043789671)
XLA Ops:
  0.6 0.0 copy-start.6
  1.3 0.0 copy-start.5
  1.3 0.0 copy-start.2
  1.3 0.0 copy-start.3
  1.3 3.2 %warp.1 = (bf16[64,16,128]{2,1,0:T(8,128)(2,1)}, bf16[4,32,512]{2,1,0:T(8,128)(2,1)S(1)}) custom-call(s32[1,1]{1,0:T(1,128)S(6)} %copy.15.shift, s32[1,4]{1,0:T(1,128)} %ids.1, bf16[4,8,4,512]{3,2,1,0:T(4,128)(2,1)} %bitcast.7, bf16[4,512,512]{2,1,0:T(8,128)(2,1)} %table.1), custom_call_target="tpu_custom_call" | custom-call | tf_op jit(solution)/shard_map/warp/pallas_call | solution.py:122
  4.5 17.1 %all-to-all-start = ((bf16[64,16,128]{2,1,0:T(8,128)(2,1)}), bf16[64,16,128]{2,1,0:T(8,128)(2,1)S(1)}, u32[]{:S(2)}, u32[]{:S(2)}) async-start(bf16[64,16,128]{2,1,0:T(8,128)(2,1)} %get-tuple-element.7), calls=%async_computation | async-start | bytes 524288 | tf_op jit(solution)/shard_map/all_to_all | solution.py:429
  21.7 0.0 copy-done.6
  21.7 0.0 copy-start
  21.7 0.0 copy-start.1
  21.7 3.3 %collective-permute-start = (bf16[1,4,512]{2,1,0:T(4,128)(2,1)S(1)}, bf16[1,4,512]{2,1,0:T(4,128)(2,1)S(1)}, u32[]{:S(2)}, u32[]{:S(2)}) collective-permute-start(bf16[1,4,512]{2,1,0:T(4,128)(2,1)S(1)} %copy-done.6), channel_id=1, source_target_pairs={{0,64},{64,0},{128,192},{192,128},{256,320},{320,256},{384,448},{4... | collective-permute-start | bytes 12296 | tf_op jit(solution)/shard_map/ppermute | solution.py:434
  25.0 1.5 %collective-permute-done = bf16[1,4,512]{2,1,0:T(4,128)(2,1)S(1)} collective-permute-done((bf16[1,4,512]{2,1,0:T(4,128)(2,1)S(1)}, bf16[1,4,512]{2,1,0:T(4,128)(2,1)S(1)}, u32[]{:S(2)}, u32[]{:S(2)}) %collective-permute-start) | collective-permute-done | bytes 4128 | tf_op jit(solution)/shard_map/ppermute | solution.py:434
  26.5 4.7 %collective-permute-start.1 = (bf16[2,4,512]{2,1,0:T(4,128)(2,1)S(1)}, bf16[2,4,512]{2,1,0:T(4,128)(2,1)S(1)}, u32[]{:S(2)}, u32[]{:S(2)}) collective-permute-start(bf16[2,4,512]{2,1,0:T(4,128)(2,1)S(1)} %pad_maximum_fusion.2), channel_id=1, source_target_pairs={{0,128},{64,192},{128,0},{192,64},{256,384},{320,448},{384,256},{4... | collective-permute-start | bytes 24584 | tf_op jit(solution)/shard_map/ppermute | solution.py:434
  31.2 1.5 %collective-permute-done.1 = bf16[2,4,512]{2,1,0:T(4,128)(2,1)S(1)} collective-permute-done((bf16[2,4,512]{2,1,0:T(4,128)(2,1)S(1)}, bf16[2,4,512]{2,1,0:T(4,128)(2,1)S(1)}, u32[]{:S(2)}, u32[]{:S(2)}) %collective-permute-start.1) | collective-permute-done | bytes 8224 | tf_op jit(solution)/shard_map/ppermute | solution.py:434
  32.7 1.8 %all-to-all-done.got = bf16[64,16,128]{2,1,0:T(8,128)(2,1)S(1)} async-done(((bf16[64,16,128]{2,1,0:T(8,128)(2,1)}), bf16[64,16,128]{2,1,0:T(8,128)(2,1)S(1)}, u32[]{:S(2)}, u32[]{:S(2)}) %all-to-all-start) | async-done | bytes 262176 | tf_op jit(solution)/shard_map/all_to_all | solution.py:429
  34.5 1.2 %regroup.1 = (bf16[8,96,384]{2,1,0:T(8,128)(2,1)}, bf16[4,4,512]{2,1,0:T(4,128)(2,1)S(1)}) custom-call(bf16[64,16,128]{2,1,0:T(8,128)(2,1)S(1)} %all-to-all-done.got, bf16[4,4,512]{2,1,0:T(4,128)(2,1)S(1)} %pad_maximum_fusion.1.bands), custom_call_target="tpu_custom_call" | custom-call | tf_op jit(solution)/shard_map/regroup/pallas_call | solution.py:245
  35.7 7.4 %all-to-all-start.1 = ((bf16[8,96,384]{2,1,0:T(8,128)(2,1)}), bf16[8,96,384]{2,1,0:T(8,128)(2,1)S(1)}, u32[]{:S(2)}, u32[]{:S(2)}) async-start(bf16[8,96,384]{2,1,0:T(8,128)(2,1)} %get-tuple-element.9), calls=%async_computation.1 | async-start | bytes 1179648 | tf_op jit(solution)/shard_map/all_to_all | solution.py:441
  43.1 5.0 %collective-permute-start.2 = (bf16[4,4,512]{2,1,0:T(4,128)(2,1)S(1)}, bf16[4,4,512]{2,1,0:T(4,128)(2,1)}, u32[]{:S(2)}, u32[]{:S(2)}) collective-permute-start(bf16[4,4,512]{2,1,0:T(4,128)(2,1)S(1)} %get-tuple-element.8), channel_id=1, source_target_pairs={{0,256},{64,320},{128,384},{192,448},{256,0},{320,64},{384,128},{4... | collective-permute-start | bytes 49160 | tf_op jit(solution)/shard_map/ppermute | solution.py:434
  48.1 0.5 iota_xor_fusion.slots
  48.6 0.0 copy-done.5
  48.6 0.3 copy.13.conv
  48.9 0.0 copy-done.2
  48.9 0.0 copy-done.3
  48.9 0.4 prepare.1.banded
  49.3 2.2 %collective-permute-done.2 = bf16[4,4,512]{2,1,0:T(4,128)(2,1)} collective-permute-done((bf16[4,4,512]{2,1,0:T(4,128)(2,1)S(1)}, bf16[4,4,512]{2,1,0:T(4,128)(2,1)}, u32[]{:S(2)}, u32[]{:S(2)}) %collective-permute-start.2) | collective-permute-done | bytes 16416 | tf_op jit(solution)/shard_map/ppermute | solution.py:434
  51.6 0.7 %pad_maximum_fusion.bands = bf16[8,4,512]{2,1,0:T(4,128)(2,1)S(1)} fusion(bf16[4,4,512]{2,1,0:T(4,128)(2,1)} %collective-permute-done.2, bf16[4,4,512]{2,1,0:T(4,128)(2,1)S(1)} %get-tuple-element.8), kind=kLoop, calls=%fused_computation | loop fusion | flops 16384 | bytes 65536 | tf_op jit(solution)/shard_map/concatenate | solution.py:434
  52.3 0.0 copy-done
  52.3 0.0 copy-done.1
  52.3 0.0 copy-start.4
  52.3 0.6 %copy-done.4 = s32[8]{0:T(128)S(1)} copy-done((s32[8]{0:T(128)S(1)}, s32[8]{0:T(128)}, u32[]{:S(2)}) %copy-start.4) | copy-done | bytes 56
  53.0 2.0 %correlate.1 = f32[4,8,4,512]{3,2,1,0:T(4,128)} custom-call(s32[8]{0:T(128)S(1)} %copy-done.4, bf16[4,32,512]{2,1,0:T(8,128)(2,1)S(1)} %get-tuple-element.6.own, bf16[8,4,512]{2,1,0:T(4,128)(2,1)S(1)} %pad_maximum_fusion.bands, bf16[512,512]{1,0:T(8,128)(2,1)S(1)} %copy-done.1, bf16[512,512]{1,0:T(8,128)(2,1)S(1)} %copy-done), custom_call_target="tpu_custom_call" | custom-call | tf_op jit(solution)/shard_map/correlate/pallas_call | solution.py:304
  55.0 0.0 all-to-all-done.1.got
  55.0 3.0 %finish.1 = bf16[32,8,256]{2,1,0:T(8,128)(2,1)} custom-call(bf16[8,96,384]{2,1,0:T(8,128)(2,1)S(1)} %all-to-all-done.1.got, bf16[256,2560]{1,0:T(8,128)(2,1)S(1)} %prepare.1.banded, f32[1,64]{1,0:T(1,128)} %bitcast.9), custom_call_target="tpu_custom_call" | custom-call | tf_op jit(solution)/shard_map/finish/pallas_call | solution.py:399
  (2 shorter events, 0.0 us)
Async XLA Ops:
  0.6 21.0 %copy-start.6 = (bf16[1,4,512]{2,1,0:T(4,128)(2,1)S(1)}, bf16[1,4,512]{2,1,0:T(4,128)(2,1)}, u32[]{:S(2)}) copy-start(bf16[1,4,512]{2,1,0:T(4,128)(2,1)} %param.12) | copy-start | bytes 12292
  1.3 47.3 %copy-start.5 = (bf16[27,64,32]{1,2,0:T(8,128)(2,1)S(1)}, bf16[27,64,32]{1,2,0:T(8,128)(2,1)}, u32[]{:S(2)}) copy-start(bf16[27,64,32]{1,2,0:T(8,128)(2,1)} %param.17) | copy-start | bytes 331780
  1.3 47.6 %copy-start.2 = (bf16[32,32]{1,0:T(8,128)(2,1)S(1)}, bf16[32,32]{1,0:T(8,128)(2,1)}, u32[]{:S(2)}) copy-start(bf16[32,32]{1,0:T(8,128)(2,1)} %unmix.1) | copy-start | bytes 6148
  1.3 47.6 %copy-start.3 = (bf16[32,64]{1,0:T(8,128)(2,1)S(1)}, bf16[32,64]{1,0:T(8,128)(2,1)}, u32[]{:S(2)}) copy-start(bf16[32,64]{1,0:T(8,128)(2,1)} %project.1) | copy-start | bytes 12292
  4.5 30.0 %all-to-all-start = ((bf16[64,16,128]{2,1,0:T(8,128)(2,1)}), bf16[64,16,128]{2,1,0:T(8,128)(2,1)S(1)}, u32[]{:S(2)}, u32[]{:S(2)}) async-start(bf16[64,16,128]{2,1,0:T(8,128)(2,1)} %get-tuple-element.7), calls=%async_computation | async-start | bytes 524288 | tf_op jit(solution)/shard_map/all_to_all | solution.py:429
  21.7 30.6 %copy-start = (bf16[512,512]{1,0:T(8,128)(2,1)S(1)}, bf16[512,512]{1,0:T(8,128)(2,1)}, u32[]{:S(2)}) copy-start(bf16[512,512]{1,0:T(8,128)(2,1)} %constant.11.clone.low) | copy-start | bytes 1572868
  21.7 30.6 %copy-start.1 = (bf16[512,512]{1,0:T(8,128)(2,1)S(1)}, bf16[512,512]{1,0:T(8,128)(2,1)}, u32[]{:S(2)}) copy-start(bf16[512,512]{1,0:T(8,128)(2,1)} %constant.10.clone.high) | copy-start | bytes 1572868
  21.7 4.8 %collective-permute-start = (bf16[1,4,512]{2,1,0:T(4,128)(2,1)S(1)}, bf16[1,4,512]{2,1,0:T(4,128)(2,1)S(1)}, u32[]{:S(2)}, u32[]{:S(2)}) collective-permute-start(bf16[1,4,512]{2,1,0:T(4,128)(2,1)S(1)} %copy-done.6), channel_id=1, source_target_pairs={{0,64},{64,0},{128,192},{192,128},{256,320},{320,256},{384,448},{4... | collective-permute-start | bytes 12296 | tf_op jit(solution)/shard_map/ppermute | solution.py:434
  26.5 6.2 %collective-permute-start.1 = (bf16[2,4,512]{2,1,0:T(4,128)(2,1)S(1)}, bf16[2,4,512]{2,1,0:T(4,128)(2,1)S(1)}, u32[]{:S(2)}, u32[]{:S(2)}) collective-permute-start(bf16[2,4,512]{2,1,0:T(4,128)(2,1)S(1)} %pad_maximum_fusion.2), channel_id=1, source_target_pairs={{0,128},{64,192},{128,0},{192,64},{256,384},{320,448},{384,256},{4... | collective-permute-start | bytes 24584 | tf_op jit(solution)/shard_map/ppermute | solution.py:434
  35.7 19.3 %all-to-all-start.1 = ((bf16[8,96,384]{2,1,0:T(8,128)(2,1)}), bf16[8,96,384]{2,1,0:T(8,128)(2,1)S(1)}, u32[]{:S(2)}, u32[]{:S(2)}) async-start(bf16[8,96,384]{2,1,0:T(8,128)(2,1)} %get-tuple-element.9), calls=%async_computation.1 | async-start | bytes 1179648 | tf_op jit(solution)/shard_map/all_to_all | solution.py:441
  43.1 8.5 %collective-permute-start.2 = (bf16[4,4,512]{2,1,0:T(4,128)(2,1)S(1)}, bf16[4,4,512]{2,1,0:T(4,128)(2,1)}, u32[]{:S(2)}, u32[]{:S(2)}) collective-permute-start(bf16[4,4,512]{2,1,0:T(4,128)(2,1)S(1)} %get-tuple-element.8), channel_id=1, source_target_pairs={{0,256},{64,320},{128,384},{192,448},{256,0},{320,64},{384,128},{4... | collective-permute-start | bytes 49160 | tf_op jit(solution)/shard_map/ppermute | solution.py:434
  52.3 0.7 %copy-start.4 = (s32[8]{0:T(128)S(1)}, s32[8]{0:T(128)}, u32[]{:S(2)}) copy-start(s32[8]{0:T(128)} %iota_xor_fusion.slots) | copy-start | bytes 100

commit v7 on v4

--- a/solution.py
+++ b/solution.py
@@ -94,20 +94,25 @@
         return jnp.where(here if only is None else here & (row == only), value, base)
 
     outward = []
+    def gather(value, outer):
+        turned = pltpu.roll(value, 128 - outer, 2)
+        turned = pltpu.roll(turned, 0, 2, stride=PLANE, stride_axis=1)
+        return jnp.sum(jnp.where(lane // PLANE == row, turned, 0.0), axis=1, keepdims=True)
+
     for half in range(HALVES):
         start = 64 * half
         main = put(left, right, start, 64, 64) if half == 0 else put(right, left, start, 0, 64)
-        more = jnp.zeros(left.shape, F32)
-        more = put(more, before, start, 64, 64, 0, 1)
-        more = put(more, after, start, 64, 64, 1, 1)
         outer = 64 if half == 0 else 48
-        slot = 32 if half == 0 else 0
-        more = put(more, left, outer, slot, PLANE)
-        more = put(more, right, outer, slot + PLANE, PLANE)
-        more = put(more, before, outer, 64 + slot // 2, PLANE, 2, 3)
-        more = put(more, after, outer, 96 + slot // 2, PLANE, 2, 2)
+        more = jnp.where(row == 0, gather(left, outer), gather(right, outer))
+        more = jnp.where(row < 2, more, 0.0)
+        more = put(more, before, start, 0, 64, 2, 3)
+        more = put(more, after, start, 64, 64, 2, 2)
+        more = put(more, before, outer, 0, PLANE, 3, 4)
+        more = put(more, after, outer, PLANE, PLANE, 3, 3)
         part = slice(half * PAIRS, (half + 1) * PAIRS)
-        sent[part] = jnp.concatenate([main, more], axis=1).astype(BF)
+        sent[part, :, :128] = main[:, :4].astype(BF)
+        sent[part, :, 128:256] = main[:, 4:].astype(BF)
+        sent[part, :, 256:] = more[:, :4].astype(BF)
         copy = pltpu.make_async_copy(sent.at[part], out.at[part], sems.at[6 + half])
         copy.start()
         outward.append(copy)
@@ -117,7 +122,7 @@
 
 def warp(shift, ids, raw, table, interpret=False):
     away = pl.BlockSpec(memory_space=pl.ANY)
-    shape = (TILES, 2 * BRICK, DEPTH * PLANE)
+    shape = (TILES, 4, 3 * 128)
     return pl.pallas_call(
         warp_kernel,
         out_shape=(
@@ -164,8 +169,9 @@
             )
     biases[...] = jnp.concatenate([bias[...]] * ROWS, axis=1)
     hole = jnp.zeros((MIXED, HIDDEN), BF)
+    halved = (0.5 * project[...].astype(F32)).astype(BF)
     for y in range(ROWS):
-        row = [project[...] if i == y else hole for i in range(ROWS)]
+        row = [halved if i == y else hole for i in range(ROWS)]
         projected[y * MIXED : (y + 1) * MIXED, :] = jnp.concatenate(row, axis=1)
 
 
@@ -183,28 +189,37 @@
     )(unmix, conv, bias, project)
 
 
-def regroup_kernel(got, band, other, out, tall, sent, sems):
-    tall[...] = got[...].astype(F32).reshape(TILES * 2 * BRICK, DEPTH * PLANE)
-    turned = []
-    for q in range(BRICK):
-        both = [tall[pl.ds(q + at, TILES, stride=2 * BRICK), :] for at in (0, BRICK)]
-        turned.append(jnp.concatenate(both, axis=0).T)
+def regroup_kernel(place, got, band, other, out, tall, sent, sems):
+    thirds = [got[:, :, at : at + 128].astype(F32) for at in (0, 128, 256)]
+    tall[...] = jnp.concatenate(thirds + thirds[2:], axis=1).reshape(TILES * 16, 128)
+
+    def turn(a, b):
+        rows = [tall[pl.ds(q, TILES, stride=16), :] for q in (a, b)]
+        return jnp.concatenate(rows, axis=0).T
+
+    turned = [turn(q, q + 1) for q in range(0, 12, 2)]
+    first_half = place[0, :1, :128] == 0
 
     def piece(slot, column):
         x = column - 1
+        inner = 1 <= slot <= 4
         if 0 <= x < 2 * BRICK:
             block, q = x // BRICK, x % BRICK
-            if 1 <= slot <= 4:
-                start, at = block * 64 + (slot - 1) * PLANE, 0
+            if inner:
+                which, start, at = q // 2, block * 64 + (slot - 1) * PLANE, q % 2 * 64
             else:
-                start, at = (32 if slot else 0) + block * PLANE, 64
+                which, start, at = 4, q * PLANE, block * 64
         else:
             side = 0 if x < 0 else 1
-            if 1 <= slot <= 4:
-                q, start, at = side, 64 + (slot - 1) * PLANE, 64
+            if inner:
+                which, start, at = 5, side * 64 + (slot - 1) * PLANE, 0
             else:
-                q, start, at = 2, 64 + 32 * side + (PLANE if slot else 0), 64
-        return turned[q][start : start + PLANE], at
+                which, start, at = 5, side * PLANE, 64
+        rows = turned[which][start : start + PLANE]
+        if not inner:
+            keep = first_half if slot else jnp.logical_not(first_half)
+            rows = jnp.where(keep, rows, 0.0)
+        return rows, at
 
     refs = jnp.concatenate([band[...].astype(F32), other[...].astype(F32)], axis=0)
     marks = []
@@ -247,21 +262,21 @@
         copy.wait()
 
 
-def regroup(got, band, other, interpret=False):
+def regroup(place, got, band, other, interpret=False):
     shape = (2 * FAR, LINES, PADDED)
     return pl.pallas_call(
         regroup_kernel,
         out_shape=jax.ShapeDtypeStruct(shape, BF),
-        in_specs=[pl.BlockSpec(memory_space=pltpu.VMEM)] * 3,
+        in_specs=[pl.BlockSpec(memory_space=pltpu.VMEM)] * 4,
         out_specs=pl.BlockSpec(memory_space=pl.ANY),
         scratch_shapes=[
-            pltpu.VMEM((TILES * 2 * BRICK, DEPTH * PLANE), F32),
+            pltpu.VMEM((TILES * 16, 128), F32),
             pltpu.VMEM(shape, BF),
             pltpu.SemaphoreType.DMA((2 * FAR,)),
         ],
         name="regroup",
         interpret=interpret,
-    )(got, band, other)
+    )(place, got, band, other)
 
 
 def tables():
@@ -379,7 +394,9 @@
             [wide[core, b * PAIRS : b * PAIRS + count, :] for core in range(2)], axis=0
         )
         total = total + dot(rows, weights[:, b * 768 : (b + 1) * 768], ((1,), (1,)))
-    hidden = jax.nn.gelu(total).astype(BF)
+    slope = math.sqrt(2.0 / math.pi)
+    hidden = total + total * jnp.tanh(total * (slope + slope * 0.044715 * (total * total)))
+    hidden = hidden.astype(BF)
     mixed = dot(hidden, projected[...], ((1,), (1,)))
     done = centre + mixed
     left = iota((MIXED, 128), 1) < 64
@@ -473,7 +490,7 @@
     high, low = close(jnp.asarray(high)), close(jnp.asarray(low))
     sent, own = warp(shifts, matrix_ids, raw_tiles[0], resample)
     got = close(swap(sent, axis_index_groups=RINGS))
-    slabs = close(swap(regroup(got, band, other), axis_index_groups=NEAR))
+    slabs = close(swap(regroup(place, got, band, other), axis_index_groups=NEAR))
     spectra = close(own_spectra(close(own), high, low))
     correlation, features = finish(
         place, spectra, slabs, high, low, spread, banded, biases, projected

time: 58.1 us -> 57.2 us (0.985)
  waiting for transfers between devices: 12.1 us -> 11.3 us
    all_to_all x1, waiting for transfers between devices: 3.94 us -> 3.26 us  [body(): got = close(swap(sent, axis_index_groups=RINGS))]
where the time goes in v7:
time: 57.2 us; the launch traced here: 56.8 us
  starting transfers between devices  31.2 us (55%)
  Pallas kernels  11.7 us (20%)
  waiting for transfers between devices  11.3 us (20%)
  between operations  1.38 us (2%)
  local copies, waits for them, and re-layouts  1.09 us (2%)
    all_to_all x1, starting transfers between devices, body(): got = close(swap(sent, axis_index_groups=RINGS))  17.3 us
    all_to_all x1, starting transfers between devices, body(): swap(regroup(place, got, band, other), axis_index_groups=NEAR)  7.01 us
    ppermute x1, starting transfers between devices, body(): other = close(lax.ppermute(band, 'round', ahead))  6.93 us
    all_to_all x1, waiting for transfers between devices, body(): swap(regroup(place, got, band, other), axis_index_groups=NEAR)  6.29 us
    pallas_call x1, Pallas kernels, finish(): pl.pallas_call(finish_kernel, in_specs=[inside] * 6 + [outside] + [inside...  4.3 us
    pallas_call x1, Pallas kernels, warp(): pl.pallas_call(warp_kernel, out_shape=(jax.ShapeDtypeStruct(shape, BF), p...  3.42 us
    all_to_all x1, waiting for transfers between devices, body(): got = close(swap(sent, axis_index_groups=RINGS))  3.26 us
    pallas_call x1, Pallas kernels, prepare(): pl.pallas_call(prepare_kernel, out_shape=(pltpu.VMEM((MIXED * ROWS, MIXED...  2.45 us
  transfers between devices with their start and end apart: 3, of which 3 were waited for; matrix products, arithmetic and copies ran while one was open for 2% of the time, Pallas kernels for 5%

profile of v7, /device:TPU:1, one launch (start us, length us, event | category | flops | bytes accessed | tf_op | source)
XLA Modules:
  0.0 56.8 jit_solution(11326655881195740425)
XLA Ops:
  0.6 0.0 copy-start.2
  1.3 0.0 copy-start.3
  1.3 3.4 %warp.1 = (bf16[64,4,384]{2,1,0:T(4,128)(2,1)}, bf16[4,32,512]{2,1,0:T(8,128)(2,1)S(1)}) custom-call(s32[1,1]{1,0:T(1,128)S(6)} %copy.15.shift, s32[1,4]{1,0:T(1,128)} %ids.1, bf16[4,8,4,512]{3,2,1,0:T(4,128)(2,1)} %bitcast.11, bf16[4,512,512]{2,1,0:T(8,128)(2,1)} %table.1), custom_call_target="tpu_custom_call" | custom-call | tf_op jit(solution)/shard_map/warp/pallas_call | solution.py:126
  4.7 0.0 copy-start
  4.7 0.0 copy-start.1
  4.8 17.3 %all-to-all-start = ((bf16[64,4,384]{2,1,0:T(4,128)(2,1)}), bf16[64,4,384]{2,1,0:T(4,128)(2,1)S(1)}, u32[]{:S(2)}, u32[]{:S(2)}) async-start(bf16[64,4,384]{2,1,0:T(4,128)(2,1)} %get-tuple-element.11), calls=%async_computation | async-start | bytes 393216 | tf_op jit(solution)/shard_map/all_to_all | solution.py:492
  22.0 0.0 copy-done.2
  22.0 6.9 %collective-permute-start = (bf16[4,512]{1,0:T(4,128)(2,1)S(1)}, bf16[4,512]{1,0:T(4,128)(2,1)S(1)}, u32[]{:S(2)}, u32[]{:S(2)}) collective-permute-start(bf16[4,512]{1,0:T(4,128)(2,1)S(1)} %bitcast.9), channel_id=1, source_target_pairs={{0,256},{64,320},{128,384},{192,448},{256,0},{320,64},{384,128},{4... | collective-permute-start | bytes 12296 | tf_op jit(solution)/shard_map/ppermute | solution.py:485
  29.0 0.1 pad_add_fusion
  29.1 1.7 %collective-permute-done.other = bf16[4,512]{1,0:T(4,128)(2,1)S(1)} collective-permute-done((bf16[4,512]{1,0:T(4,128)(2,1)S(1)}, bf16[4,512]{1,0:T(4,128)(2,1)S(1)}, u32[]{:S(2)}, u32[]{:S(2)}) %collective-permute-start) | collective-permute-done | bytes 4128 | tf_op jit(solution)/shard_map/ppermute | solution.py:485
  30.8 3.3 %all-to-all-done.got = bf16[64,4,384]{2,1,0:T(4,128)(2,1)S(1)} async-done(((bf16[64,4,384]{2,1,0:T(4,128)(2,1)}), bf16[64,4,384]{2,1,0:T(4,128)(2,1)S(1)}, u32[]{:S(2)}, u32[]{:S(2)}) %all-to-all-start) | async-done | bytes 196640 | tf_op jit(solution)/shard_map/all_to_all | solution.py:492
  34.1 0.1 broadcast_in_dim.12.place
  34.1 1.3 %regroup.1 = bf16[8,96,384]{2,1,0:T(8,128)(2,1)} custom-call(s32[2,8,512]{2,1,0:T(8,128)S(1)} %broadcast_in_dim.12.place, bf16[64,4,384]{2,1,0:T(4,128)(2,1)S(1)} %all-to-all-done.got, bf16[4,512]{1,0:T(4,128)(2,1)S(1)} %bitcast.10, bf16[4,512]{1,0:T(4,128)(2,1)S(1)} %collective-permute-done.other), custom_call_target="tpu_custom_call" | custom-call | tf_op jit(solution)/shard_map/regroup/pallas_call | solution.py:267
  35.4 7.0 %all-to-all-start.1 = ((bf16[8,96,384]{2,1,0:T(8,128)(2,1)}), bf16[8,96,384]{2,1,0:T(8,128)(2,1)S(1)}, u32[]{:S(2)}, u32[]{:S(2)}) async-start(bf16[8,96,384]{2,1,0:T(8,128)(2,1)} %regroup.1), calls=%async_computation.1 | async-start | bytes 1179648 | tf_op jit(solution)/shard_map/all_to_all | solution.py:493
  42.4 0.0 copy-done.3
  42.4 1.0 %copy.13.conv = bf16[27,64,32]{2,1,0:T(8,128)(2,1)} copy(bf16[27,64,32]{1,2,0:T(8,128)(2,1)S(1)} %copy-done.3) | data formatting | bytes 221184 | tf_op args[6]
  43.4 0.0 copy-done
  43.4 0.0 copy-done.1
  43.4 0.3 spectra.1.own
  43.7 2.5 %prepare.1 = (bf16[128,128]{1,0:T(8,128)(2,1)S(1)}, bf16[256,2304]{1,0:T(8,128)(2,1)}, f32[1,256]{1,0:T(1,128)S(1)}, bf16[128,256]{1,0:T(8,128)(2,1)S(1)}) custom-call(bf16[32,32]{1,0:T(8,128)(2,1)} %unmix.1, bf16[27,64,32]{2,1,0:T(8,128)(2,1)} %copy.13.conv, f32[1,64]{1,0:T(1,128)} %bitcast.12, bf16[32,64]{1,0:T(8,128)(2,1)} %project.1), custom_call_target="tpu_custom_call" | custom-call | tf_op jit(solution)/shard_map/prepare/pallas_call | solution.py:179
  46.2 6.3 %all-to-all-done.1.got = bf16[8,96,384]{2,1,0:T(8,128)(2,1)S(1)} async-done(((bf16[8,96,384]{2,1,0:T(8,128)(2,1)}), bf16[8,96,384]{2,1,0:T(8,128)(2,1)S(1)}, u32[]{:S(2)}, u32[]{:S(2)}) %all-to-all-start.1) | async-done | bytes 589856 | tf_op jit(solution)/shard_map/all_to_all | solution.py:493
  52.5 4.3 %finish.1 = (f32[4,8,4,512]{3,2,1,0:T(4,128)}, bf16[32,8,256]{2,1,0:T(8,128)(2,1)}) custom-call(s32[2,8,512]{2,1,0:T(8,128)S(1)} %broadcast_in_dim.12.place, f32[128,512]{1,0:T(8,128)S(1)} %spectra.1.own, bf16[8,96,384]{2,1,0:T(8,128)(2,1)S(1)} %all-to-all-done.1.got, bf16[512,512]{1,0:T(8,128)(2,1)S(1)} %copy-done, bf16[512,512]{1,0:T(8,128)(2,1)S(1)} %copy-done.1, ...), custom_call_target="tpu_custom_call" | custom-call | tf_op jit(solution)/shard_map/finish/pallas_call | solution.py:449
Async XLA Ops:
  0.6 21.4 %copy-start.2 = (bf16[1,4,512]{2,1,0:T(4,128)(2,1)S(1)}, bf16[1,4,512]{2,1,0:T(4,128)(2,1)}, u32[]{:S(2)}) copy-start(bf16[1,4,512]{2,1,0:T(4,128)(2,1)} %param.12) | copy-start | bytes 12292
  1.3 41.1 %copy-start.3 = (bf16[27,64,32]{1,2,0:T(8,128)(2,1)S(1)}, bf16[27,64,32]{1,2,0:T(8,128)(2,1)}, u32[]{:S(2)}) copy-start(bf16[27,64,32]{1,2,0:T(8,128)(2,1)} %param.17) | copy-start | bytes 331780
  4.7 38.7 %copy-start = (bf16[512,512]{1,0:T(8,128)(2,1)S(1)}, bf16[512,512]{1,0:T(8,128)(2,1)}, u32[]{:S(2)}) copy-start(bf16[512,512]{1,0:T(8,128)(2,1)} %constant.17.clone.high) | copy-start | bytes 1572868
  4.7 38.7 %copy-start.1 = (bf16[512,512]{1,0:T(8,128)(2,1)S(1)}, bf16[512,512]{1,0:T(8,128)(2,1)}, u32[]{:S(2)}) copy-start(bf16[512,512]{1,0:T(8,128)(2,1)} %constant.18.clone.low) | copy-start | bytes 1572868
  4.8 29.3 %all-to-all-start = ((bf16[64,4,384]{2,1,0:T(4,128)(2,1)}), bf16[64,4,384]{2,1,0:T(4,128)(2,1)S(1)}, u32[]{:S(2)}, u32[]{:S(2)}) async-start(bf16[64,4,384]{2,1,0:T(4,128)(2,1)} %get-tuple-element.11), calls=%async_computation | async-start | bytes 393216 | tf_op jit(solution)/shard_map/all_to_all | solution.py:492
  22.0 8.8 %collective-permute-start = (bf16[4,512]{1,0:T(4,128)(2,1)S(1)}, bf16[4,512]{1,0:T(4,128)(2,1)S(1)}, u32[]{:S(2)}, u32[]{:S(2)}) collective-permute-start(bf16[4,512]{1,0:T(4,128)(2,1)S(1)} %bitcast.9), channel_id=1, source_target_pairs={{0,256},{64,320},{128,384},{192,448},{256,0},{320,64},{384,128},{4... | collective-permute-start | bytes 12296 | tf_op jit(solution)/shard_map/ppermute | solution.py:485
  35.4 17.1 %all-to-all-start.1 = ((bf16[8,96,384]{2,1,0:T(8,128)(2,1)}), bf16[8,96,384]{2,1,0:T(8,128)(2,1)S(1)}, u32[]{:S(2)}, u32[]{:S(2)}) async-start(bf16[8,96,384]{2,1,0:T(8,128)(2,1)} %regroup.1), calls=%async_computation.1 | async-start | bytes 1179648 | tf_op jit(solution)/shard_map/all_to_all | solution.py:493

commit v8 on v7

--- a/solution.py
+++ b/solution.py
@@ -19,9 +19,10 @@
 PLANE = CH * ROWS
 BRICK = WIDTH // TILES
 SPAN = BRICK + 2
-LINES = 3 * HALVES * PLANE
+BODY = 3 * HALVES * PLANE
+LINES = BODY + 2 * PLANE + 2 * ROWS
 ALONG = SPAN * PAIRS
-PADDED = 384
+PADDED = 256
 
 
 def device(half, far, pair, core):
@@ -222,39 +223,44 @@
         return rows, at
 
     refs = jnp.concatenate([band[...].astype(F32), other[...].astype(F32)], axis=0)
-    marks = []
-    for p in range(0, 8, 2):
-        pair = refs[:, p * 64 : (p + 2) * 64]
-        marks.append(jnp.concatenate([pltpu.roll(pair, 64, 1), pair], axis=0))
+    marks = jnp.concatenate([refs[:, :128], refs[:, 128:256]], axis=0).astype(BF)
+    marks_end = refs[:, 256:].astype(BF)
     lane = iota((PLANE, 128), 1)
     outward = []
+
+    def place_pieces(pieces, half, block, first):
+        for k, (rows, at) in enumerate(pieces):
+            to = (first + k) * PAIRS
+            turn = (to - at - half * PAIRS) % 128
+            rows = pltpu.roll(rows, turn, 1) if turn else rows
+            block = jnp.where((lane >= to) & (lane < to + PAIRS), rows, block)
+        return block
+
+    empty = jnp.zeros((PLANE, 128), F32)
     for core in range(2):
         for slot in range(6):
             pieces = [piece(slot, core * BRICK + k) for k in range(SPAN)]
-            for half in range(HALVES):
-                blocks = []
-                for m in range(3):
-                    block = jnp.zeros((PLANE, 128), F32)
-                    for k in range(4 * m, min(4 * m + 4, SPAN)):
-                        rows, at = pieces[k]
-                        to = k % 4 * PAIRS
-                        turn = (to - at - half * PAIRS) % 128
-                        rows = pltpu.roll(rows, turn, 1) if turn else rows
-                        block = jnp.where((lane >= to) & (lane < to + PAIRS), rows, block)
-                    blocks.append(block)
-                main = [block.astype(BF) for block in blocks[:2]]
-                for far in range(FAR):
-                    step = slot - far
-                    if not 0 <= step < 3:
-                        continue
-                    w = step * HALVES + half
-                    last = jnp.where(lane >= 64, marks[w], blocks[2]) if w < 4 else blocks[2]
-                    rows = slice(w * PLANE, (w + 1) * PLANE)
-                    sent[2 * far + core, rows, :128] = main[0]
-                    sent[2 * far + core, rows, 128:256] = main[1]
-                    sent[2 * far + core, rows, 256:] = last.astype(BF)
+            main = [
+                [place_pieces(pieces[m : m + 4], half, empty, 0).astype(BF) for m in (0, 4)]
+                for half in range(HALVES)
+            ]
+            tail = place_pieces(pieces[8:], 0, empty, 0)
+            tail = place_pieces(pieces[8:], 1, tail, 2).astype(BF)
+            for far in range(FAR):
+                step = slot - far
+                if not 0 <= step < 3:
+                    continue
+                peer = 2 * far + core
+                for half in range(HALVES):
+                    start = (step * HALVES + half) * PLANE
+                    sent[peer, start : start + PLANE, :128] = main[half][0]
+                    sent[peer, start : start + PLANE, 128:] = main[half][1]
+                start = BODY + step // 2 * PLANE
+                sent[peer, start : start + PLANE, step % 2 * 128 : (step % 2 + 1) * 128] = tail
             if slot >= 2:
                 peer = 2 * (slot - 2) + core
+                sent[peer, BODY + PLANE : BODY + 2 * PLANE, 128:] = marks
+                sent[peer, BODY + 2 * PLANE :, :] = marks_end
                 copy = pltpu.make_async_copy(sent.at[peer], out.at[peer], sems.at[peer])
                 copy.start()
                 outward.append(copy)
@@ -307,20 +313,22 @@
 def correlate(place, own, got, high, low, out):
     half = WIDTH // 2
     count = CH * DEPTH * ROWS
-    left = iota((2 * ROWS, 128), 1) < 64
+    mine = place[1, :1, :128] == 0
     near, away = [], []
     for far in range(FAR):
-        pieces = jnp.where(
-            place[1, :1, :128] == 0,
-            got[2 * far, :64, 256:].astype(F32),
-            got[2 * far + 1, :64, 256:].astype(F32),
+        a, b = got[2 * far, BODY + PLANE :, :], got[2 * far + 1, BODY + PLANE :, :]
+        a, b = a.astype(F32), b.astype(F32)
+        under = jnp.where(mine, a[:, :128], b[:, :128])
+        top = jnp.where(mine, a[:, 128:], b[:, 128:])
+        rows = jnp.concatenate(
+            [
+                top[: 2 * ROWS],
+                top[2 * ROWS : 4 * ROWS],
+                under[4 * ROWS :],
+                top[4 * ROWS :],
+            ],
+            axis=1,
         )
-        lanes = []
-        for p in range(0, 8, 2):
-            a = pieces[p * 2 * ROWS : (p + 1) * 2 * ROWS]
-            b = pieces[(p + 1) * 2 * ROWS : (p + 2) * 2 * ROWS]
-            lanes.append(jnp.where(left, pltpu.roll(a, 64, 1), b))
-        rows = jnp.concatenate(lanes, axis=1)
         near.append(rows[:ROWS])
         away.append(rows[ROWS:])
     near, away = jnp.concatenate(near, axis=0), jnp.concatenate(away, axis=0)
@@ -370,13 +378,21 @@
         at = a * 256
         planes = []
         for core in range(2):
-            mixed = jnp.concatenate(
+            inner = jnp.concatenate(
                 [
                     got[2 * far + core, a * HALVES * PLANE : (a + 1) * HALVES * PLANE, :]
                     for far in range(FAR)
                 ],
                 axis=0,
             )
+            tails = []
+            for far in range(FAR):
+                start = BODY + a // 2 * PLANE
+                tail = got[
+                    2 * far + core, start : start + PLANE, a % 2 * 128 : (a % 2 + 1) * 128
+                ]
+                tails += [tail, pltpu.roll(tail.astype(F32), 64, 1).astype(BF)]
+            mixed = jnp.concatenate([inner, jnp.concatenate(tails, axis=0)], axis=1)
             plane = dot(mixed, spread[...], ((0,), (0,)))[:ALONG].astype(BF)
             wide[core, :, at : at + 128] = plane
             planes.append(plane.astype(F32))

time: 57.2 us -> 56.7 us (level)
  no operation moved by 1% of the time
where the time goes in v8:
time: 56.7 us; the launch traced here: 56.3 us
  starting transfers between devices  31.1 us (55%)
  Pallas kernels  11.7 us (21%)
  waiting for transfers between devices  10.9 us (19%)
  between operations  1.38 us (2%)
  local copies, waits for them, and re-layouts  1.1 us (2%)
    all_to_all x1, starting transfers between devices, body(): got = close(swap(sent, axis_index_groups=RINGS))  17.1 us
    all_to_all x1, starting transfers between devices, body(): swap(regroup(place, got, band, other), axis_index_groups=NEAR)  7.01 us
    ppermute x1, starting transfers between devices, body(): other = close(lax.ppermute(band, 'round', ahead))  6.93 us
    all_to_all x1, waiting for transfers between devices, body(): swap(regroup(place, got, band, other), axis_index_groups=NEAR)  5.92 us
    pallas_call x1, Pallas kernels, finish(): pl.pallas_call(finish_kernel, in_specs=[inside] * 6 + [outside] + [inside...  4.27 us
    pallas_call x1, Pallas kernels, warp(): pl.pallas_call(warp_kernel, out_shape=(jax.ShapeDtypeStruct(shape, BF), p...  3.47 us
    all_to_all x1, waiting for transfers between devices, body(): got = close(swap(sent, axis_index_groups=RINGS))  3.26 us
    pallas_call x1, Pallas kernels, prepare(): pl.pallas_call(prepare_kernel, out_shape=(pltpu.VMEM((MIXED * ROWS, MIXED...  2.45 us
  transfers between devices with their start and end apart: 3, of which 3 were waited for; matrix products, arithmetic and copies ran while one was open for 2% of the time, Pallas kernels for 5%

profile of v8, /device:TPU:1, one launch (start us, length us, event | category | flops | bytes accessed | tf_op | source)
XLA Modules:
  0.0 56.3 jit_solution(15689444221667616044)
XLA Ops:
  0.6 0.0 copy-start.2
  1.3 0.0 copy-start.3
  1.3 0.0 copy-start
  1.3 0.0 copy-start.1
  1.3 3.5 %warp.1 = (bf16[64,4,384]{2,1,0:T(4,128)(2,1)}, bf16[4,32,512]{2,1,0:T(8,128)(2,1)S(1)}) custom-call(s32[1,1]{1,0:T(1,128)S(6)} %copy.15.shift, s32[1,4]{1,0:T(1,128)} %ids.1, bf16[4,8,4,512]{3,2,1,0:T(4,128)(2,1)} %bitcast.11, bf16[4,512,512]{2,1,0:T(8,128)(2,1)} %table.1), custom_call_target="tpu_custom_call" | custom-call | tf_op jit(solution)/shard_map/warp/pallas_call | solution.py:127
  4.8 17.1 %all-to-all-start = ((bf16[64,4,384]{2,1,0:T(4,128)(2,1)}), bf16[64,4,384]{2,1,0:T(4,128)(2,1)S(1)}, u32[]{:S(2)}, u32[]{:S(2)}) async-start(bf16[64,4,384]{2,1,0:T(4,128)(2,1)} %get-tuple-element.11), calls=%async_computation | async-start | bytes 393216 | tf_op jit(solution)/shard_map/all_to_all | solution.py:508
  22.0 0.0 copy-done.2
  22.0 6.9 %collective-permute-start = (bf16[4,512]{1,0:T(4,128)(2,1)S(1)}, bf16[4,512]{1,0:T(4,128)(2,1)S(1)}, u32[]{:S(2)}, u32[]{:S(2)}) collective-permute-start(bf16[4,512]{1,0:T(4,128)(2,1)S(1)} %bitcast.9), channel_id=1, source_target_pairs={{0,256},{64,320},{128,384},{192,448},{256,0},{320,64},{384,128},{4... | collective-permute-start | bytes 12296 | tf_op jit(solution)/shard_map/ppermute | solution.py:501
  28.9 0.1 pad_add_fusion
  29.0 1.7 %collective-permute-done.other = bf16[4,512]{1,0:T(4,128)(2,1)S(1)} collective-permute-done((bf16[4,512]{1,0:T(4,128)(2,1)S(1)}, bf16[4,512]{1,0:T(4,128)(2,1)S(1)}, u32[]{:S(2)}, u32[]{:S(2)}) %collective-permute-start) | collective-permute-done | bytes 4128 | tf_op jit(solution)/shard_map/ppermute | solution.py:501
  30.7 3.3 %all-to-all-done.got = bf16[64,4,384]{2,1,0:T(4,128)(2,1)S(1)} async-done(((bf16[64,4,384]{2,1,0:T(4,128)(2,1)}), bf16[64,4,384]{2,1,0:T(4,128)(2,1)S(1)}, u32[]{:S(2)}, u32[]{:S(2)}) %all-to-all-start) | async-done | bytes 196640 | tf_op jit(solution)/shard_map/all_to_all | solution.py:508
  34.0 0.1 broadcast_in_dim.12.place
  34.1 1.2 %regroup.1 = bf16[8,136,256]{2,1,0:T(8,128)(2,1)} custom-call(s32[2,8,512]{2,1,0:T(8,128)S(1)} %broadcast_in_dim.12.place, bf16[64,4,384]{2,1,0:T(4,128)(2,1)S(1)} %all-to-all-done.got, bf16[4,512]{1,0:T(4,128)(2,1)S(1)} %bitcast.10, bf16[4,512]{1,0:T(4,128)(2,1)S(1)} %collective-permute-done.other), custom_call_target="tpu_custom_call" | custom-call | tf_op jit(solution)/shard_map/regroup/pallas_call | solution.py:273
  35.3 7.0 %all-to-all-start.1 = ((bf16[8,136,256]{2,1,0:T(8,128)(2,1)}), bf16[8,136,256]{2,1,0:T(8,128)(2,1)S(1)}, u32[]{:S(2)}, u32[]{:S(2)}) async-start(bf16[8,136,256]{2,1,0:T(8,128)(2,1)} %regroup.1), calls=%async_computation.1 | async-start | bytes 1114112 | tf_op jit(solution)/shard_map/all_to_all | solution.py:509
  42.3 0.0 copy-done.3
  42.3 1.0 %copy.13.conv = bf16[27,64,32]{2,1,0:T(8,128)(2,1)} copy(bf16[27,64,32]{1,2,0:T(8,128)(2,1)S(1)} %copy-done.3) | data formatting | bytes 221184 | tf_op args[6]
  43.3 0.0 copy-done
  43.3 0.0 copy-done.1
  43.3 0.3 spectra.1.own
  43.6 2.5 %prepare.1 = (bf16[128,128]{1,0:T(8,128)(2,1)S(1)}, bf16[256,2304]{1,0:T(8,128)(2,1)}, f32[1,256]{1,0:T(1,128)S(1)}, bf16[128,256]{1,0:T(8,128)(2,1)S(1)}) custom-call(bf16[32,32]{1,0:T(8,128)(2,1)} %unmix.1, bf16[27,64,32]{2,1,0:T(8,128)(2,1)} %copy.13.conv, f32[1,64]{1,0:T(1,128)} %bitcast.12, bf16[32,64]{1,0:T(8,128)(2,1)} %project.1), custom_call_target="tpu_custom_call" | custom-call | tf_op jit(solution)/shard_map/prepare/pallas_call | solution.py:180
  46.1 5.9 %all-to-all-done.1.got = bf16[8,136,256]{2,1,0:T(8,128)(2,1)S(1)} async-done(((bf16[8,136,256]{2,1,0:T(8,128)(2,1)}), bf16[8,136,256]{2,1,0:T(8,128)(2,1)S(1)}, u32[]{:S(2)}, u32[]{:S(2)}) %all-to-all-start.1) | async-done | bytes 557088 | tf_op jit(solution)/shard_map/all_to_all | solution.py:509
  52.0 4.3 %finish.1 = (f32[4,8,4,512]{3,2,1,0:T(4,128)}, bf16[32,8,256]{2,1,0:T(8,128)(2,1)}) custom-call(s32[2,8,512]{2,1,0:T(8,128)S(1)} %broadcast_in_dim.12.place, f32[128,512]{1,0:T(8,128)S(1)} %spectra.1.own, bf16[8,136,256]{2,1,0:T(8,128)(2,1)S(1)} %all-to-all-done.1.got, bf16[512,512]{1,0:T(8,128)(2,1)S(1)} %copy-done, bf16[512,512]{1,0:T(8,128)(2,1)S(1)} %copy-done.1, ...), custom_call_target="tpu_custom_call" | custom-call | tf_op jit(solution)/shard_map/finish/pallas_call | solution.py:465
Async XLA Ops:
  0.6 21.3 %copy-start.2 = (bf16[1,4,512]{2,1,0:T(4,128)(2,1)S(1)}, bf16[1,4,512]{2,1,0:T(4,128)(2,1)}, u32[]{:S(2)}) copy-start(bf16[1,4,512]{2,1,0:T(4,128)(2,1)} %param.12) | copy-start | bytes 12292
  1.3 41.0 %copy-start.3 = (bf16[27,64,32]{1,2,0:T(8,128)(2,1)S(1)}, bf16[27,64,32]{1,2,0:T(8,128)(2,1)}, u32[]{:S(2)}) copy-start(bf16[27,64,32]{1,2,0:T(8,128)(2,1)} %param.17) | copy-start | bytes 331780
  1.3 42.0 %copy-start = (bf16[512,512]{1,0:T(8,128)(2,1)S(1)}, bf16[512,512]{1,0:T(8,128)(2,1)}, u32[]{:S(2)}) copy-start(bf16[512,512]{1,0:T(8,128)(2,1)} %constant.17.clone.high) | copy-start | bytes 1572868
  1.3 42.0 %copy-start.1 = (bf16[512,512]{1,0:T(8,128)(2,1)S(1)}, bf16[512,512]{1,0:T(8,128)(2,1)}, u32[]{:S(2)}) copy-start(bf16[512,512]{1,0:T(8,128)(2,1)} %constant.18.clone.low) | copy-start | bytes 1572868
  4.8 29.2 %all-to-all-start = ((bf16[64,4,384]{2,1,0:T(4,128)(2,1)}), bf16[64,4,384]{2,1,0:T(4,128)(2,1)S(1)}, u32[]{:S(2)}, u32[]{:S(2)}) async-start(bf16[64,4,384]{2,1,0:T(4,128)(2,1)} %get-tuple-element.11), calls=%async_computation | async-start | bytes 393216 | tf_op jit(solution)/shard_map/all_to_all | solution.py:508
  22.0 8.8 %collective-permute-start = (bf16[4,512]{1,0:T(4,128)(2,1)S(1)}, bf16[4,512]{1,0:T(4,128)(2,1)S(1)}, u32[]{:S(2)}, u32[]{:S(2)}) collective-permute-start(bf16[4,512]{1,0:T(4,128)(2,1)S(1)} %bitcast.9), channel_id=1, source_target_pairs={{0,256},{64,320},{128,384},{192,448},{256,0},{320,64},{384,128},{4... | collective-permute-start | bytes 12296 | tf_op jit(solution)/shard_map/ppermute | solution.py:501
  35.3 16.7 %all-to-all-start.1 = ((bf16[8,136,256]{2,1,0:T(8,128)(2,1)}), bf16[8,136,256]{2,1,0:T(8,128)(2,1)S(1)}, u32[]{:S(2)}, u32[]{:S(2)}) async-start(bf16[8,136,256]{2,1,0:T(8,128)(2,1)} %regroup.1), calls=%async_computation.1 | async-start | bytes 1114112 | tf_op jit(solution)/shard_map/all_to_all | solution.py:509
